TPU v7x, 32 devices: a whole 2x2x4 slice. The times are simulated.
32 devices in a mesh: wide: 4 (over y, x), narrow: 8 (over z, core).
Axes of the slice: x: 2, y: 2, z: 4, core: 2. Of those that a mesh axis runs over, the one named last changes fastest.
Arguments:
- tokens: bfloat16 [16384, 1024], P(('wide', 'narrow')), may hold values from -6 to 6
- cotangent: bfloat16 [16384, 1024], P(('wide', 'narrow')), may hold values from -6 to 6
- item_lengths: int32 [4, 4], P('wide'), may hold values from 0 to 4096, as said below
- attn_gain: bfloat16 [1024], replicated, may hold values from 0.099609375 to 1.8984375
- attn_bias: bfloat16 [1024], replicated, may hold values from -0.099609375 to 0.099609375
- qkv_weight: bfloat16 [1024, 3072], P(None, 'narrow'), may hold values from -0.1875 to 0.1875
- proj_weight: bfloat16 [1024, 1024], P('narrow'), may hold values from -3 to 3
- mlp_gain: bfloat16 [1024], replicated, may hold values from 0.099609375 to 1.8984375
- mlp_bias: bfloat16 [1024], replicated, may hold values from -0.19921875 to 0.19921875
- up_weight: bfloat16 [1024, 4096], P(None, 'narrow'), may hold values from -0.1875 to 0.1875
- down_weight: bfloat16 [4096, 1024], P('narrow'), may hold values from -0.09375 to 0.09375
Outputs:
- output: bfloat16 [16384, 1024], P(('wide', 'narrow'))
- grad_tokens: bfloat16 [16384, 1024], P(('wide', 'narrow'))
- grad_attn_gain: float32 [1024], P('narrow')
- grad_attn_bias: float32 [1024], P('narrow')
- grad_qkv: float32 [1024, 3072], P(None, 'narrow')
- grad_proj: float32 [1024, 1024], P('narrow')
- grad_mlp_gain: float32 [1024], P('narrow')
- grad_mlp_bias: float32 [1024], P('narrow')
- grad_up: float32 [1024, 4096], P(None, 'narrow')
- grad_down: float32 [4096, 1024], P('narrow')
Inputs may be any that keep to these rules, and one draw needn't show every extreme that they name: `item_lengths`: each row sums to 4096. In every draw one wide position holds a single item of 4096 patches followed by zeros; every other position holds 4 items of 1024 plus or minus up to 3 * (128) patches.
All inputs are finite; a program needn't handle non-finite values.
Results may differ from a plain program's by a relative error of at most 0.015.
Values may be sent and summed in bfloat16 or wider, within the bound.
A program may use at most 192 MiB of HBM per device.

v0:
```python
import jax
import jax.numpy as jnp
from jax import lax
from jax.sharding import PartitionSpec as P

HEAD_DIM = 64
CAP = 4096
QBLOCK = 512


epsilon = 1e-05


def norm_forward(values, norm_gain, norm_bias):
    average = jnp.mean(values, axis=-1, keepdims=True)
    centred = values - average
    variance = jnp.mean(centred * centred, axis=-1, keepdims=True)
    return centred * lax.rsqrt(variance + epsilon) * norm_gain + norm_bias


def gelu_exact(values):
    return jax.nn.gelu(values, approximate=False)


def segment_ids(item_lengths):
    item_ends = jnp.cumsum(item_lengths[0])
    row_index = jnp.arange(CAP, dtype=jnp.int32)
    return jnp.sum((row_index[:, None] >= item_ends[None, :]).astype(jnp.int32), axis=1)


def block_scores(query_block, keys_all, segment_block, segment):
    score_scale = HEAD_DIM ** (-0.5)
    scores = (
        jnp.einsum("qhd,khd->hqk", query_block, keys_all, preferred_element_type=jnp.float32)
        * score_scale
    )
    same_item = segment_block[:, None] == segment[None, :]
    return jnp.where(same_item[None], scores, -1e30)


def attend_forward(packed, segment):
    heads_local = packed.shape[1]
    blocks = CAP // QBLOCK
    keys_all = packed[:, :, 1]
    values_all = packed[:, :, 2]

    def one_block(block_in):
        query_block, segment_block = block_in
        scores = block_scores(query_block, keys_all, segment_block, segment)
        maximum = jnp.max(scores, axis=-1, keepdims=True)
        raised = jnp.exp(scores - maximum)
        row_total = jnp.sum(raised, axis=-1, keepdims=True)
        weights = (raised / row_total).astype(jnp.bfloat16)
        attended = jnp.einsum(
            "hqk,khd->qhd", weights, values_all, preferred_element_type=jnp.float32
        )
        return (attended.astype(jnp.bfloat16), (maximum + jnp.log(row_total))[:, :, 0])

    queries = packed[:, :, 0].reshape(blocks, QBLOCK, heads_local, HEAD_DIM)
    attended, log_total = lax.map(one_block, (queries, segment.reshape(blocks, QBLOCK)))
    return (attended.reshape(CAP, heads_local * HEAD_DIM), log_total)


def attend_backward(packed, segment, log_total, grad_attended):
    heads_local = packed.shape[1]
    blocks = CAP // QBLOCK
    score_scale = HEAD_DIM ** (-0.5)
    keys_all = packed[:, :, 1]
    values_all = packed[:, :, 2]

    def one_block(running, block_in):
        grad_keys, grad_values = running
        query_block, segment_block, log_block, grad_block = block_in
        scores = block_scores(query_block, keys_all, segment_block, segment)
        probability = jnp.exp(scores - log_block[:, :, None])
        grad_probs = jnp.einsum(
            "qhd,khd->hqk", grad_block, values_all, preferred_element_type=jnp.float32
        )
        row_inner = jnp.sum(probability * grad_probs, axis=-1, keepdims=True)
        grad_scores = (probability * (grad_probs - row_inner)).astype(jnp.bfloat16)
        grad_query = (
            jnp.einsum("hqk,khd->qhd", grad_scores, keys_all, preferred_element_type=jnp.float32)
            * score_scale
        )
        grad_keys = (
            grad_keys
            + jnp.einsum(
                "hqk,qhd->khd", grad_scores, query_block, preferred_element_type=jnp.float32
            )
            * score_scale
        )
        grad_values = grad_values + jnp.einsum(
            "hqk,qhd->khd",
            probability.astype(jnp.bfloat16),
            grad_block,
            preferred_element_type=jnp.float32,
        )
        return ((grad_keys, grad_values), grad_query.astype(jnp.bfloat16))

    initial = jnp.zeros((CAP, heads_local, HEAD_DIM), jnp.float32)
    block_inputs = (
        packed[:, :, 0].reshape(blocks, QBLOCK, heads_local, HEAD_DIM),
        segment.reshape(blocks, QBLOCK),
        log_total,
        grad_attended.reshape(blocks, QBLOCK, heads_local, HEAD_DIM),
    )
    (grad_keys, grad_values), grad_queries = lax.scan(one_block, (initial, initial), block_inputs)
    grad_packed = jnp.stack(
        [
            grad_queries.reshape(CAP, heads_local, HEAD_DIM),
            grad_keys.astype(jnp.bfloat16),
            grad_values.astype(jnp.bfloat16),
        ],
        axis=2,
    )
    return grad_packed.reshape(CAP, heads_local * 3 * HEAD_DIM)


def body(
    tokens,
    cotangent,
    item_lengths,
    attn_gain,
    attn_bias,
    qkv_weight,
    proj_weight,
    mlp_gain,
    mlp_bias,
    up_weight,
    down_weight,
):
    segment = segment_ids(item_lengths)
    token_rows = tokens.astype(jnp.float32)
    heads_local = qkv_weight.shape[1] // (3 * HEAD_DIM)
    gain_one = attn_gain.astype(jnp.float32)
    bias_one = attn_bias.astype(jnp.float32)
    gain_two = mlp_gain.astype(jnp.float32)
    bias_two = mlp_bias.astype(jnp.float32)
    normed = norm_forward(token_rows, gain_one, bias_one).astype(jnp.bfloat16)
    normed_all = lax.all_gather(normed, "narrow", axis=0, tiled=True)
    packed = jnp.dot(normed_all, qkv_weight, preferred_element_type=jnp.float32).astype(
        jnp.bfloat16
    )
    packed = packed.reshape(CAP, heads_local, 3, HEAD_DIM)
    attended, log_total = attend_forward(packed, segment)
    selected = attended
    branch = lax.psum_scatter(
        jnp.dot(selected, proj_weight, preferred_element_type=jnp.float32),
        "narrow",
        scatter_dimension=0,
        tiled=True,
    )
    normed_all, packed, attended, log_total, middle = (
        normed_all,
        packed,
        attended,
        log_total,
        token_rows + branch,
    )
    expand_in = norm_forward(middle, gain_two, bias_two).astype(jnp.bfloat16)
    expand_all = lax.all_gather(expand_in, "narrow", axis=0, tiled=True)
    hidden_pre = jnp.dot(expand_all, up_weight, preferred_element_type=jnp.float32)
    expand_all, hidden_pre, hidden = (
        expand_all,
        hidden_pre,
        gelu_exact(hidden_pre).astype(jnp.bfloat16),
    )
    selected = hidden
    mlp_out = lax.psum_scatter(
        jnp.dot(selected, down_weight, preferred_element_type=jnp.float32).astype(jnp.bfloat16),
        "narrow",
        scatter_dimension=0,
        tiled=True,
    ).astype(jnp.float32)
    output = (middle + mlp_out).astype(jnp.bfloat16)
    grad_rows = lax.all_gather(cotangent, "narrow", axis=0, tiled=True)
    grad_down = jnp.einsum("rf,rd->fd", hidden, grad_rows, preferred_element_type=jnp.float32)
    grad_hidden = jnp.einsum(
        "rd,fd->rf", grad_rows, down_weight, preferred_element_type=jnp.float32
    )
    gelu_values, gelu_pull = jax.vjp(gelu_exact, hidden_pre)
    grad_pre = gelu_pull(grad_hidden)[0].astype(jnp.bfloat16)
    grad_up = jnp.einsum("rd,rf->df", expand_all, grad_pre, preferred_element_type=jnp.float32)
    selected = grad_pre
    grad_expand = lax.psum_scatter(
        jnp.einsum("rf,df->rd", selected, up_weight, preferred_element_type=jnp.float32),
        "narrow",
        scatter_dimension=0,
        tiled=True,
    )
    norm_two_values, norm_two_pull = jax.vjp(norm_forward, middle, gain_two, bias_two)
    grad_middle_norm, grad_gain_two, grad_bias_two = norm_two_pull(grad_expand)
    grad_middle = cotangent.astype(jnp.float32) + grad_middle_norm
    grad_branch_all = lax.all_gather(grad_middle.astype(jnp.bfloat16), "narrow", axis=0, tiled=True)
    grad_proj = jnp.einsum(
        "ra,rd->ad", attended, grad_branch_all, preferred_element_type=jnp.float32
    )
    grad_attended = jnp.einsum(
        "rd,ad->ra", grad_branch_all, proj_weight, preferred_element_type=jnp.float32
    ).astype(jnp.bfloat16)
    grad_packed = attend_backward(packed, segment, log_total, grad_attended)
    grad_qkv = jnp.einsum("rd,rc->dc", normed_all, grad_packed, preferred_element_type=jnp.float32)
    selected = grad_packed
    grad_normed = lax.psum_scatter(
        jnp.einsum("rc,dc->rd", selected, qkv_weight, preferred_element_type=jnp.float32),
        "narrow",
        scatter_dimension=0,
        tiled=True,
    )
    norm_one_values, norm_one_pull = jax.vjp(norm_forward, token_rows, gain_one, bias_one)
    grad_token_norm, grad_gain_one, grad_bias_one = norm_one_pull(grad_normed)
    grad_tokens = (grad_middle + grad_token_norm).astype(jnp.bfloat16)
    norm_parts = jnp.stack([grad_gain_one, grad_bias_one, grad_gain_two, grad_bias_two])
    norm_shares = lax.psum_scatter(norm_parts, "narrow", scatter_dimension=1, tiled=True)
    summed = (
        lax.psum(grad_qkv.astype(jnp.bfloat16), "wide").astype(jnp.float32),
        lax.psum(grad_proj.astype(jnp.bfloat16), "wide").astype(jnp.float32),
        lax.psum(grad_up.astype(jnp.bfloat16), "wide").astype(jnp.float32),
        lax.psum(grad_down.astype(jnp.bfloat16), "wide").astype(jnp.float32),
        lax.psum(norm_shares.astype(jnp.bfloat16), "wide").astype(jnp.float32),
    )
    shares = summed[4]
    return (
        output,
        grad_tokens,
        shares[0],
        shares[1],
        summed[0],
        summed[1],
        shares[2],
        shares[3],
        summed[2],
        summed[3],
    )


def solution(mesh):
    return jax.shard_map(
        body,
        mesh=mesh,
        in_specs=(
            P(("wide", "narrow"), None),
            P(("wide", "narrow"), None),
            P("wide", None),
            P(),
            P(),
            P(None, "narrow"),
            P("narrow", None),
            P(),
            P(),
            P(None, "narrow"),
            P("narrow", None),
        ),
        out_specs=(
            P(("wide", "narrow"), None),
            P(("wide", "narrow"), None),
            P("narrow"),
            P("narrow"),
            P(None, "narrow"),
            P("narrow", None),
            P("narrow"),
            P("narrow"),
            P(None, "narrow"),
            P("narrow", None),
        ),
        check_vma=False,
    )
```

profile of v0, /device:TPU:0, one launch (start us, length us, event | category | flops | bytes accessed | tf_op | source)
XLA Modules:
  0.0 1703.8 jit_solution(5403743624793534049)
XLA Ops:
  16.1 83.9 %all-gather.5.cloned.1.call-done = bf16[4096,1024]{1,0:T(8,128)(2,1)} async-done(((bf16[512,1024]{1,0:T(8,128)(2,1)}), bf16[4096,1024]{1,0:T(8,128)(2,1)}) %all-gather.5.cloned.1.call-update) | async-done | bytes 8388624 | tf_op jit(solution)/shard_map/all_gather | solution.py:140
  100.0 7.0 convolution_convert_fusion.1
  110.0 129.1 %while.27 = (s32[]{:T(128)}, bf16[8,512,2,64]{1,3,2,0:T(8,128)(2,1)}, f32[8,2,512]{2,1,0:T(2,128)S(1)}, s32[8,512]{1,0:T(8,128)S(1)}, s32[4096]{0:T(1024)S(1)}, ...) while((s32[]{:T(128)}, ...), condition=%wide.region_7.8_spmd, body=%wide.region_4.7_spmd.sunk | while | flops 1126235136 | bytes 61134964 | solution.py:60
  120.7 5.5 fusion.124
  136.8 5.5 fusion.124
  153.0 5.5 fusion.124
  169.1 5.5 fusion.124
  185.2 5.5 fusion.124
  201.3 5.5 fusion.124
  217.4 5.5 fusion.124
  243.0 8.1 fusion.67
  251.9 166.3 %reduce-scatter.8.cloned.1.call-done = f32[512,1024]{1,0:T(8,128)} async-done(((f32[4096,1024]{1,0:T(8,128)}), f32[512,1024]{1,0:T(8,128)}) %reduce-scatter.8.cloned.1.call-update) | async-done | bytes 2097168 | tf_op jit(solution)/shard_map/reduce_scatter | solution.py:147
  422.7 79.9 %all-gather.7.cloned.1.call-done = bf16[4096,1024]{1,0:T(8,128)(2,1)} async-done(((bf16[512,1024]{1,0:T(8,128)(2,1)}), bf16[4096,1024]{1,0:T(8,128)(2,1)}) %all-gather.7.cloned.1.call-update) | async-done | bytes 8388624 | tf_op jit(solution)/shard_map/all_gather | solution.py:161
  502.6 11.7 fusion.68
  514.2 70.4 %all-gather.9.cloned.1.call-done = bf16[4096,1024]{1,0:T(8,128)(2,1)} async-done(((bf16[512,1024]{1,0:T(8,128)(2,1)}), bf16[4096,1024]{1,0:T(8,128)(2,1)}) %all-gather.9.cloned.1.call-update) | async-done | bytes 8388624 | tf_op jit(solution)/shard_map/all_gather | solution.py:176
  584.7 26.6 %add_convert_fusion = (bf16[4096,512]{1,0:T(8,128)(2,1)S(1)}, f32[4096,512]{1,0:T(8,128)}) fusion(f32[4096,512]{1,0:T(8,128)} %fusion.68, bf16[4096,1024]{1,0:T(8,128)(2,1)} %all-gather.9.cloned.1.call-done, bf16[512,1024]{1,0:T(8,128)(2,1)S(1)} %copy-done), kind=kOutput, calls=%fused_computation.54 | convolution fusion | flops 4445962240 | bytes 30408704 | tf_op jit(solution)/shard_map/rd,fd->rf/dot_general | solution.py:178
  613.2 8.2 fusion.69
  621.9 10.8 multiply_convert_fusion.1
  632.6 9.0 convolution_convert_fusion
  641.8 146.5 %reduce-scatter.12.cloned.1.call-done = f32[512,1024]{1,0:T(8,128)} async-done(((f32[4096,1024]{1,0:T(8,128)}), f32[512,1024]{1,0:T(8,128)}) %reduce-scatter.12.cloned.1.call-update) | async-done | bytes 2097168 | tf_op jit(solution)/shard_map/reduce_scatter | solution.py:185
  791.2 87.2 %reduce-scatter.10.cloned.1.call-done = bf16[512,1024]{1,0:T(8,128)(2,1)} async-done(((bf16[4096,1024]{1,0:T(8,128)(2,1)}), bf16[512,1024]{1,0:T(8,128)(2,1)}) %reduce-scatter.10.cloned.1.call-update) | async-done | bytes 1048592 | tf_op jit(solution)/shard_map/reduce_scatter | solution.py:169
  884.9 10.3 convolution_convert_fusion.3
  895.2 8.1 convolution_convert_fusion.4
  903.4 61.9 %all-gather.11.cloned.1.call-done = bf16[4096,1024]{1,0:T(8,128)(2,1)} async-done(((bf16[512,1024]{1,0:T(8,128)(2,1)}), bf16[4096,1024]{1,0:T(8,128)(2,1)}) %all-gather.11.cloned.1.call-update) | async-done | bytes 8388624 | tf_op jit(solution)/shard_map/all_gather | solution.py:194
  965.2 6.7 convolution_convert_fusion.2
  976.9 5.9 copy.51
  983.8 391.6 %while.28 = (s32[]{:T(128)}, f32[4096,2,64]{0,2,1:T(8,128)S(1)}, f32[4096,2,64]{0,2,1:T(8,128)}, bf16[8,512,2,64]{1,3,2,0:T(8,128)(2,1)}, bf16[8,512,2,64]{1,3,2...) while((s32[]{:T(128)}, f32[4096,2,64]{0,2,1:T(8,128)S(1)}, ...), condition=%wide.region_17.18_spmd.clone, body=%wide.region_15.17_spmd.clone.sunk | while | flops 2752117760 | bytes 217762032 | solution.py:107
  988.7 5.7 copy-done.2
  994.4 7.2 fusion.136
  1001.6 12.6 multiply_reduce_fusion.5
  1014.2 12.3 multiply_convert_fusion.3
  1037.2 5.7 copy-done.2
  1043.0 7.6 fusion.136
  1050.6 12.6 multiply_reduce_fusion.5
  1063.2 12.3 multiply_convert_fusion.3
  1086.2 5.7 copy-done.2
  1091.9 7.6 fusion.136
  1099.5 12.6 multiply_reduce_fusion.5
  1112.1 12.3 multiply_convert_fusion.3
  1135.1 5.7 copy-done.2
  1140.8 7.6 fusion.136
  1148.5 12.6 multiply_reduce_fusion.5
  1161.1 12.3 multiply_convert_fusion.3
  1184.1 5.7 copy-done.2
  1189.8 7.6 fusion.136
  1197.4 12.6 multiply_reduce_fusion.5
  1210.0 12.3 multiply_convert_fusion.3
  1233.0 5.7 copy-done.2
  1238.7 7.6 fusion.136
  1246.3 12.6 multiply_reduce_fusion.5
  1259.0 12.3 multiply_convert_fusion.3
  1281.9 5.7 copy-done.2
  1287.7 7.6 fusion.136
  1295.3 12.6 multiply_reduce_fusion.5
  1307.9 12.3 multiply_convert_fusion.3
  1330.9 5.7 copy-done.2
  1336.6 7.6 fusion.136
  1344.2 12.6 multiply_reduce_fusion.5
  1356.8 12.3 multiply_convert_fusion.3
  1392.7 10.1 fusion.70
  1403.2 75.9 %all-reduce.3.cloned.1.call-done = (bf16[1024,384]{1,0:T(8,128)(2,1)}, bf16[128,1024]{1,0:T(8,128)(2,1)}, bf16[1024,512]{1,0:T(8,128)(2,1)}, bf16[512,1024]{1,0:T(8,128)(2,1)}) async-done(((bf16[1024,384]{1,0:T(8,128)(2,1)}, bf16[128,1024]{1,0:T(8,128)(2,1)}, bf16[1024,512]{1,0:T(8,128)(2,1)}, bf16[512,1024]{1,0:T(8,128)(2,1)}), (bf16[1024,384]{1,0:T(8,128)(2,1)}, bf16[128,1024]{1,0:T(8,128)(2,1)}, ...) | async-done | bytes 3145744 | tf_op jit(solution)/shard_map/psum | solution.py:216
  1489.1 160.7 %reduce-scatter.14.cloned.1.call-done = f32[512,1024]{1,0:T(8,128)} async-done(((f32[4096,1024]{1,0:T(8,128)}), f32[512,1024]{1,0:T(8,128)}) %reduce-scatter.14.cloned.1.call-update) | async-done | bytes 2097168 | tf_op jit(solution)/shard_map/reduce_scatter | solution.py:204
  1659.2 26.0 %reduce-scatter.16.cloned.1.call-done = f32[128,4]{1,0:T(8,128)} async-done(((f32[1024,4]{1,0:T(8,128)}), f32[128,4]{1,0:T(8,128)}) %reduce-scatter.16.cloned.1.call-update) | async-done | bytes 2064
  1686.1 9.8 psum.35
  (259 shorter events, 252.3 us)
Async XLA Ops:
  7.2 577.5 %copy-start = (bf16[512,1024]{1,0:T(8,128)(2,1)S(1)}, bf16[512,1024]{1,0:T(8,128)(2,1)}, u32[]{:S(2)}) copy-start(bf16[512,1024]{1,0:T(8,128)(2,1)} %param.25) | copy-start | bytes 3145732
  7.2 92.8 %all-gather.5.cloned.1.call-start = ((), (), s32[]{:S(2)}) async-start(), calls=%async_computation.5 | async-start | bytes 9437184 | tf_op jit(solution)/shard_map/all_gather | solution.py:140
  8.8 3.6 copy-start.18
  10.4 0.6 copy-start.24
  11.0 1.4 copy-start.20
  11.7 0.7 copy-start.16
  15.1 403.1 %reduce-scatter.8.cloned.1.call-start = ((), (), s32[]{:S(2)}) async-start(), calls=%async_computation.6 | async-start | bytes 18874368 | tf_op jit(solution)/shard_map/reduce_scatter | solution.py:147
  110.0 133.1 %copy-start.15 = (bf16[128,1024]{1,0:T(8,128)(2,1)S(1)}, bf16[128,1024]{1,0:T(8,128)(2,1)}, u32[]{:S(2)}) copy-start(bf16[128,1024]{1,0:T(8,128)(2,1)} %param.21) | copy-start | bytes 786436
  239.1 12.1 copy-start.3
  239.1 12.8 copy-start.6
  242.0 1.0 copy-start.10
  251.2 0.7 copy-start.28
  251.2 0.7 copy-start.29
  251.2 251.4 %all-gather.7.cloned.1.call-start = ((), (), s32[]{:S(2)}) async-start(), calls=%async_computation.7 | async-start | bytes 9437184 | tf_op jit(solution)/shard_map/all_gather | solution.py:161
  422.0 162.6 %all-gather.9.cloned.1.call-start = ((), (), s32[]{:S(2)}) async-start(), calls=%async_computation.9 | async-start | bytes 9437184 | tf_op jit(solution)/shard_map/all_gather | solution.py:176
  422.6 365.7 %reduce-scatter.12.cloned.1.call-start = ((), (), s32[]{:S(2)}) async-start(), calls=%async_computation.10 | async-start | bytes 18874368 | tf_op jit(solution)/shard_map/reduce_scatter | solution.py:185
  584.6 28.5 %copy-start.30 = (bf16[1024,512]{1,0:T(8,128)(2,1)S(1)}, bf16[1024,512]{1,0:T(8,128)(2,1)}, u32[]{:S(2)}) copy-start(bf16[1024,512]{1,0:T(8,128)(2,1)} %param.24) | copy-start | bytes 3145732
  611.2 1.9 copy-start.31
  621.4 257.1 %reduce-scatter.10.cloned.1.call-start = ((), (), s32[]{:S(2)}) async-start(), calls=%async_computation.8 | async-start | bytes 9437184 | tf_op jit(solution)/shard_map/reduce_scatter | solution.py:169
  641.7 241.7 %copy-start.12 = (bf16[512,1024]{1,0:T(8,128)(2,1)S(1)}, bf16[512,1024]{1,0:T(8,128)(2,1)}, u32[]{:S(2)}) copy-start(bf16[512,1024]{1,0:T(8,128)(2,1)} %param.16) | copy-start | bytes 3145732
  641.7 323.5 %all-gather.11.cloned.1.call-start = ((), (), s32[]{:S(2)}) async-start(), calls=%async_computation.11 | async-start | bytes 9437184 | tf_op jit(solution)/shard_map/all_gather | solution.py:194
  882.0 1.3 copy-start.8
  882.0 1.3 copy-start.22
  884.7 594.4 %all-reduce.3.cloned.1.call-start = ((), (), s32[]{:S(2)}) async-start(), calls=%async_computation.14 | async-start | bytes 6291456 | tf_op jit(solution)/shard_map/psum | solution.py:216
  884.9 10.3 copy-start.32
  903.4 80.5 %copy-start.4 = (bf16[4096,2,64]{0,2,1:T(8,128)(2,1)S(1)}, bf16[4096,2,64]{0,2,1:T(8,128)(2,1)}, u32[]{:S(2)}) copy-start(bf16[4096,2,64]{0,2,1:T(8,128)(2,1)} %copy-done.3) | copy-start | bytes 3145732
  988.7 5.7 copy-start.2
  994.4 7.2 copy-start.7
  1037.2 5.7 copy-start.2
  1043.0 7.6 copy-start.7
  1086.2 5.7 copy-start.2
  1091.9 7.6 copy-start.7
  1135.1 5.7 copy-start.2
  1140.8 7.6 copy-start.7
  1184.0 5.7 copy-start.2
  1189.8 7.6 copy-start.7
  1233.0 5.7 copy-start.2
  1238.7 7.6 copy-start.7
  1281.9 5.7 copy-start.2
  1287.7 7.6 copy-start.7
  1330.9 5.7 copy-start.2
  1336.6 7.6 copy-start.7
  1378.6 4.1 slice-start
  1378.6 4.2 copy-start.11
  1380.6 2.9 slice-start.1
  1382.3 3.1 slice-start.2
  1383.5 2.0 copy-start.9
  1383.5 3.7 slice-start.3
  1387.2 5.5 copy-start.14
  1392.6 257.2 %reduce-scatter.14.cloned.1.call-start = ((), (), s32[]{:S(2)}) async-start(), calls=%async_computation.12 | async-start | bytes 18874368 | tf_op jit(solution)/shard_map/reduce_scatter | solution.py:204
  1402.8 247.1 %copy-start.5 = (bf16[512,1024]{1,0:T(8,128)(2,1)S(1)}, bf16[512,1024]{1,0:T(8,128)(2,1)}, u32[]{:S(2)}) copy-start(bf16[512,1024]{1,0:T(8,128)(2,1)} %param.15) | copy-start | bytes 3145732
  1402.8 247.0 %copy-start.17 = (f32[1024]{0:T(1024)S(1)}, f32[1024]{0:T(1024)}, u32[]{:S(2)}) copy-start(f32[1024]{0:T(1024)} %copy-done.16) | copy-start | bytes 12292
  1402.8 247.0 %copy-start.19 = (f32[512]{0:T(512)S(1)}, f32[512]{0:T(512)}, u32[]{:S(2)}) copy-start(f32[512]{0:T(512)} %copy-done.18) | copy-start | bytes 6148
  1402.8 249.1 %copy-start.25 = (f32[512]{0:T(512)S(1)}, f32[512]{0:T(512)}, u32[]{:S(2)}) copy-start(f32[512]{0:T(512)} %copy-done.24) | copy-start | bytes 6148
  1402.8 249.1 %copy-start.21 = (f32[512]{0:T(512)S(1)}, f32[512]{0:T(512)}, u32[]{:S(2)}) copy-start(f32[512]{0:T(512)} %copy-done.20) | copy-start | bytes 6148
  1402.8 251.7 %copy-start.26 = (f32[1024]{0:T(1024)S(1)}, f32[1024]{0:T(1024)}, u32[]{:S(2)}) copy-start(f32[1024]{0:T(1024)} %get-tuple-element.221) | copy-start | bytes 12292
  1402.8 251.7 %copy-start.27 = (f32[1024]{0:T(1024)S(1)}, f32[1024]{0:T(1024)}, u32[]{:S(2)}) copy-start(f32[1024]{0:T(1024)} %get-tuple-element.226) | copy-start | bytes 12292
  1402.9 282.3 %reduce-scatter.16.cloned.1.call-start = ((), (), s32[]{:S(2)}) async-start(), calls=%async_computation.13 | async-start | bytes 589824
  1479.1 176.6 %copy-start.13 = (bf16[512,1024]{1,0:T(8,128)(2,1)S(1)}, bf16[512,1024]{1,0:T(8,128)(2,1)}, u32[]{:S(2)}) copy-start(bf16[512,1024]{1,0:T(8,128)(2,1)} %param.16) | copy-start | bytes 3145732
  1479.1 176.6 %copy-start.23 = (f32[512]{0:T(512)S(1)}, f32[512]{0:T(512)}, u32[]{:S(2)}) copy-start(f32[512]{0:T(512)} %copy-done.22) | copy-start | bytes 6148
  1486.2 210.3 %copy-start.1 = (bf16[512,1024]{1,0:T(8,128)(2,1)S(1)}, bf16[512,1024]{1,0:T(8,128)(2,1)}, u32[]{:S(2)}) copy-start(bf16[512,1024]{1,0:T(8,128)(2,1)} %param.25) | copy-start | bytes 3145732
Sparse Core Ops, SparseCore 0:
  15.2 84.7 all-gather.4
  251.3 166.7 reduce-scatter.7
  422.1 80.3 all-gather.6
  504.0 80.5 all-gather.8
  621.5 166.7 reduce-scatter.11
  790.5 87.9 reduce-scatter.9
  884.8 80.3 all-gather.10
  1392.7 86.2 all-reduce.2
  1481.6 168.2 reduce-scatter.13
  1655.8 29.3 reduce-scatter.15
where the time goes:
time: 1710 us; the launch traced here: 1700 us
  waiting for transfers between devices  959 us (56%)
  matrix products  430 us (25%)
  other arithmetic  209 us (12%)
  local copies, waits for them, and re-layouts  77.6 us (5%)
    reduce_scatter x1, waiting for transfers between devices, body(): lax.psum_scatter(jnp.dot(selected, proj_weight, preferred_element_type=jn...  166 us
    reduce_scatter x1, waiting for transfers between devices, body(): lax.psum_scatter(jnp.einsum('rc,dc->rd', selected, qkv_weight, preferred_...  161 us
    reduce_scatter x1, waiting for transfers between devices, body(): lax.psum_scatter(jnp.einsum('rf,df->rd', selected, up_weight, preferred_e...  147 us
    dot_general x8, matrix products, one_block(): jnp.einsum('qhd,khd->hqk', grad_block, values_all, preferred_element_type...  101 us
    convert_element_type x8, other arithmetic, one_block(): grad_scores = (probability * (grad_probs - row_inner)).astype(jnp.bfloat16)  98.2 us
    reduce_scatter x1, waiting for transfers between devices, body(): lax.psum_scatter(jnp.dot(selected, down_weight, preferred_element_type=jn...  87.2 us
    all_gather x1, waiting for transfers between devices, body(): normed_all = lax.all_gather(normed, 'narrow', axis=0, tiled=True)  83.9 us
    all_gather x1, waiting for transfers between devices, body(): expand_all = lax.all_gather(expand_in, 'narrow', axis=0, tiled=True)  79.9 us
  transfers between devices with their start and end apart: 10, of which 10 were waited for; matrix products, arithmetic and copies ran while one was open for 5% of the time, Pallas kernels for 0%

commit v1 on v0

v1 whole, which is shorter than its diff:
```python
import functools

import jax
import jax.numpy as jnp
from jax import lax
from jax.experimental import pallas as pl
from jax.experimental.pallas import tpu as pltpu
from jax.sharding import PartitionSpec as P

HEAD_DIM = 64
EXTRA = 16
EXCLUDED = -1e30
bf16 = jnp.bfloat16
f32 = jnp.float32
epsilon = 1e-05


def norm_forward(values, norm_gain, norm_bias):
    average = jnp.mean(values, axis=-1, keepdims=True)
    centred = values - average
    variance = jnp.mean(centred * centred, axis=-1, keepdims=True)
    return centred * lax.rsqrt(variance + epsilon) * norm_gain + norm_bias


def gelu_exact(values):
    return jax.nn.gelu(values, approximate=False)


def mask_rows(item_lengths, rows):
    lengths = item_lengths[0]
    items = lengths.shape[0]
    index = jnp.arange(items)
    ends = jnp.sum(jnp.where(index[:, None] >= index[None, :], lengths[None, :], 0), axis=1)
    segment = jnp.sum((jnp.arange(rows)[None, :] >= ends[:, None]).astype(jnp.int32), axis=0)
    extra = jnp.arange(EXTRA)[:, None]
    own = segment[None, :] == extra
    query_extra = jnp.where(own & (extra <= items), 1.0, 0.0).astype(bf16)
    key_extra = jnp.where(
        extra <= items,
        jnp.where(own, 0.0, EXCLUDED),
        jnp.where(extra <= items + 3, 1.0, 0.0),
    ).astype(bf16)
    return query_extra, key_extra


def forward_kernel(block, rows, qx_ref, kx_ref, q_ref, k_ref, v_ref, o_ref, log_ref, keys):
    width = q_ref.shape[-1]

    @pl.when(pl.program_id(1) == 0)
    def _():
        keys[...] = jnp.concatenate([k_ref[0], kx_ref[...]], axis=0).T

    query = jnp.concatenate([q_ref[0] * jnp.asarray(0.125, bf16), qx_ref[...]], axis=0)
    maximum = jnp.full((1, width), -3e38, f32)
    total = jnp.zeros((1, width), f32)
    gathered = jnp.zeros((HEAD_DIM, width), f32)
    for i in range(rows // block):
        part = pl.ds(i * block, block)
        scores = jnp.dot(keys[part, :], query, preferred_element_type=f32)
        larger = jnp.maximum(maximum, jnp.max(scores, axis=0, keepdims=True))
        raised = jnp.exp(scores - larger)
        shrink = jnp.exp(maximum - larger)
        total = shrink * total + jnp.sum(raised, axis=0, keepdims=True)
        gathered = shrink * gathered + jnp.dot(
            v_ref[0, :, part], raised.astype(bf16), preferred_element_type=f32
        )
        maximum = larger
    o_ref[0] = (gathered / total).astype(bf16)
    log_ref[0] = maximum + jnp.log(total)


def attend_forward(packed, query_extra, key_extra, width=1024, block=1024):
    heads, _, _, rows = packed.shape

    def whole(j):
        return pl.BlockSpec((1, None, HEAD_DIM, rows), lambda h, i: (h, j, 0, 0))

    return pl.pallas_call(
        functools.partial(forward_kernel, block, rows),
        grid=(heads, rows // width),
        in_specs=[
            pl.BlockSpec((EXTRA, width), lambda h, i: (0, i)),
            pl.BlockSpec((EXTRA, rows), lambda h, i: (0, 0)),
            pl.BlockSpec((1, None, HEAD_DIM, width), lambda h, i: (h, 0, 0, i)),
            whole(1),
            whole(2),
        ],
        out_specs=(
            pl.BlockSpec((1, HEAD_DIM, width), lambda h, i: (h, 0, i)),
            pl.BlockSpec((1, 1, width), lambda h, i: (h, 0, i)),
        ),
        out_shape=(
            jax.ShapeDtypeStruct((heads, HEAD_DIM, rows), bf16),
            jax.ShapeDtypeStruct((heads, 1, rows), f32),
        ),
        scratch_shapes=[pltpu.VMEM((rows, HEAD_DIM + EXTRA), bf16)],
        compiler_params=pltpu.CompilerParams(vmem_limit_bytes=48 << 20),
        cost_estimate=pl.CostEstimate(
            flops=4 * heads * rows * rows * 256,
            bytes_accessed=heads * rows * HEAD_DIM * 8,
            transcendentals=heads * rows * rows,
        ),
        name="attend_forward",
    )(query_extra, key_extra, packed, packed, packed)


def backward_kernel(
    block, rows, items, qx_ref, kx_ref, q_ref, k_ref, v_ref, o_ref, do_ref, log_ref,
    grad_ref, keys, values, grad_k, grad_v,
):
    width = q_ref.shape[-1]
    step = pl.program_id(1)

    @pl.when(step == 0)
    def _():
        keys[...] = jnp.concatenate([k_ref[0], kx_ref[...]], axis=0)
        values[...] = jnp.concatenate([v_ref[0], kx_ref[...]], axis=0)
        grad_k[...] = jnp.zeros_like(grad_k)
        grad_v[...] = jnp.zeros_like(grad_v)

    row = lax.broadcasted_iota(jnp.int32, (EXTRA, width), 0) - items

    def pieces(term, base):
        high = term.astype(bf16).astype(f32)
        middle = (term - high).astype(bf16).astype(f32)
        small = term - high - middle
        return jnp.where(
            row == 1, high, jnp.where(row == 2, middle, jnp.where(row == 3, small, base))
        ).astype(bf16)

    query = q_ref[0] * jnp.asarray(0.125, bf16)
    grad = do_ref[0]
    inner = jnp.sum(grad.astype(f32) * o_ref[0].astype(f32), axis=0, keepdims=True)
    query_wide = jnp.concatenate(
        [query, pieces(-log_ref[0], qx_ref[...].astype(f32))], axis=0
    ).T
    grad_wide = jnp.concatenate(
        [grad, pieces(-inner, jnp.zeros((EXTRA, width), f32))], axis=0
    ).T
    grad_q = jnp.zeros((HEAD_DIM, width), f32)
    for i in range(rows // block):
        part = pl.ds(i * block, block)
        probs = jnp.exp(jnp.dot(query_wide, keys[:, part], preferred_element_type=f32))
        grad_scores = (
            probs * jnp.dot(grad_wide, values[:, part], preferred_element_type=f32)
        ).astype(bf16)
        grad_v[:, part] += jnp.dot(grad, probs.astype(bf16), preferred_element_type=f32)
        grad_k[:, part] += jnp.dot(query, grad_scores, preferred_element_type=f32)
        grad_q += lax.dot_general(
            k_ref[0, :, part], grad_scores, (((1,), (1,)), ((), ())), preferred_element_type=f32
        )
    grad_ref[0, 0, :, pl.ds(pl.multiple_of(step * width, width), width)] = (
        grad_q * 0.125
    ).astype(bf16)

    @pl.when(step == pl.num_programs(1) - 1)
    def _():
        grad_ref[0, 1] = grad_k[...].astype(bf16)
        grad_ref[0, 2] = grad_v[...].astype(bf16)


def attend_backward(packed, query_extra, key_extra, attended, grad, log_total, items, width=1024, block=512):
    heads, _, _, rows = packed.shape

    def whole(j):
        return pl.BlockSpec((1, None, HEAD_DIM, rows), lambda h, i: (h, j, 0, 0))

    part = pl.BlockSpec((1, HEAD_DIM, width), lambda h, i: (h, 0, i))
    return pl.pallas_call(
        functools.partial(backward_kernel, block, rows, items),
        grid=(heads, rows // width),
        in_specs=[
            pl.BlockSpec((EXTRA, width), lambda h, i: (0, i)),
            pl.BlockSpec((EXTRA, rows), lambda h, i: (0, 0)),
            pl.BlockSpec((1, None, HEAD_DIM, width), lambda h, i: (h, 0, 0, i)),
            whole(1),
            whole(2),
            part,
            part,
            pl.BlockSpec((1, 1, width), lambda h, i: (h, 0, i)),
        ],
        out_specs=pl.BlockSpec((1, 3, HEAD_DIM, rows), lambda h, i: (h, 0, 0, 0)),
        out_shape=jax.ShapeDtypeStruct((heads, 3, HEAD_DIM, rows), bf16),
        scratch_shapes=[
            pltpu.VMEM((HEAD_DIM + EXTRA, rows), bf16),
            pltpu.VMEM((HEAD_DIM + EXTRA, rows), bf16),
            pltpu.VMEM((HEAD_DIM, rows), f32),
            pltpu.VMEM((HEAD_DIM, rows), f32),
        ],
        compiler_params=pltpu.CompilerParams(vmem_limit_bytes=48 << 20),
        cost_estimate=pl.CostEstimate(
            flops=10 * heads * rows * rows * 256,
            bytes_accessed=heads * rows * HEAD_DIM * 16,
            transcendentals=heads * rows * rows,
        ),
        name="attend_backward",
    )(query_extra, key_extra, packed, packed, packed, attended, grad, log_total)


def product(spec, left, right):
    return jnp.einsum(spec, left, right, preferred_element_type=f32)


def scatter_rows(partial_sum):
    return lax.psum_scatter(
        partial_sum.astype(bf16), "narrow", scatter_dimension=0, tiled=True
    ).astype(f32)


def body(
    tokens, cotangent, item_lengths, attn_gain, attn_bias, qkv_weight, proj_weight,
    mlp_gain, mlp_bias, up_weight, down_weight,
):
    items = item_lengths.shape[1]
    token_rows = tokens.astype(f32)
    heads = qkv_weight.shape[1] // (3 * HEAD_DIM)
    gain_one, bias_one = attn_gain.astype(f32), attn_bias.astype(f32)
    gain_two, bias_two = mlp_gain.astype(f32), mlp_bias.astype(f32)
    normed = norm_forward(token_rows, gain_one, bias_one).astype(bf16)
    normed_all = lax.all_gather(normed, "narrow", axis=0, tiled=True)
    rows = normed_all.shape[0]
    query_extra, key_extra = mask_rows(item_lengths, rows)
    packed = (
        product("rd,dc->cr", normed_all, qkv_weight).astype(bf16).reshape(heads, 3, HEAD_DIM, rows)
    )
    attended, log_total = attend_forward(packed, query_extra, key_extra)
    attended_flat = attended.reshape(heads * HEAD_DIM, rows)
    branch = scatter_rows(product("ar,ad->rd", attended_flat, proj_weight))
    middle = token_rows + branch
    expand_in = norm_forward(middle, gain_two, bias_two).astype(bf16)
    expand_all = lax.all_gather(expand_in, "narrow", axis=0, tiled=True)
    hidden_pre = product("rd,df->rf", expand_all, up_weight)
    hidden = gelu_exact(hidden_pre).astype(bf16)
    output = (middle + scatter_rows(product("rf,fd->rd", hidden, down_weight))).astype(bf16)

    grad_rows = lax.all_gather(cotangent, "narrow", axis=0, tiled=True)
    grad_down = product("rf,rd->fd", hidden, grad_rows)
    grad_hidden = product("rd,fd->rf", grad_rows, down_weight)
    grad_pre = jax.vjp(gelu_exact, hidden_pre)[1](grad_hidden)[0].astype(bf16)
    grad_up = product("rd,rf->df", expand_all, grad_pre)
    grad_expand = scatter_rows(product("rf,df->rd", grad_pre, up_weight))
    grad_middle_norm, grad_gain_two, grad_bias_two = jax.vjp(
        norm_forward, middle, gain_two, bias_two
    )[1](grad_expand)
    grad_middle = cotangent.astype(f32) + grad_middle_norm
    grad_branch_all = lax.all_gather(grad_middle.astype(bf16), "narrow", axis=0, tiled=True)
    grad_proj = product("ar,rd->ad", attended_flat, grad_branch_all)
    grad_attended = (
        product("rd,ad->ar", grad_branch_all, proj_weight)
        .astype(bf16)
        .reshape(heads, HEAD_DIM, rows)
    )
    grad_packed = attend_backward(
        packed, query_extra, key_extra, attended, grad_attended, log_total, items
    ).reshape(heads * 3 * HEAD_DIM, rows)
    grad_qkv = product("rd,cr->dc", normed_all, grad_packed)
    grad_normed = scatter_rows(product("cr,dc->rd", grad_packed, qkv_weight))
    grad_token_norm, grad_gain_one, grad_bias_one = jax.vjp(
        norm_forward, token_rows, gain_one, bias_one
    )[1](grad_normed)
    grad_tokens = (grad_middle + grad_token_norm).astype(bf16)
    norm_parts = jnp.stack([grad_gain_one, grad_bias_one, grad_gain_two, grad_bias_two])
    norm_shares = lax.psum_scatter(norm_parts, "narrow", scatter_dimension=1, tiled=True)

    def over_items(share):
        return lax.psum(share.astype(bf16), "wide").astype(f32)

    shares = over_items(norm_shares)
    return (
        output, grad_tokens, shares[0], shares[1], over_items(grad_qkv), over_items(grad_proj),
        shares[2], shares[3], over_items(grad_up), over_items(grad_down),
    )


def solution(mesh):
    by_rows = P(("wide", "narrow"), None)
    return jax.shard_map(
        body,
        mesh=mesh,
        in_specs=(
            by_rows, by_rows, P("wide", None), P(), P(), P(None, "narrow"), P("narrow", None),
            P(), P(), P(None, "narrow"), P("narrow", None),
        ),
        out_specs=(
            by_rows, by_rows, P("narrow"), P("narrow"), P(None, "narrow"), P("narrow", None),
            P("narrow"), P("narrow"), P(None, "narrow"), P("narrow", None),
        ),
        check_vma=False,
    )
```

time: 1710 us -> 1060 us (0.62)
  matrix products: 430 us -> 111 us
  waiting for transfers between devices: 959 us -> 726 us
  other arithmetic: 209 us -> 50.7 us
  Pallas kernels: 0 us -> 130 us
  local copies, waits for them, and re-layouts: 77.6 us -> 6.49 us
    dot_general x68 -> x12, matrix products: 430 us -> 111 us  [product(): return jnp.einsum(spec, left, right, preferred_element_type=f32)]
    reduce_scatter x4, waiting for transfers between devices: 561 us -> 326 us  [scatter_rows(): lax.psum_scatter(partial_sum.astype(bf16), 'narrow', scatter_dimension=0,...]
    pallas_call x0 -> x2, Pallas kernels: none -> 130 us  [the longest x1 83.1 us: attend_backward(): pl.pallas_call(functools.partial(backward_kernel, block, rows, items), gr...]
    convert_element_type x22 -> x16, other arithmetic: 129 us -> 33.5 us  [the longest x1 10.8 us: body(): hidden = gelu_exact(hidden_pre).astype(bf16)]
    while x35 -> x0, local copies, waits for them, and re-layouts: 51.5 us -> none
    reduce_sum x9 -> x2, other arithmetic: 36.8 us -> 0.89 us  [the longest x1 0.77 us: mask_rows(): jnp.sum(jnp.where(index[:, None] >= index[None, :], lengths[None, :], 0),...]
    eq x16 -> x0, other arithmetic: 21 us -> none  [block_scores(): same_item = segment_block[:, None] == segment[None, :]]
  transfers between devices with their start and end apart: 10 -> 10, of which waited for: 10 -> 10; matrix products, arithmetic and copies ran while one was open for 5% -> 7% of each run, Pallas kernels for 0% -> 0%
where the time goes in v1:
time: 1060 us; the launch traced here: 1050 us
  waiting for transfers between devices  726 us (68%)
  Pallas kernels  130 us (12%)
  matrix products  111 us (10%)
  other arithmetic  50.7 us (5%)
  between operations  14.9 us (1%)
    reduce_scatter x4, waiting for transfers between devices, scatter_rows(): lax.psum_scatter(partial_sum.astype(bf16), 'narrow', scatter_dimension=0,...  326 us
    dot_general x12, matrix products, product(): return jnp.einsum(spec, left, right, preferred_element_type=f32)  111 us
    all_gather x1, waiting for transfers between devices, body(): normed_all = lax.all_gather(normed, 'narrow', axis=0, tiled=True)  83.7 us
    pallas_call x1, Pallas kernels, attend_backward(): pl.pallas_call(functools.partial(backward_kernel, block, rows, items), gr...  83.1 us
    all_gather x1, waiting for transfers between devices, body(): expand_all = lax.all_gather(expand_in, 'narrow', axis=0, tiled=True)  79.9 us
    psum x1, waiting for transfers between devices, over_items(): return lax.psum(share.astype(bf16), 'wide').astype(f32)  77.5 us
    all_gather x1, waiting for transfers between devices, body(): grad_rows = lax.all_gather(cotangent, 'narrow', axis=0, tiled=True)  70.4 us
    all_gather x1, waiting for transfers between devices, body(): lax.all_gather(grad_middle.astype(bf16), 'narrow', axis=0, tiled=True)  62 us
  transfers between devices with their start and end apart: 10, of which 10 were waited for; matrix products, arithmetic and copies ran while one was open for 7% of the time, Pallas kernels for 0%

profile of v1, /device:TPU:0, one launch (start us, length us, event | category | flops | bytes accessed | tf_op | source)
XLA Modules:
  0.0 1050.0 jit_solution(5522254011439952715)
XLA Ops:
  7.2 1.5 convert_reduce_fusion.2
  8.8 1.6 fusion.17
  10.4 0.6 copy-done.15
  11.0 0.7 convert_element_type.118
  11.7 0.7 convert_element_type.119
  12.4 2.6 fusion.15
  15.0 0.0 reduce-scatter.8.cloned.1.call-start
  15.2 0.8 select_reduce_fusion
  15.9 0.1 convert_reduce_fusion.3
  16.0 0.1 select_convert_fusion.1.qx_ref
  16.2 0.1 select_convert_fusion.kx_ref
  16.2 83.7 %all-gather.5.cloned.1.call-done = bf16[4096,1024]{1,0:T(8,128)(2,1)} async-done(((bf16[512,1024]{1,0:T(8,128)(2,1)}), bf16[4096,1024]{1,0:T(8,128)(2,1)}) %all-gather.5.cloned.1.call-update) | async-done | bytes 8388624 | tf_op jit(solution)/shard_map/all_gather | solution.py:220
  100.0 7.0 convolution_convert_fusion.4
  107.0 46.8 %attend_forward.1 = (bf16[2,64,4096]{2,1,0:T(8,128)(2,1)S(1)}, f32[2,1,4096]{2,1,0:T(1,128)S(1)}) custom-call(bf16[16,4096]{1,0:T(8,128)(2,1)S(1)} %select_convert_fusion.1.qx_ref, bf16[16,4096]{1,0:T(8,128)(2,1)S(1)} %select_convert_fusion.kx_ref, bf16[2,3,64,4096]{3,2,1,0:T(8,128)(2,1)S(1)} %bitcast.49, bf16[2,3,64,4096]{3,2,1,0:T(8,128)(2,1)S(1)} %bitcast.50, ...), custom_call_target="tpu_custom_call" | custom-call | flops 34359738368 | bytes 4194304 | tf_op jit(solution)/shard_map/attend_forward/pallas_call | solution.py:78
  153.8 5.6 convolution_convert_fusion.3
  159.4 0.5 all-gather.7.cloned.1.call-start
  160.0 87.7 %reduce-scatter.8.cloned.1.call-done = bf16[512,1024]{1,0:T(8,128)(2,1)} async-done(((bf16[4096,1024]{1,0:T(8,128)(2,1)}), bf16[512,1024]{1,0:T(8,128)(2,1)}) %reduce-scatter.8.cloned.1.call-update) | async-done | bytes 1048592 | tf_op jit(solution)/shard_map/reduce_scatter | solution.py:205
  247.7 1.6 fusion.22
  249.3 1.7 multiply_reduce_fusion
  251.0 2.7 add_convert_fusion.3
  253.8 0.0 all-gather.9.cloned.1.call-start
  253.9 0.5 all-gather.9.cloned.1.call-update
  254.4 0.0 reduce-scatter.12.cloned.1.call-start
  254.4 79.9 %all-gather.7.cloned.1.call-done = bf16[4096,1024]{1,0:T(8,128)(2,1)} async-done(((bf16[512,1024]{1,0:T(8,128)(2,1)}), bf16[4096,1024]{1,0:T(8,128)(2,1)}) %all-gather.7.cloned.1.call-update) | async-done | bytes 8388624 | tf_op jit(solution)/shard_map/all_gather | solution.py:231
  334.4 11.7 %fusion.30 = f32[4096,512]{1,0:T(8,128)} fusion(bf16[4096,1024]{1,0:T(8,128)(2,1)} %all-gather.7.cloned.1.call-done, bf16[1024,512]{1,0:T(8,128)(2,1)} %param.20), kind=kOutput, calls=%fused_computation.88 | convolution fusion | flops 4294967296 | bytes 17825792 | tf_op jit(solution)/shard_map/rd,df->rf/dot_general | solution.py:201
  346.0 70.4 %all-gather.9.cloned.1.call-done = bf16[4096,1024]{1,0:T(8,128)(2,1)} async-done(((bf16[512,1024]{1,0:T(8,128)(2,1)}), bf16[4096,1024]{1,0:T(8,128)(2,1)}) %all-gather.9.cloned.1.call-update) | async-done | bytes 8388624 | tf_op jit(solution)/shard_map/all_gather | solution.py:236
  416.4 26.6 %add_convert_fusion = (bf16[4096,512]{1,0:T(8,128)(2,1)S(1)}, f32[4096,512]{1,0:T(8,128)}) fusion(f32[4096,512]{1,0:T(8,128)} %fusion.30, bf16[4096,1024]{1,0:T(8,128)(2,1)} %all-gather.9.cloned.1.call-done, bf16[512,1024]{1,0:T(8,128)(2,1)S(1)} %copy-done), kind=kOutput, calls=%fused_computation.2 | convolution fusion | flops 4445962240 | bytes 30408704 | tf_op jit(solution)/shard_map/rd,fd->rf/dot_general | solution.py:201
  443.0 2.0 copy-done.21
  445.0 7.2 convolution_convert_fusion.1
  452.2 0.2 reduce-scatter.10.cloned.1.call-start
  452.5 10.8 %multiply_convert_fusion = bf16[4096,512]{1,0:T(8,128)(2,1)} fusion(f32[4096,512]{1,0:T(8,128)} %get-tuple-element.27, f32[4096,512]{1,0:T(8,128)} %fusion.30), kind=kLoop, calls=%fused_computation.3 | loop fusion | flops 6291456 | bytes 20971520 | tf_op jit(solution)/shard_map/convert_element_type | solution.py:233
  463.2 9.0 convolution_convert_fusion.2
  472.3 0.0 all-gather.11.cloned.1.call-start
  472.3 68.2 %reduce-scatter.12.cloned.1.call-done = bf16[512,1024]{1,0:T(8,128)(2,1)} async-done(((bf16[4096,1024]{1,0:T(8,128)(2,1)}), bf16[512,1024]{1,0:T(8,128)(2,1)}) %reduce-scatter.12.cloned.1.call-update) | async-done | bytes 1048592 | tf_op jit(solution)/shard_map/reduce_scatter | solution.py:205
  540.6 2.2 fusion.19
  542.8 87.9 %reduce-scatter.10.cloned.1.call-done = bf16[512,1024]{1,0:T(8,128)(2,1)} async-done(((bf16[4096,1024]{1,0:T(8,128)(2,1)}), bf16[512,1024]{1,0:T(8,128)(2,1)}) %reduce-scatter.10.cloned.1.call-update) | async-done | bytes 1048592 | tf_op jit(solution)/shard_map/reduce_scatter | solution.py:205
  630.7 3.5 fusion.28
  634.2 1.3 copy-done.6
  635.5 2.5 fusion.24
  638.1 0.0 all-reduce.3.cloned.1.call-start
  638.1 10.3 convolution_convert_fusion.6
  648.4 8.3 convolution_convert_fusion.7
  656.7 62.0 %all-gather.11.cloned.1.call-done = bf16[4096,1024]{1,0:T(8,128)(2,1)} async-done(((bf16[512,1024]{1,0:T(8,128)(2,1)}), bf16[4096,1024]{1,0:T(8,128)(2,1)}) %all-gather.11.cloned.1.call-update) | async-done | bytes 8388624 | tf_op jit(solution)/shard_map/all_gather | solution.py:246
  718.6 6.4 convolution_convert_fusion.5
  725.0 83.1 %attend_backward.1 = bf16[2,3,64,4096]{3,2,1,0:T(8,128)(2,1)S(1)} custom-call(bf16[16,4096]{1,0:T(8,128)(2,1)S(1)} %select_convert_fusion.1.qx_ref, bf16[16,4096]{1,0:T(8,128)(2,1)S(1)} %select_convert_fusion.kx_ref, bf16[2,3,64,4096]{3,2,1,0:T(8,128)(2,1)} %bitcast.52, bf16[2,3,64,4096]{3,2,1,0:T(8,128)(2,1)} %bitcast.53, ...), custom_call_target="tpu_custom_call" | custom-call | flops 85899345920 | bytes 8388608 | tf_op jit(solution)/shard_map/attend_backward/pallas_call | solution.py:169
  808.2 2.0 convolution_convert_fusion.9
  810.2 8.0 convolution_convert_fusion.8
  818.2 0.0 reduce-scatter.14.cloned.1.call-start
  818.3 8.8 convolution_convert_fusion
  827.1 0.0 reduce-scatter.16.cloned.1.call-start
  827.2 77.5 %all-reduce.3.cloned.1.call-done = (bf16[1024,384]{1,0:T(8,128)(2,1)}, bf16[128,1024]{1,0:T(8,128)(2,1)}, bf16[1024,512]{1,0:T(8,128)(2,1)}, bf16[512,1024]{1,0:T(8,128)(2,1)}) async-done(((bf16[1024,384]{1,0:T(8,128)(2,1)}, bf16[128,1024]{1,0:T(8,128)(2,1)}, bf16[1024,512]{1,0:T(8,128)(2,1)}, bf16[512,1024]{1,0:T(8,128)(2,1)}), (bf16[1024,384]{1,0:T(8,128)(2,1)}, bf16[128,1024]{1,0:T(8,128)(2,1)}, ...) | async-done | bytes 3145744 | tf_op jit(solution)/shard_map/psum | solution.py:266
  904.7 1.8 convert_element_type.147
  906.5 2.4 convert_element_type.145
  908.8 2.9 convert_element_type.149
  911.8 2.8 convert_element_type.151
  914.6 82.1 %reduce-scatter.14.cloned.1.call-done = bf16[512,1024]{1,0:T(8,128)(2,1)} async-done(((bf16[4096,1024]{1,0:T(8,128)(2,1)}), bf16[512,1024]{1,0:T(8,128)(2,1)}) %reduce-scatter.14.cloned.1.call-update) | async-done | bytes 1048592 | tf_op jit(solution)/shard_map/reduce_scatter | solution.py:205
  996.7 1.8 fusion.18
  998.5 2.3 fusion.20
  1000.9 1.0 copy.21
  1001.9 3.3 add_convert_fusion.1
  1005.2 26.2 %reduce-scatter.16.cloned.1.call-done = f32[128,4]{1,0:T(8,128)} async-done(((f32[1024,4]{1,0:T(8,128)}), f32[128,4]{1,0:T(8,128)}) %reduce-scatter.16.cloned.1.call-update) | async-done | bytes 2064
  1031.4 0.9 copy.22
  1032.3 9.8 psum.35
  1042.2 0.5 slice_bitcast_fusion
  (72 shorter events, 0.4 us)
Async XLA Ops:
  7.2 409.3 %copy-start = (bf16[512,1024]{1,0:T(8,128)(2,1)S(1)}, bf16[512,1024]{1,0:T(8,128)(2,1)}, u32[]{:S(2)}) copy-start(bf16[512,1024]{1,0:T(8,128)(2,1)} %param.21) | copy-start | bytes 3145732
  7.2 92.8 %all-gather.5.cloned.1.call-start = ((), (), s32[]{:S(2)}) async-start(), calls=%async_computation.5 | async-start | bytes 9437184 | tf_op jit(solution)/shard_map/all_gather | solution.py:220
  8.8 6.4 copy-start.11
  10.4 0.6 copy-start.15
  11.0 4.1 copy-start.13
  11.7 3.5 copy-start.9
  15.0 232.7 %reduce-scatter.8.cloned.1.call-start = ((), (), s32[]{:S(2)}) async-start(), calls=%async_computation.6 | async-start | bytes 9437184 | tf_op jit(solution)/shard_map/reduce_scatter | solution.py:205
  107.0 46.8 %copy-start.2 = (bf16[4096,384]{0,1:T(8,128)(2,1)}, bf16[4096,384]{0,1:T(8,128)(2,1)S(1)}, u32[]{:S(2)}) copy-start(bf16[4096,384]{0,1:T(8,128)(2,1)S(1)} %convolution_convert_fusion.4) | copy-start | bytes 9437188
  107.0 46.8 %copy-start.8 = (bf16[128,1024]{1,0:T(8,128)(2,1)S(1)}, bf16[128,1024]{1,0:T(8,128)(2,1)}, u32[]{:S(2)}) copy-start(bf16[128,1024]{1,0:T(8,128)(2,1)} %param.17) | copy-start | bytes 786436
  153.8 6.2 copy-start.17
  153.8 6.2 copy-start.18
  153.8 93.9 %copy-start.4 = (bf16[512,1024]{1,0:T(8,128)(2,1)S(1)}, bf16[512,1024]{1,0:T(8,128)(2,1)}, u32[]{:S(2)}) copy-start(bf16[512,1024]{1,0:T(8,128)(2,1)} %param.11) | copy-start | bytes 3145732
  159.4 174.9 %all-gather.7.cloned.1.call-start = ((), (), s32[]{:S(2)}) async-start(), calls=%async_computation.7 | async-start | bytes 9437184 | tf_op jit(solution)/shard_map/all_gather | solution.py:231
  253.8 162.6 %all-gather.9.cloned.1.call-start = ((), (), s32[]{:S(2)}) async-start(), calls=%async_computation.9 | async-start | bytes 9437184 | tf_op jit(solution)/shard_map/all_gather | solution.py:236
  254.4 286.2 %reduce-scatter.12.cloned.1.call-start = ((), (), s32[]{:S(2)}) async-start(), calls=%async_computation.10 | async-start | bytes 9437184 | tf_op jit(solution)/shard_map/reduce_scatter | solution.py:205
  416.4 28.6 %copy-start.19 = (bf16[1024,512]{1,0:T(8,128)(2,1)S(1)}, bf16[1024,512]{1,0:T(8,128)(2,1)}, u32[]{:S(2)}) copy-start(bf16[1024,512]{1,0:T(8,128)(2,1)} %param.20) | copy-start | bytes 3145732
  443.0 2.0 copy-start.21
  452.2 178.4 %reduce-scatter.10.cloned.1.call-start = ((), (), s32[]{:S(2)}) async-start(), calls=%async_computation.8 | async-start | bytes 9437184 | tf_op jit(solution)/shard_map/reduce_scatter | solution.py:205
  472.3 68.3 %copy-start.5 = (bf16[512,1024]{1,0:T(8,128)(2,1)S(1)}, bf16[512,1024]{1,0:T(8,128)(2,1)}, u32[]{:S(2)}) copy-start(bf16[512,1024]{1,0:T(8,128)(2,1)} %reduce-scatter.8.cloned.1.call-done) | copy-start | bytes 3145732
  472.3 246.3 %all-gather.11.cloned.1.call-start = ((), (), s32[]{:S(2)}) async-start(), calls=%async_computation.11 | async-start | bytes 9437184 | tf_op jit(solution)/shard_map/all_gather | solution.py:246
  634.2 1.3 copy-start.6
  638.1 266.6 %all-reduce.3.cloned.1.call-start = ((), (), s32[]{:S(2)}) async-start(), calls=%async_computation.14 | async-start | bytes 6291456 | tf_op jit(solution)/shard_map/psum | solution.py:266
  638.1 10.3 copy-start.22
  718.6 89.5 %slice-start = ((s8[8388608]{0:T(1024)(128)(4,1)}), s8[4194304]{0:T(1024)(128)(4,1)S(1)}, s32[]{:S(2)}) async-start(s8[8388608]{0:T(1024)(128)(4,1)} %bitcast.58), calls=%async_computation.15 | async-start | bytes 8388608
  725.0 83.2 %slice-start.1 = ((s8[8388608]{0:T(1024)(128)(4,1)}), s8[4194304]{0:T(1024)(128)(4,1)S(1)}, s32[]{:S(2)}) async-start(s8[8388608]{0:T(1024)(128)(4,1)} %bitcast.58), calls=%async_computation.16 | async-start | bytes 8388608
  808.2 2.0 copy-start.3
  810.2 8.1 copy-start.20
  818.2 178.5 %reduce-scatter.14.cloned.1.call-start = ((), (), s32[]{:S(2)}) async-start(), calls=%async_computation.12 | async-start | bytes 9437184 | tf_op jit(solution)/shard_map/reduce_scatter | solution.py:205
  827.1 169.7 %copy-start.10 = (f32[1024]{0:T(1024)S(1)}, f32[1024]{0:T(1024)}, u32[]{:S(2)}) copy-start(f32[1024]{0:T(1024)} %copy-done.9) | copy-start | bytes 12292
  827.1 169.7 %copy-start.12 = (f32[512]{0:T(512)S(1)}, f32[512]{0:T(512)}, u32[]{:S(2)}) copy-start(f32[512]{0:T(512)} %copy-done.11) | copy-start | bytes 6148
  827.1 171.4 %copy-start.16 = (f32[512]{0:T(512)S(1)}, f32[512]{0:T(512)}, u32[]{:S(2)}) copy-start(f32[512]{0:T(512)} %copy-done.15) | copy-start | bytes 6148
  827.1 171.4 %copy-start.14 = (f32[512]{0:T(512)S(1)}, f32[512]{0:T(512)}, u32[]{:S(2)}) copy-start(f32[512]{0:T(512)} %copy-done.13) | copy-start | bytes 6148
  827.1 174.8 %copy-start.7 = (bf16[512,1024]{1,0:T(8,128)(2,1)S(1)}, bf16[512,1024]{1,0:T(8,128)(2,1)}, u32[]{:S(2)}) copy-start(bf16[512,1024]{1,0:T(8,128)(2,1)} %param.12) | copy-start | bytes 3145732
  827.1 204.3 %reduce-scatter.16.cloned.1.call-start = ((), (), s32[]{:S(2)}) async-start(), calls=%async_computation.13 | async-start | bytes 589824
  908.8 133.9 %copy-start.1 = (bf16[512,1024]{1,0:T(8,128)(2,1)S(1)}, bf16[512,1024]{1,0:T(8,128)(2,1)}, u32[]{:S(2)}) copy-start(bf16[512,1024]{1,0:T(8,128)(2,1)} %param.21) | copy-start | bytes 3145732
Sparse Core Ops, SparseCore 0:
  15.2 84.7 all-gather.4
  159.5 88.1 reduce-scatter.7
  253.9 80.3 all-gather.6
  335.8 80.5 all-gather.8
  452.4 88.1 reduce-scatter.11
  542.7 87.9 reduce-scatter.9
  638.2 80.4 all-gather.10
  818.3 86.3 all-reduce.2
  907.1 89.5 reduce-scatter.13
  1002.0 29.3 reduce-scatter.15

commit v2 on v1

--- a/solution.py
+++ b/solution.py
@@ -1,4 +1,5 @@
 import functools
+import math
 
 import jax
 import jax.numpy as jnp
@@ -12,6 +13,7 @@
 EXCLUDED = -1e30
 bf16 = jnp.bfloat16
 f32 = jnp.float32
+MESH = pl.DeviceIdType.MESH
 epsilon = 1e-05
 
 
@@ -207,6 +209,133 @@
     ).astype(f32)
 
 
+def greet(W,N,w,n):
+    bar=pltpu.get_barrier_semaphore()
+    z=n//2; core=lax.rem(n,2)
+    def col(t,_):
+        nn=lax.rem(n+t,N)
+        pl.semaphore_signal(bar,inc=1,device_id=(w,nn),device_id_type=MESH); return 0
+    lax.fori_loop(1,N,col,0)
+    def plane(t,_):
+        ww=lax.rem(w+t,W)
+        pl.semaphore_signal(bar,inc=1,device_id=(ww,n),device_id_type=MESH); return 0
+    lax.fori_loop(1,W,plane,0)
+    pl.semaphore_wait(bar,N-1+W-1)
+
+def gather_kernel(W,N,own,out,lsem,s1,s1b,r1,s2,r2,s3,r3,fs0,fr0,fs1,fr1,fs2,fr2,fs3,fr3):
+    w=lax.axis_index("wide"); n=lax.axis_index("narrow")
+    W1=math.isqrt(W); H=N//2
+    a=w//W1; b=lax.rem(w,W1); z=n//2; core=lax.rem(n,2); sib=n+1-2*core
+    greet(W,N,w,n)
+    def rc(src,dst,ss,rs,dw,dn):
+        return pltpu.make_async_remote_copy(src_ref=src,dst_ref=dst,send_sem=ss,recv_sem=rs,device_id=(dw,dn),device_id_type=MESH)
+    def arrived(ref,sem):
+        pltpu.make_async_copy(ref,ref,sem).wait()
+    oa=lambda i: lax.rem(a+i,W1)
+    ob=lambda i: lax.rem(b+i,W1)
+    def d1(zs,step):
+        return rc(out.at[2*zs+core,a,b],out.at[2*zs+core,a,b],s1b.at[zs],r1.at[zs],w,n+2*step)
+    def own1(step):
+        return rc(own.at[a,b],out.at[n,a,b],s1.at[z+step],r1.at[z],w,n+2*step)
+    def d2(ns,zs,h,i):
+        if h==0: return rc(out.at[ns,a,b,0],out.at[ns,a,b,0],s2.at[zs,0,i],r2.at[zs,0,b],a*W1+ob(i),n)
+        return rc(out.at[ns,a,b,1],out.at[ns,a,b,1],s2.at[zs,1,i],r2.at[zs,1,a],oa(i)*W1+b,n)
+    def d3(ns,zs,h,i):
+        if h==0: return rc(out.at[ns,a,:,0],out.at[ns,a,:,0],s3.at[zs,0,i],r3.at[zs,0,a],oa(i)*W1+b,n)
+        return rc(out.at[ns,:,b,1],out.at[ns,:,b,1],s3.at[zs,1,i],r3.at[zs,1,b],a*W1+ob(i),n)
+    f0=rc(own,out.at[n],fs0,fr0,w,sib)
+    def f1(ns,zs): return rc(out.at[ns,a,b],out.at[ns,a,b],fs1.at[zs],fr1.at[zs],w,sib)
+    def f2(ns,zs,h,i):
+        v=out.at[ns,a,ob(i),0] if h==0 else out.at[ns,oa(i),b,1]
+        k=ob(i) if h==0 else oa(i)
+        return rc(v,v,fs2.at[zs,h,k],fr2.at[zs,h,k],w,sib)
+    def f3(ns,zs,h,i):
+        v=out.at[ns,oa(i),:,0] if h==0 else out.at[ns,:,ob(i),1]
+        k=oa(i) if h==0 else ob(i)
+        return rc(v,v,fs3.at[zs,h,k],fr3.at[zs,h,k],w,sib)
+    local=pltpu.make_async_copy(own,out.at[n],lsem)
+    up=z<H-1; down=z>0
+    @pl.when(up)
+    def _(): own1(1).start()
+    @pl.when(down)
+    def _(): own1(-1).start()
+    local.start(); f0.start()
+    def sides(d,f):
+        @pl.when(jnp.logical_and(d<=H-1,z-d>=0))
+        def _(): f(z-d,1,up)
+        @pl.when(jnp.logical_and(d<=H-1,z+d<=H-1))
+        def _(): f(z+d,-1,down)
+    def step1(zs,step,more):
+        ns=2*zs+core
+        arrived(out.at[ns,a,b],r1.at[zs])
+        @pl.when(more)
+        def _(): d1(zs,step).start()
+        for i in range(1,W1):
+            d2(ns,zs,0,i).start(); d2(ns,zs,1,i).start()
+        f1(ns,zs).start()
+    def step2(zs,step,more):
+        ns=2*zs+core
+        for i in range(1,W1):
+            arrived(out.at[ns,a,ob(i),0],r2.at[zs,0,ob(i)])
+        for i in range(1,W1): d3(ns,zs,0,i).start()
+        for i in range(1,W1):
+            arrived(out.at[ns,oa(i),b,1],r2.at[zs,1,oa(i)])
+        for i in range(1,W1): d3(ns,zs,1,i).start()
+        for i in range(1,W1):
+            f2(ns,zs,0,i).start(); f2(ns,zs,1,i).start()
+    def step3(zs,step,more):
+        ns=2*zs+core
+        for i in range(1,W1):
+            arrived(out.at[ns,oa(i),:,0],r3.at[zs,0,oa(i)])
+            f3(ns,zs,0,i).start()
+            arrived(out.at[ns,:,ob(i),1],r3.at[zs,1,ob(i)])
+            f3(ns,zs,1,i).start()
+    def run(d,_):
+        sides(d,step1)
+        @pl.when(d>1)
+        def _(): sides(d-1,step2)
+        @pl.when(d>2)
+        def _(): sides(d-2,step3)
+        return 0
+    lax.fori_loop(1,H+2,run,0)
+    local.wait()
+    f0.wait_send(); arrived(out.at[sib],fr0)
+    @pl.when(up)
+    def _(): own1(1).wait_send()
+    @pl.when(down)
+    def _(): own1(-1).wait_send()
+    def finish(zs,step,more):
+        ns=2*zs+core; nb=ns+1-2*core
+        @pl.when(more)
+        def _(): d1(zs,step).wait_send()
+        f1(ns,zs).wait_send(); arrived(out.at[nb,a,b],fr1.at[zs])
+        for h in (0,1):
+            for i in range(1,W1):
+                d2(ns,zs,h,i).wait_send(); d3(ns,zs,h,i).wait_send()
+                f2(ns,zs,h,i).wait_send(); f3(ns,zs,h,i).wait_send()
+                v2=out.at[nb,a,ob(i),0] if h==0 else out.at[nb,oa(i),b,1]
+                arrived(v2,fr2.at[zs,h,ob(i) if h==0 else oa(i)])
+                v3=out.at[nb,oa(i),:,0] if h==0 else out.at[nb,:,ob(i),1]
+                arrived(v3,fr3.at[zs,h,oa(i) if h==0 else ob(i)])
+    def fin(d,_):
+        sides(d,finish); return 0
+    lax.fori_loop(1,H,fin,0)
+
+def gather_weights(W,N,own):
+    W1=math.isqrt(W); H=N//2
+    D=pltpu.SemaphoreType.DMA
+    return pl.pallas_call(functools.partial(gather_kernel,W,N),out_shape=jax.ShapeDtypeStruct((N,)+own.shape,bf16),
+      in_specs=[pl.BlockSpec(memory_space=pl.ANY)],out_specs=pl.BlockSpec(memory_space=pl.ANY),
+      scratch_shapes=[D(()),D((H,)),D((H,)),D((H,)),D((H,2,W1)),D((H,2,W1)),D((H,2,W1)),D((H,2,W1)),D(()),D(()),D((H,)),D((H,)),D((H,2,W1)),D((H,2,W1)),D((H,2,W1)),D((H,2,W1))],
+      compiler_params=pltpu.CompilerParams(collective_id=1,has_side_effects=True,vmem_limit_bytes=1<<20),name="gather_weights")(own)
+
+def scatter_share(partial_sum):
+    part = lax.psum_scatter(
+        partial_sum.astype(bf16), "narrow", scatter_dimension=0, tiled=True
+    )
+    return lax.psum(part, "wide").astype(f32)
+
+
 def body(
     tokens, cotangent, item_lengths, attn_gain, attn_bias, qkv_weight, proj_weight,
     mlp_gain, mlp_bias, up_weight, down_weight,
@@ -216,59 +345,70 @@
     heads = qkv_weight.shape[1] // (3 * HEAD_DIM)
     gain_one, bias_one = attn_gain.astype(f32), attn_bias.astype(f32)
     gain_two, bias_two = mlp_gain.astype(f32), mlp_bias.astype(f32)
+    wide, narrow = lax.axis_size("wide"), lax.axis_size("narrow")
+    side = math.isqrt(wide)
+
+    def cut(shard):
+        return shard.reshape(side, side, 2, shard.shape[0] // (2 * wide), shard.shape[1])
+
+    shards = [cut(up_weight.T), cut(down_weight), cut(proj_weight)]
+    everything = gather_weights(wide, narrow, jnp.concatenate(shards, axis=3))
+    first = shards[0].shape[3]
+    features = tokens.shape[1]
     normed = norm_forward(token_rows, gain_one, bias_one).astype(bf16)
     normed_all = lax.all_gather(normed, "narrow", axis=0, tiled=True)
+    normed_all, everything = lax.optimization_barrier((normed_all, everything))
     rows = normed_all.shape[0]
     query_extra, key_extra = mask_rows(item_lengths, rows)
     packed = (
         product("rd,dc->cr", normed_all, qkv_weight).astype(bf16).reshape(heads, 3, HEAD_DIM, rows)
     )
     attended, log_total = attend_forward(packed, query_extra, key_extra)
-    attended_flat = attended.reshape(heads * HEAD_DIM, rows)
-    branch = scatter_rows(product("ar,ad->rd", attended_flat, proj_weight))
+    up_all = everything[:, :, :, :, :first].reshape(-1, tokens.shape[1])
+    down_all = everything[:, :, :, :, first : 2 * first].reshape(-1, tokens.shape[1])
+    proj_all = everything[:, :, :, :, 2 * first :].reshape(-1, tokens.shape[1])
+    attended_rows = lax.all_to_all(
+        attended.reshape(heads * HEAD_DIM, rows), "narrow", split_axis=1, concat_axis=0, tiled=True
+    )
+    branch = product("ar,ad->rd", attended_rows, proj_all)
     middle = token_rows + branch
     expand_in = norm_forward(middle, gain_two, bias_two).astype(bf16)
-    expand_all = lax.all_gather(expand_in, "narrow", axis=0, tiled=True)
-    hidden_pre = product("rd,df->rf", expand_all, up_weight)
+    hidden_pre = product("rd,fd->rf", expand_in, up_all)
     hidden = gelu_exact(hidden_pre).astype(bf16)
-    output = (middle + scatter_rows(product("rf,fd->rd", hidden, down_weight))).astype(bf16)
-
-    grad_rows = lax.all_gather(cotangent, "narrow", axis=0, tiled=True)
-    grad_down = product("rf,rd->fd", hidden, grad_rows)
-    grad_hidden = product("rd,fd->rf", grad_rows, down_weight)
+    output = (middle + product("rf,fd->rd", hidden, down_all)).astype(bf16)
+
+    grad_hidden = product("rd,fd->rf", cotangent, down_all)
     grad_pre = jax.vjp(gelu_exact, hidden_pre)[1](grad_hidden)[0].astype(bf16)
-    grad_up = product("rd,rf->df", expand_all, grad_pre)
-    grad_expand = scatter_rows(product("rf,df->rd", grad_pre, up_weight))
+    grad_expand = product("rf,fd->rd", grad_pre, up_all)
     grad_middle_norm, grad_gain_two, grad_bias_two = jax.vjp(
         norm_forward, middle, gain_two, bias_two
     )[1](grad_expand)
     grad_middle = cotangent.astype(f32) + grad_middle_norm
-    grad_branch_all = lax.all_gather(grad_middle.astype(bf16), "narrow", axis=0, tiled=True)
-    grad_proj = product("ar,rd->ad", attended_flat, grad_branch_all)
-    grad_attended = (
-        product("rd,ad->ar", grad_branch_all, proj_weight)
-        .astype(bf16)
-        .reshape(heads, HEAD_DIM, rows)
-    )
+    grad_branch = grad_middle.astype(bf16)
+    grad_attended = lax.all_to_all(
+        product("rd,ad->ar", grad_branch, proj_all).astype(bf16),
+        "narrow", split_axis=0, concat_axis=1, tiled=True,
+    ).reshape(heads, HEAD_DIM, rows)
+    grad_down = scatter_share(product("rf,rd->fd", hidden, cotangent))
+    grad_up = scatter_share(product("rf,rd->fd", grad_pre, expand_in)).T
+    grad_proj = scatter_share(product("ar,rd->ad", attended_rows, grad_branch))
     grad_packed = attend_backward(
         packed, query_extra, key_extra, attended, grad_attended, log_total, items
     ).reshape(heads * 3 * HEAD_DIM, rows)
+    grad_normed = scatter_rows(product("cr,dc->rd", grad_packed, qkv_weight))
     grad_qkv = product("rd,cr->dc", normed_all, grad_packed)
-    grad_normed = scatter_rows(product("cr,dc->rd", grad_packed, qkv_weight))
     grad_token_norm, grad_gain_one, grad_bias_one = jax.vjp(
         norm_forward, token_rows, gain_one, bias_one
     )[1](grad_normed)
     grad_tokens = (grad_middle + grad_token_norm).astype(bf16)
     norm_parts = jnp.stack([grad_gain_one, grad_bias_one, grad_gain_two, grad_bias_two])
-    norm_shares = lax.psum_scatter(norm_parts, "narrow", scatter_dimension=1, tiled=True)
-
-    def over_items(share):
-        return lax.psum(share.astype(bf16), "wide").astype(f32)
-
-    shares = over_items(norm_shares)
+    norm_sums = lax.psum(norm_parts, ("wide", "narrow"))
+    share = norm_sums.shape[1] // lax.axis_size("narrow")
+    shares = lax.dynamic_slice_in_dim(norm_sums, lax.axis_index("narrow") * share, share, 1)
+    grad_qkv = lax.psum(grad_qkv.astype(bf16), "wide").astype(f32)
     return (
-        output, grad_tokens, shares[0], shares[1], over_items(grad_qkv), over_items(grad_proj),
-        shares[2], shares[3], over_items(grad_up), over_items(grad_down),
+        output, grad_tokens, shares[0], shares[1], grad_qkv, grad_proj,
+        shares[2], shares[3], grad_up, grad_down,
     )
 
 

time: 1060 us -> 747 us (0.70)
  waiting for transfers between devices: 726 us -> 189 us
  Pallas kernels: 130 us -> 278 us
  blocking collectives: 9.85 us -> 79.3 us
  local copies, waits for them, and re-layouts: 6.49 us -> 36.5 us
  other arithmetic: 50.7 us -> 23 us
    reduce_scatter x4 -> x1, waiting for transfers between devices: 326 us -> 79.3 us  [scatter_rows(): lax.psum_scatter(partial_sum.astype(bf16), 'narrow', scatter_dimension=0,...]
    all_gather x3 -> x0, waiting for transfers between devices: 212 us -> none  [the longest x1 79.9 us: body(): expand_all = lax.all_gather(expand_in, 'narrow', axis=0, tiled=True)]
    pallas_call x0 -> x1, Pallas kernels: none -> 149 us  [gather_weights(): pl.pallas_call(functools.partial(gather_kernel, W, N), out_shape=jax.Shap...]
    all_gather x1, waiting for transfers between devices: 83.7 us -> 0.02 us  [body(): normed_all = lax.all_gather(normed, 'narrow', axis=0, tiled=True)]
    reduce_scatter x0 -> x3, waiting for transfers between devices: none -> 54.3 us  [scatter_share(): lax.psum_scatter(partial_sum.astype(bf16), 'narrow', scatter_dimension=0,...]
    all_to_all x0 -> x1, blocking collectives: none -> 41.1 us  [body(): lax.all_to_all(product('rd,ad->ar', grad_branch, proj_all).astype(bf16),...]
    psum x1, waiting for transfers between devices: 77.5 us -> 44.5 us  [scatter_share(): return lax.psum(part, 'wide').astype(f32)]
    psum x1, blocking collectives: 9.85 us -> 38.2 us  [body(): norm_sums = lax.psum(norm_parts, ('wide', 'narrow'))]
  transfers between devices with their start and end apart: 10 -> 7, of which waited for: 10 -> 4; matrix products, arithmetic and copies ran while one was open for 7% -> 11% of each run, Pallas kernels for 0% -> 31%
where the time goes in v2:
time: 747 us; the launch traced here: 738 us
  Pallas kernels  278 us (37%)
  waiting for transfers between devices  189 us (25%)
  matrix products  112 us (15%)
  blocking collectives  79.3 us (11%)
  local copies, waits for them, and re-layouts  36.5 us (5%)
  other arithmetic  23 us (3%)
  between operations  15 us (2%)
    pallas_call x1, Pallas kernels, gather_weights(): pl.pallas_call(functools.partial(gather_kernel, W, N), out_shape=jax.Shap...  149 us
    dot_general x12, matrix products, product(): return jnp.einsum(spec, left, right, preferred_element_type=f32)  112 us
    pallas_call x1, Pallas kernels, attend_backward(): pl.pallas_call(functools.partial(backward_kernel, block, rows, items), gr...  82.7 us
    reduce_scatter x1, waiting for transfers between devices, scatter_rows(): lax.psum_scatter(partial_sum.astype(bf16), 'narrow', scatter_dimension=0,...  79.3 us
    reduce_scatter x3, waiting for transfers between devices, scatter_share(): lax.psum_scatter(partial_sum.astype(bf16), 'narrow', scatter_dimension=0,...  54.3 us
    pallas_call x1, Pallas kernels, attend_forward(): pl.pallas_call(functools.partial(forward_kernel, block, rows), grid=(head...  46.8 us
    psum x1, waiting for transfers between devices, scatter_share(): return lax.psum(part, 'wide').astype(f32)  44.5 us
    all_to_all x1, blocking collectives, body(): lax.all_to_all(product('rd,ad->ar', grad_branch, proj_all).astype(bf16),...  41.1 us
  transfers between devices with their start and end apart: 7, of which 4 were waited for; matrix products, arithmetic and copies ran while one was open for 11% of the time, Pallas kernels for 31%

profile of v2, /device:TPU:0, one launch (start us, length us, event | category | flops | bytes accessed | tf_op | source)
XLA Modules:
  0.0 737.5 jit_solution(129753192873200935)
XLA Ops:
  7.2 0.0 all-gather.2.cloned.1.call-start
  7.3 1.6 convert_reduce_fusion.1
  8.8 1.6 fusion.21
  10.5 0.5 copy-done.22
  11.0 0.7 convert_element_type.89
  11.7 0.7 convert_element_type.90
  12.4 2.6 fusion.20
  15.1 0.0 all-gather.2.cloned.1.call-update
  15.1 0.5 copy.35
  15.7 1.5 pad_maximum_fusion.own
  17.2 148.9 %gather_weights.1 = bf16[8,2,2,2,144,1024]{5,4,3,2,1,0:T(8,128)(2,1)S(1)} custom-call(bf16[2,2,2,144,1024]{4,3,2,1,0:T(8,128)(2,1)S(1)} %pad_maximum_fusion.own), custom_call_target="tpu_custom_call" | custom-call | tf_op jit(solution)/shard_map/gather_weights/pallas_call | solution.py:327
  166.0 6.4 copy-done.1
  172.5 0.1 select_reduce_fusion
  172.6 0.1 convert_reduce_fusion.2
  172.7 0.1 select_convert_fusion.1.qx_ref
  172.9 0.1 select_convert_fusion.kx_ref
  172.9 0.0 all-gather.2.cloned.1.call-done
  173.0 6.8 convolution_convert_fusion.3
  179.8 46.8 %attend_forward.1 = (bf16[2,64,4096]{2,1,0:T(8,128)(2,1)S(1)}, f32[2,1,4096]{2,1,0:T(1,128)S(1)}) custom-call(bf16[16,4096]{1,0:T(8,128)(2,1)S(1)} %select_convert_fusion.1.qx_ref, bf16[16,4096]{1,0:T(8,128)(2,1)S(1)} %select_convert_fusion.kx_ref, bf16[2,3,64,4096]{3,2,1,0:T(8,128)(2,1)S(1)} %bitcast.75, bf16[2,3,64,4096]{3,2,1,0:T(8,128)(2,1)S(1)} %bitcast.76, ...), custom_call_target="tpu_custom_call" | custom-call | flops 34359738368 | bytes 4194304 | tf_op jit(solution)/shard_map/attend_forward/pallas_call | solution.py:80
  226.7 0.4 copy.41
  227.1 1.3 copy.36
  228.3 4.2 all-to-all-start
  232.6 0.0 reduce-scatter.7.cloned.1.call-start
  232.7 3.2 slice.21
  235.9 12.7 %fusion.32 = (bf16[8,2,2,2,64,1024]{5,4,3,2,1,0:T(8,128)(2,1)}, bf16[8,2,2,2,64,1024]{5,4,3,2,1,0:T(8,128)(2,1)}) fusion(bf16[8,2,2,2,144,1024]{5,4,3,2,1,0:T(8,128)(2,1)} %copy-done.1), kind=kLoop, calls=%fused_computation.89 | loop fusion | bytes 33554432 | tf_op jit(solution)/shard_map/slice | solution.py:368
  248.6 10.6 %all-to-all-done = bf16[128,8,512]{2,0,1:T(8,128)(2,1)} async-done(((bf16[128,8,512]{2,0,1:T(8,128)(2,1)}), bf16[128,8,512]{2,0,1:T(8,128)(2,1)}, u32[]{:S(2)}, u32[]{:S(2)}) %all-to-all-start) | async-done | bytes 1048608 | tf_op jit(solution)/shard_map/all_to_all | solution.py:370
  259.2 3.4 fusion.33
  262.6 0.3 multiply_reduce_fusion.2
  263.0 28.0 %multiply_convert_fusion = (bf16[512,4096]{1,0:T(8,128)(2,1)}, f32[512,4096]{1,0:T(8,128)}, f32[512,4096]{1,0:T(8,128)}) fusion(bf16[4096,1024]{1,0:T(8,128)(2,1)} %bitcast.89, f32[512,1024]{1,0:T(8,128)S(1)} %get-tuple-element.79, f32[1024]{0:T(1024)S(1)} %convert_element_type.95, f32[1024]{0:T(1024)S(1)} %convert_element_type.94, f32[512]{0:T(512)S(1)} %fusion.28, ...), kind=kOutput, calls=%fused_computation.11 | convolution fusion | flops 4433903616 | bytes 31469568 | tf_op jit(solution)/shard_map/rd,fd->rf/dot_general | solution.py:203
  291.0 10.5 %fusion.6 = bf16[512,4096]{1,0:T(8,128)(2,1)S(1)} fusion(f32[512,4096]{1,0:T(8,128)} %get-tuple-element.71, f32[512,4096]{1,0:T(8,128)} %get-tuple-element.80, bf16[4096,1024]{1,0:T(8,128)(2,1)S(1)} %bitcast.88, bf16[512,1024]{1,0:T(8,128)(2,1)S(1)} %copy-done.9), kind=kOutput, calls=%fused_computation.9 | convolution fusion | flops 4324327424 | bytes 30408704 | tf_op jit(solution)/shard_map/rd,fd->rf/dot_general | solution.py:203
  301.5 8.9 %multiply_reduce_fusion = (f32[1024]{0:T(1024)S(1)}, f32[512]{0:T(512)S(1)}, f32[1024]{0:T(1024)S(1)}, f32[512,1024]{1,0:T(8,128)S(1)}) fusion(f32[512,1024]{1,0:T(8,128)S(1)} %get-tuple-element.79, f32[512]{0:T(512)S(1)} %fusion.28, f32[512]{0:T(512)S(1)} %broadcast_multiply_fusion, f32[1024]{0:T(1024)S(1)} %convert_element_type.94, ...), kind=kOutput, calls=%fused_computation.49 | convolution fusion | flops 4299159040 | bytes 16795648 | tf_op jit(solution)/shard_map/rf,fd->rd/dot_general | solution.py:203
  310.4 0.7 fusion.30
  311.1 1.3 copy-done.7
  312.5 0.3 fusion.25
  312.8 1.0 copy-done.11
  313.8 3.8 convolution_convert_fusion.4
  317.6 0.0 reduce-scatter.9.cloned.1.call-start
  317.6 10.8 %convolution_convert_fusion.1 = bf16[4096,1024]{1,0:T(8,128)(2,1)} fusion(bf16[512,4096]{1,0:T(8,128)(2,1)} %copy-done.27, f32[512,1024]{1,0:T(8,128)} %copy-done.6, f32[1024]{0:T(1024)S(1)} %convert_element_type.95, f32[1024]{0:T(1024)S(1)} %convert_element_type.94, f32[512]{0:T(512)S(1)} %fusion.28, f32[512]{0:T(512)S(1)} %broadcast_multiply_fusion), kind=kOutput, calls=%fused_computation.26 | convolution fusion | flops 4301783040 | bytes 14692352 | tf_op jit(solution)/shard_map/rf,rd->fd/dot_general | solution.py:203
  328.5 0.0 reduce-scatter.11.cloned.1.call-start
  328.6 9.1 %convolution_convert_fusion = bf16[4096,1024]{1,0:T(8,128)(2,1)} fusion(bf16[512,4096]{1,0:T(8,128)(2,1)} %get-tuple-element.70, bf16[512,1024]{1,0:T(8,128)(2,1)S(1)} %copy-done.9), kind=kOutput, calls=%fused_computation.25 | convolution fusion | flops 4299161600 | bytes 13631488 | tf_op jit(solution)/shard_map/rf,rd->fd/dot_general | solution.py:203
  337.7 0.0 reduce-scatter.5.cloned.1.call-start
  337.8 1.2 copy-done.12
  338.9 2.9 convolution_convert_fusion.5
  341.8 41.1 %all_to_all.35 = bf16[8,128,512]{2,1,0:T(8,128)(2,1)S(1)} all-to-all(bf16[8,128,512]{2,1,0:T(8,128)(2,1)S(1)} %bitcast.96), channel_id=1, replica_groups=mesh['wide'=4,'narrow'=8] {'narrow'}, dimensions={0} | all-to-all | bytes 2097152 | tf_op jit(solution)/shard_map/all_to_all | solution.py:388
  382.9 1.5 copy.38
  384.5 1.6 reshape.149.do_ref
  386.0 82.7 %attend_backward.1 = bf16[2,3,64,4096]{3,2,1,0:T(8,128)(2,1)S(1)} custom-call(bf16[16,4096]{1,0:T(8,128)(2,1)S(1)} %select_convert_fusion.1.qx_ref, bf16[16,4096]{1,0:T(8,128)(2,1)S(1)} %select_convert_fusion.kx_ref, bf16[2,3,64,4096]{3,2,1,0:T(8,128)(2,1)} %bitcast.78, bf16[2,3,64,4096]{3,2,1,0:T(8,128)(2,1)} %bitcast.79, ...), custom_call_target="tpu_custom_call" | custom-call | flops 85899345920 | bytes 8388608 | tf_op jit(solution)/shard_map/attend_backward/pallas_call | solution.py:171
  468.8 1.6 copy-done.3
  470.4 6.9 convolution_convert_fusion.2
  477.3 0.3 all-reduce.3.cloned.1.call-start
  477.6 9.8 %convolution_convert_fusion.6 = bf16[1024,384]{1,0:T(8,128)(2,1)} fusion(bf16[4096,1024]{1,0:T(8,128)(2,1)} %all-gather.2.cloned.1.call-done, bf16[384,4096]{1,0:T(8,128)(2,1)} %bitcast.82), kind=kOutput, calls=%fused_computation.58 | convolution fusion | flops 3221618688 | bytes 12320768 | tf_op jit(solution)/shard_map/rd,cr->dc/dot_general | solution.py:203
  487.4 54.3 %reduce-scatter.11.cloned.1.call-done = bf16[512,1024]{1,0:T(8,128)(2,1)} async-done(((bf16[4096,1024]{1,0:T(8,128)(2,1)}), bf16[512,1024]{1,0:T(8,128)(2,1)}) %reduce-scatter.11.cloned.1.call-update) | async-done | bytes 1048592 | tf_op jit(solution)/shard_map/reduce_scatter | solution.py:333
  541.8 10.8 %add_convert_fusion.1 = bf16[512,1024]{1,0:T(8,128)(2,1)} fusion(f32[512,1024]{1,0:T(8,128)} %copy-done.6, bf16[512,4096]{1,0:T(8,128)(2,1)} %get-tuple-element.70, bf16[4096,1024]{1,0:T(8,128)(2,1)} %bitcast.85), kind=kOutput, calls=%fused_computation.53 | convolution fusion | flops 4296015872 | bytes 15728640 | tf_op jit(solution)/shard_map/rf,fd->rd/dot_general | solution.py:203
  552.6 79.3 %reduce-scatter.5.cloned.1.call-done = bf16[512,1024]{1,0:T(8,128)(2,1)} async-done(((bf16[4096,1024]{1,0:T(8,128)(2,1)}), bf16[512,1024]{1,0:T(8,128)(2,1)}) %reduce-scatter.5.cloned.1.call-update) | async-done | bytes 1048592 | tf_op jit(solution)/shard_map/reduce_scatter | solution.py:207
  631.9 1.8 fusion.22
  633.8 2.3 fusion.23
  636.1 38.2 %psum.35 = f32[4,1024]{1,0:T(4,128)S(1)} all-reduce(f32[4,1024]{1,0:T(4,128)S(1)} %pad_maximum_fusion.1), channel_id=1, replica_groups=mesh['wide'=4,'narrow'=8] {'wide','narrow'}, use_global_device_ids=true, to_apply=%region_15.16 | all-reduce | flops 4096 | bytes 32768 | tf_op jit(solution)/shard_map/psum | solution.py:405
  674.4 0.5 slice_bitcast_fusion
  674.9 3.3 add_convert_fusion
  678.2 44.5 %all-reduce.3.cloned.1.call-done = (bf16[1024,512]{0,1:T(8,128)(2,1)}, bf16[1024,384]{1,0:T(8,128)(2,1)}, bf16[128,1024]{1,0:T(8,128)(2,1)}, bf16[512,1024]{1,0:T(8,128)(2,1)}) async-done(((bf16[1024,512]{0,1:T(8,128)(2,1)}, bf16[1024,384]{1,0:T(8,128)(2,1)}, bf16[128,1024]{1,0:T(8,128)(2,1)}, bf16[512,1024]{1,0:T(8,128)(2,1)}), (bf16[1024,512]{0,1:T(8,128)(2,1)}, bf16[1024,384]{1,0:T(8,128)(2,1)}, ...) | async-done | bytes 3145744 | tf_op jit(solution)/shard_map/psum | solution.py:336
  722.7 2.9 convert_element_type.112
  725.6 2.6 copy.39
  728.2 1.2 convert_element_type.107
  729.4 0.8 convert_element_type.109
  (76 shorter events, 0.3 us)
Async XLA Ops:
  7.2 165.8 %copy-start = (bf16[1024,384]{1,0:T(8,128)(2,1)S(1)}, bf16[1024,384]{1,0:T(8,128)(2,1)}, u32[]{:S(2)}) copy-start(bf16[1024,384]{1,0:T(8,128)(2,1)} %param.16) | copy-start | bytes 2359300
  7.2 7.9 %copy-start.10 = (bf16[1024,512]{1,0:T(8,128)(2,1)S(1)}, bf16[1024,512]{1,0:T(8,128)(2,1)}, u32[]{:S(2)}) copy-start(bf16[1024,512]{1,0:T(8,128)(2,1)} %param.20) | copy-start | bytes 3145732
  7.2 8.4 %copy-start.14 = (bf16[128,1024]{1,0:T(8,128)(2,1)S(1)}, bf16[128,1024]{1,0:T(8,128)(2,1)}, u32[]{:S(2)}) copy-start(bf16[128,1024]{1,0:T(8,128)(2,1)} %param.17) | copy-start | bytes 786436
  7.2 165.7 %all-gather.2.cloned.1.call-start = ((), (), s32[]{:S(2)}) async-start(), calls=%async_computation.6 | async-start | bytes 9437184 | tf_op jit(solution)/shard_map/all_gather | solution.py:359
  8.8 3.6 copy-start.18
  10.5 0.5 copy-start.22
  11.0 1.4 copy-start.20
  11.7 0.7 copy-start.16
  17.1 155.4 %copy-start.26 = (s32[1,4]{1,0:T(1,128)S(1)}, s32[1,4]{1,0:T(1,128)}, u32[]{:S(2)}) copy-start(s32[1,4]{1,0:T(1,128)} %param.13) | copy-start | bytes 52
  166.0 6.5 copy-start.1
  179.8 46.8 %copy-start.2 = (bf16[4096,384]{0,1:T(8,128)(2,1)}, bf16[4096,384]{0,1:T(8,128)(2,1)S(1)}, u32[]{:S(2)}) copy-start(bf16[4096,384]{0,1:T(8,128)(2,1)S(1)} %convolution_convert_fusion.3) | copy-start | bytes 9437188
  226.6 6.0 copy-start.24
  226.6 6.0 copy-start.25
  228.3 30.8 %all-to-all-start = ((bf16[128,8,512]{2,0,1:T(8,128)(2,1)}), bf16[128,8,512]{2,0,1:T(8,128)(2,1)}, u32[]{:S(2)}, u32[]{:S(2)}) async-start(bf16[128,8,512]{2,0,1:T(8,128)(2,1)} %copy.36), calls=%async_computation | async-start | bytes 2097152 | tf_op jit(solution)/shard_map/all_to_all | solution.py:370
  232.6 254.8 %reduce-scatter.7.cloned.1.call-start = ((), (), s32[]{:S(2)}) async-start(), calls=%async_computation.8 | async-start | bytes 2359296 | tf_op jit(solution)/shard_map/reduce_scatter | solution.py:333
  235.9 23.3 %copy-start.4 = (bf16[512,1024]{1,0:T(8,128)(2,1)S(1)}, bf16[512,1024]{1,0:T(8,128)(2,1)}, u32[]{:S(2)}) copy-start(bf16[512,1024]{1,0:T(8,128)(2,1)} %param.11) | copy-start | bytes 3145732
  259.2 31.8 %slice-start = ((s8[8388608]{0:T(1024)(128)(4,1)}), s8[4194304]{0:T(1024)(128)(4,1)S(1)}, s32[]{:S(2)}) async-start(s8[8388608]{0:T(1024)(128)(4,1)} %bitcast.86), calls=%async_computation.12 | async-start | bytes 8388608
  262.6 47.8 %copy-start.6 = (f32[512,1024]{1,0:T(8,128)}, f32[512,1024]{1,0:T(8,128)S(1)}, u32[]{:S(2)}) copy-start(f32[512,1024]{1,0:T(8,128)S(1)} %get-tuple-element.79) | copy-start | bytes 6291460
  263.0 28.0 %slice-start.1 = ((s8[8388608]{0:T(1024)(128)(4,1)}), s8[4194304]{0:T(1024)(128)(4,1)S(1)}, s32[]{:S(2)}) async-start(s8[8388608]{0:T(1024)(128)(4,1)} %bitcast.86), calls=%async_computation.13 | async-start | bytes 8388608
  263.0 28.0 %copy-start.9 = (bf16[512,1024]{1,0:T(8,128)(2,1)S(1)}, bf16[512,1024]{1,0:T(8,128)(2,1)}, u32[]{:S(2)}) copy-start(bf16[512,1024]{1,0:T(8,128)(2,1)} %param.12) | copy-start | bytes 3145732
  301.5 8.9 %copy-start.27 = (bf16[512,4096]{1,0:T(8,128)(2,1)}, bf16[512,4096]{1,0:T(8,128)(2,1)S(1)}, u32[]{:S(2)}) copy-start(bf16[512,4096]{1,0:T(8,128)(2,1)S(1)} %fusion.6) | copy-start | bytes 12582916
  311.1 1.3 copy-start.7
  312.8 1.0 copy-start.11
  317.6 169.8 %reduce-scatter.9.cloned.1.call-start = ((), (), s32[]{:S(2)}) async-start(), calls=%async_computation.9 | async-start | bytes 9437184 | tf_op jit(solution)/shard_map/reduce_scatter | solution.py:333
  328.5 213.2 %reduce-scatter.11.cloned.1.call-start = ((), (), s32[]{:S(2)}) async-start(), calls=%async_computation.10 | async-start | bytes 9437184 | tf_op jit(solution)/shard_map/reduce_scatter | solution.py:333
  337.7 1.2 copy-start.12
  337.7 294.2 %reduce-scatter.5.cloned.1.call-start = ((), (), s32[]{:S(2)}) async-start(), calls=%async_computation.7 | async-start | bytes 9437184 | tf_op jit(solution)/shard_map/reduce_scatter | solution.py:207
  468.8 1.6 copy-start.3
  477.3 245.4 %all-reduce.3.cloned.1.call-start = ((), (), s32[]{:S(2)}) async-start(), calls=%async_computation.11 | async-start | bytes 6291456 | tf_op jit(solution)/shard_map/psum | solution.py:336
  541.8 90.1 %copy-start.5 = (bf16[512,1024]{1,0:T(8,128)(2,1)S(1)}, bf16[512,1024]{1,0:T(8,128)(2,1)}, u32[]{:S(2)}) copy-start(bf16[512,1024]{1,0:T(8,128)(2,1)} %param.11) | copy-start | bytes 3145732
  541.8 90.1 %copy-start.17 = (f32[1024]{0:T(1024)S(1)}, f32[1024]{0:T(1024)}, u32[]{:S(2)}) copy-start(f32[1024]{0:T(1024)} %copy-done.16) | copy-start | bytes 12292
  541.8 90.1 %copy-start.19 = (f32[512]{0:T(512)S(1)}, f32[512]{0:T(512)}, u32[]{:S(2)}) copy-start(f32[512]{0:T(512)} %copy-done.18) | copy-start | bytes 6148
  541.8 91.9 %copy-start.23 = (f32[512]{0:T(512)S(1)}, f32[512]{0:T(512)}, u32[]{:S(2)}) copy-start(f32[512]{0:T(512)} %copy-done.22) | copy-start | bytes 6148
  541.8 91.9 %copy-start.21 = (f32[512]{0:T(512)S(1)}, f32[512]{0:T(512)}, u32[]{:S(2)}) copy-start(f32[512]{0:T(512)} %copy-done.20) | copy-start | bytes 6148
  631.9 43.0 %copy-start.8 = (bf16[512,1024]{1,0:T(8,128)(2,1)S(1)}, bf16[512,1024]{1,0:T(8,128)(2,1)}, u32[]{:S(2)}) copy-start(bf16[512,1024]{1,0:T(8,128)(2,1)} %reduce-scatter.5.cloned.1.call-done) | copy-start | bytes 3145732
  722.7 5.5 copy-start.13
  722.7 6.7 copy-start.15
Sparse Core Ops, SparseCore 0:
  15.2 105.8 all-gather.1
  317.7 34.8 reduce-scatter.6
  355.0 92.1 reduce-scatter.8
  449.4 92.3 reduce-scatter.10
  543.9 87.9 reduce-scatter.4
  635.7 86.9 all-reduce.2

commit v3 on v2

--- a/solution.py
+++ b/solution.py
@@ -10,6 +10,7 @@
 
 HEAD_DIM = 64
 EXTRA = 16
+ATTENTION_STEPS = 16
 EXCLUDED = -1e30
 bf16 = jnp.bfloat16
 f32 = jnp.float32
@@ -106,12 +107,231 @@
     )(query_extra, key_extra, packed, packed, packed)
 
 
+def remote(src, dst, sent, received, wide_to, narrow_to):
+    return pltpu.make_async_remote_copy(
+        src_ref=src,
+        dst_ref=dst,
+        send_sem=sent,
+        recv_sem=received,
+        device_id=(wide_to, narrow_to),
+        device_id_type=MESH,
+    )
+
+
+def arrived(ref, semaphore):
+    pltpu.make_async_copy(ref, ref, semaphore).wait()
+
+
+def greet(wide, narrow, w, n):
+    barrier = pltpu.get_barrier_semaphore()
+
+    def column(t, carry):
+        pl.semaphore_signal(
+            barrier, inc=1, device_id=(w, lax.rem(n + t, narrow)), device_id_type=MESH
+        )
+        return carry
+
+    def plane(t, carry):
+        pl.semaphore_signal(
+            barrier, inc=1, device_id=(lax.rem(w + t, wide), n), device_id_type=MESH
+        )
+        return carry
+
+    lax.fori_loop(1, narrow, column, 0)
+    lax.fori_loop(1, wide, plane, 0)
+    pl.semaphore_wait(barrier, narrow + wide - 2)
+
+
+def accumulate(into, *others):
+    rows = into.shape[0]
+    few = max([d for d in (16, 32, 48, 64) if rows % d == 0], default=rows)
+
+    def piece(j, carry):
+        part = pl.ds(j * few if rows == few else pl.multiple_of(j * few, few), few)
+        total = into[part, :].astype(f32)
+        for other in others:
+            total = total + other[part, :].astype(f32)
+        into[part, :] = total.astype(bf16)
+        return carry
+
+    if rows == few:
+        piece(0, 0)
+    else:
+        lax.fori_loop(0, rows // few, piece, 0)
+
+
+def reduce_steps(
+    wide, narrow, parts, final, held, from_sibling, from_first, from_second, from_line,
+    loaded, sib_sent, sib_got, first_sent, first_got, second_sent, second_got, line_sent, line_got,
+):
+    w, n = lax.axis_index("wide"), lax.axis_index("narrow")
+    side, lines = math.isqrt(wide), narrow // 2
+    a, b, z, core = w // side, lax.rem(w, side), n // 2, lax.rem(n, 2)
+    sibling = n + 1 - 2 * core
+
+    def other_a(i):
+        return lax.rem(a + i, side)
+
+    def other_b(i):
+        return lax.rem(b + i, side)
+
+    def to_sibling(zs):
+        return remote(
+            parts.at[2 * zs + 1 - core], from_sibling.at[zs], sib_sent.at[zs], sib_got.at[zs], w, sibling
+        )
+
+    def load(zs):
+        return pltpu.make_async_copy(parts.at[2 * zs + core], held.at[zs], loaded.at[zs])
+
+    def first(zs, h, i):
+        if h == 0:
+            src, to = held.at[zs, other_a(i), :, 0], other_a(i) * side + b
+        else:
+            src, to = held.at[zs, :, other_b(i), 1], a * side + other_b(i)
+        k = i - 1
+        return remote(
+            src, from_first.at[zs, h, k], first_sent.at[zs, h, k], first_got.at[zs, h, k], to, n
+        )
+
+    def second(zs, h, i):
+        if h == 0:
+            src, to = held.at[zs, a, other_b(i), 0], a * side + other_b(i)
+        else:
+            src, to = held.at[zs, other_a(i), b, 1], other_a(i) * side + b
+        k = i - 1
+        return remote(
+            src, from_second.at[zs, h, k], second_sent.at[zs, h, k], second_got.at[zs, h, k], to, n
+        )
+
+    def along(zs):
+        slot = jnp.where(z < zs, z, z - 1)
+        return remote(
+            held.at[zs, a, b], from_line.at[slot], line_sent.at[zs], line_got.at[slot], w, 2 * zs + core
+        )
+
+    order = []
+    for i in range((lines + 1) // 2):
+        order += [lines - 1 - i] if lines - 1 - i == i else [lines - 1 - i, i]
+    halves = [(h, i) for i in range(1, side) for h in (0, 1)]
+
+    def begin():
+        greet(wide, narrow, w, n)
+        for zs in order:
+            to_sibling(zs).start()
+            load(zs).start()
+
+    def combine(zs):
+        load(zs).wait()
+        arrived(from_sibling.at[zs], sib_got.at[zs])
+
+        def piece(j, carry):
+            p, q = j // side, lax.rem(j, side)
+            for h in (0, 1):
+                accumulate(held.at[zs, p, q, h], from_sibling.at[zs, p, q, h])
+            return carry
+
+        lax.fori_loop(0, wide, piece, 0)
+        for h, i in halves:
+            first(zs, h, i).start()
+
+    def narrow_down(zs):
+        for h in (0, 1):
+            for i in range(1, side):
+                arrived(from_first.at[zs, h, i - 1], first_got.at[zs, h, i - 1])
+
+            def piece(j, carry, h=h):
+                into = held.at[zs, a, j, 0] if h == 0 else held.at[zs, j, b, 1]
+                accumulate(into, *[from_first.at[zs, h, i, j] for i in range(side - 1)])
+                return carry
+
+            lax.fori_loop(0, side, piece, 0)
+        for h, i in halves:
+            second(zs, h, i).start()
+
+    def send_home(zs):
+        for h, i in halves:
+            arrived(from_second.at[zs, h, i - 1], second_got.at[zs, h, i - 1])
+        for h in (0, 1):
+            accumulate(
+                held.at[zs, a, b, h], *[from_second.at[zs, h, i] for i in range(side - 1)]
+            )
+
+        @pl.when(z != zs)
+        def _():
+            along(zs).start()
+
+    def finish():
+        for slot in range(lines - 1):
+            arrived(from_line.at[slot], line_got.at[slot])
+        for h in (0, 1):
+            total = held[z, a, b, h].astype(f32)
+            for slot in range(lines - 1):
+                total = total + from_line[slot, h].astype(f32)
+            final[h] = total.astype(bf16)
+        for zs in order:
+            to_sibling(zs).wait_send()
+            for h, i in halves:
+                first(zs, h, i).wait_send()
+                second(zs, h, i).wait_send()
+
+            @pl.when(z != zs)
+            def _():
+                along(zs).wait_send()
+
+    steps = [(0.0, begin)]
+    for i, zs in enumerate(order):
+        at = 1 + 4 * i
+        steps += [
+            (at, functools.partial(combine, zs)),
+            (at + 3.2, functools.partial(narrow_down, zs)),
+            (at + 5.4, functools.partial(send_home, zs)),
+        ]
+    steps.append((99, finish))
+    return [step for _, step in sorted(steps, key=lambda s: s[0])], sorted(at for at, _ in steps)
+
+
+def reduce_scratch(wide, narrow, rows, features):
+    side, lines = math.isqrt(wide), narrow // 2
+    dma = pltpu.SemaphoreType.DMA
+    return [
+        pltpu.VMEM((lines, side, side, 2, rows, features), bf16),
+        pltpu.VMEM((lines, side, side, 2, rows, features), bf16),
+        pltpu.VMEM((lines, 2, side - 1, side, rows, features), bf16),
+        pltpu.VMEM((lines, 2, side - 1, rows, features), bf16),
+        pltpu.VMEM((lines - 1, 2, rows, features), bf16),
+        dma((lines,)),
+        dma((lines,)),
+        dma((lines,)),
+        dma((lines, 2, side - 1)),
+        dma((lines, 2, side - 1)),
+        dma((lines, 2, side - 1)),
+        dma((lines, 2, side - 1)),
+        dma((lines,)),
+        dma((lines - 1,)),
+    ]
+
+
 def backward_kernel(
-    block, rows, items, qx_ref, kx_ref, q_ref, k_ref, v_ref, o_ref, do_ref, log_ref,
-    grad_ref, keys, values, grad_k, grad_v,
+    block, rows, items, wide, narrow, qx_ref, kx_ref, q_ref, k_ref, v_ref, o_ref, do_ref, log_ref,
+    parts_ref, grad_ref, final_ref, keys, values, grad_k, grad_v, *reduce_refs,
 ):
     width = q_ref.shape[-1]
     step = pl.program_id(1)
+    steps_per_head = pl.num_programs(1)
+    moment = pl.program_id(0) * steps_per_head + step
+    ticks = ATTENTION_STEPS
+    moves, times = reduce_steps(wide, narrow, parts_ref, final_ref, *reduce_refs)
+
+    def perform(lower, upper):
+        for move, time in zip(moves, times):
+            if lower <= time < upper:
+                move()
+
+    for tick in range(ticks):
+
+        @pl.when(moment == tick)
+        def _():
+            perform(tick, tick + 1)
 
     @pl.when(step == 0)
     def _():
@@ -155,21 +375,29 @@
         grad_q * 0.125
     ).astype(bf16)
 
-    @pl.when(step == pl.num_programs(1) - 1)
+    @pl.when(step == steps_per_head - 1)
     def _():
         grad_ref[0, 1] = grad_k[...].astype(bf16)
         grad_ref[0, 2] = grad_v[...].astype(bf16)
 
-
-def attend_backward(packed, query_extra, key_extra, attended, grad, log_total, items, width=1024, block=512):
+    @pl.when(moment == ticks - 1)
+    def _():
+        perform(ticks, 1000)
+
+
+def attend_backward(
+    wide, narrow, packed, query_extra, key_extra, attended, grad, log_total, parts, items, block=512
+):
     heads, _, _, rows = packed.shape
+    width = heads * rows // ATTENTION_STEPS
+    piece = parts.shape[4:]
 
     def whole(j):
         return pl.BlockSpec((1, None, HEAD_DIM, rows), lambda h, i: (h, j, 0, 0))
 
     part = pl.BlockSpec((1, HEAD_DIM, width), lambda h, i: (h, 0, i))
     return pl.pallas_call(
-        functools.partial(backward_kernel, block, rows, items),
+        functools.partial(backward_kernel, block, rows, items, wide, narrow),
         grid=(heads, rows // width),
         in_specs=[
             pl.BlockSpec((EXTRA, width), lambda h, i: (0, i)),
@@ -180,47 +408,363 @@
             part,
             part,
             pl.BlockSpec((1, 1, width), lambda h, i: (h, 0, i)),
+            pl.BlockSpec(memory_space=pl.ANY),
         ],
-        out_specs=pl.BlockSpec((1, 3, HEAD_DIM, rows), lambda h, i: (h, 0, 0, 0)),
-        out_shape=jax.ShapeDtypeStruct((heads, 3, HEAD_DIM, rows), bf16),
+        out_specs=(
+            pl.BlockSpec((1, 3, HEAD_DIM, rows), lambda h, i: (h, 0, 0, 0)),
+            pl.BlockSpec((2, *piece), lambda h, i: (0, 0, 0)),
+        ),
+        out_shape=(
+            jax.ShapeDtypeStruct((heads, 3, HEAD_DIM, rows), bf16),
+            jax.ShapeDtypeStruct((2, *piece), bf16),
+        ),
         scratch_shapes=[
             pltpu.VMEM((HEAD_DIM + EXTRA, rows), bf16),
             pltpu.VMEM((HEAD_DIM + EXTRA, rows), bf16),
             pltpu.VMEM((HEAD_DIM, rows), f32),
             pltpu.VMEM((HEAD_DIM, rows), f32),
+            *reduce_scratch(wide, narrow, *piece),
         ],
-        compiler_params=pltpu.CompilerParams(vmem_limit_bytes=48 << 20),
+        compiler_params=pltpu.CompilerParams(
+            vmem_limit_bytes=58 << 20, collective_id=2, has_side_effects=True
+        ),
         cost_estimate=pl.CostEstimate(
             flops=10 * heads * rows * rows * 256,
             bytes_accessed=heads * rows * HEAD_DIM * 16,
             transcendentals=heads * rows * rows,
         ),
         name="attend_backward",
-    )(query_extra, key_extra, packed, packed, packed, attended, grad, log_total)
+    )(query_extra, key_extra, packed, packed, packed, attended, grad, log_total, parts)
+
+
+def finish_kernel(
+    wide, narrow, chunks,
+    packed_ref, weight_ref, normed_ref, token_ref, middle_ref, gain_ref, norm_ref, piece_ref,
+    tokens_out, qkv_out, shard_out, norms_out,
+    normed, held, for_sibling, from_sibling, from_line, total_qkv, own_qkv, first_qkv, second_qkv,
+    half_qkv, norms, norm_column, norm_half, norm_plane,
+    loaded, copied, sib_sent, sib_got, line_sent, line_got, piece_sent, piece_got,
+    first_sent, first_got, second_sent, second_got, column_sent, column_got, plane_sent, plane_got,
+):
+    w, n = lax.axis_index("wide"), lax.axis_index("narrow")
+    side, lines = math.isqrt(wide), narrow // 2
+    a, b, z, core = w // side, lax.rem(w, side), n // 2, lax.rem(n, 2)
+    sibling = n + 1 - 2 * core
+    rows, features = held.shape[1:]
+    step = rows // chunks
+    load = pltpu.make_async_copy(normed_ref, normed, loaded)
+    load.start()
+    greet(wide, narrow, w, n)
+
+    keep = pltpu.make_async_copy(piece_ref, shard_out.at[w], copied)
+    keep.start()
+
+    def spread(t):
+        return remote(
+            piece_ref, shard_out.at[w], piece_sent.at[t], piece_got.at[t], lax.rem(w + t, wide), n
+        )
+
+    for t in range(1, wide):
+        spread(t).start()
+
+    order = []
+    for i in range((lines + 1) // 2):
+        order += [lines - 1 - i] if lines - 1 - i == i else [lines - 1 - i, i]
+
+    def block(owner):
+        columns = pl.ds(pl.multiple_of(owner * rows, rows), rows)
+        return lax.dot_general(
+            packed_ref[:, columns], weight_ref[...], (((0,), (0,)), ((), ())),
+            preferred_element_type=f32,
+        ).astype(bf16)
+
+    def to_sibling(zs):
+        return remote(
+            for_sibling.at[zs], from_sibling.at[zs], sib_sent.at[zs], sib_got.at[zs], w, sibling
+        )
+
+    def pass_on(zs, c, up):
+        part = pl.ds(c * step, step)
+        slot = zs if up else jnp.where(z - 1 == zs, lines, zs)
+        to = n + 2 if up else n - 2
+        return remote(
+            held.at[zs, part], from_line.at[slot, part], line_sent.at[zs, c], line_got.at[slot, c], w, to
+        )
+
+    def merge(zs):
+        arrived(from_sibling.at[zs], sib_got.at[zs])
+        accumulate(held.at[zs], from_sibling.at[zs])
+
+    def feed(t):
+        @pl.when(z == 0)
+        def _():
+            for c in range(chunks):
+                pass_on(lines - 1 - t, c, True).start()
+
+        @pl.when(z == lines - 1)
+        def _():
+            for c in range(chunks):
+                pass_on(t, c, False).start()
+
+    def fed(t):
+        @pl.when(z == 0)
+        def _():
+            for c in range(chunks):
+                pass_on(lines - 1 - t, c, True).wait_send()
+
+        @pl.when(z == lines - 1)
+        def _():
+            for c in range(chunks):
+                pass_on(t, c, False).wait_send()
+
+    for i, zs in enumerate(order):
+        for_sibling[zs] = block(2 * zs + 1 - core)
+        to_sibling(zs).start()
+        held[zs] = block(2 * zs + core)
+        if i >= 1:
+            merge(order[i - 1])
+        if i == 2:
+            feed(0)
+    merge(order[-1])
+    if lines <= 2:
+        feed(0)
+
+    load.wait()
+    total_qkv[...] = jnp.dot(packed_ref[...], normed[...], preferred_element_type=f32)
+    half = total_qkv.shape[0] // 2
+    for h in (0, 1):
+        own_qkv[h] = total_qkv[h * half : (h + 1) * half].astype(bf16)
+
+    def along(h, i):
+        if h == 0:
+            return lax.rem(a + i, side) * side + b
+        return a * side + lax.rem(b + i, side)
+
+    halves = [(h, i) for i in range(1, side) for h in (0, 1)]
+
+    def first(h, i):
+        return remote(
+            own_qkv.at[h], first_qkv.at[h, i - 1], first_sent.at[h, i - 1], first_got.at[h, i - 1],
+            along(h, i), n,
+        )
+
+    def second(h, i):
+        return remote(
+            half_qkv.at[h], second_qkv.at[h, i - 1], second_sent.at[h, i - 1], second_got.at[h, i - 1],
+            along(1 - h, i), n,
+        )
+
+    def qkv_first():
+        for h, i in halves:
+            first(h, i).start()
+
+    def qkv_second():
+        for h, i in halves:
+            arrived(first_qkv.at[h, i - 1], first_got.at[h, i - 1])
+        for h in (0, 1):
+            total = own_qkv[h].astype(f32)
+            for i in range(1, side):
+                total = total + first_qkv[h, i - 1].astype(f32)
+            half_qkv[h] = total.astype(bf16)
+        for h, i in halves:
+            second(h, i).start()
+
+    def qkv_last():
+        for h, i in halves:
+            arrived(second_qkv.at[h, i - 1], second_got.at[h, i - 1])
+        for h in (0, 1):
+            total = half_qkv[h].astype(f32)
+            for i in range(1, side):
+                total = total + second_qkv[h, i - 1].astype(f32)
+            qkv_out[h * half : (h + 1) * half] = total.astype(bf16)
+
+    qkv_first()
+    for t in range(1, lines):
+        if t <= lines - 2:
+            fed(t - 1)
+            feed(t)
+        below, above = lines - 1 - (t - z), t - (lines - 1 - z)
+        for c in range(chunks):
+            part = pl.ds(c * step, step)
+            if t < lines - 1:
+
+                @pl.when(jnp.logical_and(z >= 1, t >= z))
+                def _():
+                    arrived(from_line.at[below, part], line_got.at[below, c])
+                    accumulate(held.at[below, part], from_line.at[below, part])
+                    pass_on(below, c, True).start()
+
+                @pl.when(jnp.logical_and(z <= lines - 2, above >= 0))
+                def _():
+                    arrived(from_line.at[above, part], line_got.at[above, c])
+                    accumulate(held.at[above, part], from_line.at[above, part])
+                    pass_on(above, c, False).start()
+        if t == 1:
+            qkv_second()
+        if t == min(2, lines - 1):
+            qkv_last()
+
+    def zero_edges(at_edge, slot):
+        @pl.when(at_edge)
+        def _():
+            from_line[slot] = jnp.zeros((rows, features), bf16)
+
+    zero_edges(z == 0, z)
+    zero_edges(z == lines - 1, lines)
+    for c in range(chunks):
+        part = pl.ds(c * step, step)
+
+        @pl.when(z >= 1)
+        def _():
+            arrived(from_line.at[z, part], line_got.at[z, c])
+
+        @pl.when(z <= lines - 2)
+        def _():
+            arrived(from_line.at[lines, part], line_got.at[lines, c])
+
+        def norm_rows(j, carry):
+            gain_sum, bias_sum = carry
+            few = pl.ds(pl.multiple_of(c * step + j * 32, 32), 32)
+            grad = (
+                held[z, few].astype(f32)
+                + from_line[z, few].astype(f32)
+                + from_line[lines, few].astype(f32)
+            )
+            values = token_ref[few, :].astype(f32)
+            centred = values - jnp.mean(values, axis=-1, keepdims=True)
+            inverse = lax.rsqrt(jnp.mean(centred * centred, axis=-1, keepdims=True) + epsilon)
+            scaled = centred * inverse
+            term = grad * gain_ref[...]
+            back = inverse * (
+                term
+                - jnp.mean(term, axis=-1, keepdims=True)
+                - scaled * jnp.mean(term * scaled, axis=-1, keepdims=True)
+            )
+            tokens_out[few, :] = (middle_ref[few, :] + back).astype(bf16)
+            gain_sum = gain_sum + jnp.sum(grad * scaled, axis=0, keepdims=True)
+            bias_sum = bias_sum + jnp.sum(grad, axis=0, keepdims=True)
+            return gain_sum, bias_sum
+
+        start = (jnp.zeros((1, features), f32), jnp.zeros((1, features), f32))
+        sums = lax.fori_loop(0, step // 32, norm_rows, start)
+        if c == 0:
+            gain_sum, bias_sum = sums
+        else:
+            gain_sum, bias_sum = gain_sum + sums[0], bias_sum + sums[1]
+
+    row = lax.broadcasted_iota(jnp.int32, (8, features), 0)
+    norms[...] = jnp.where(row == 0, gain_sum, jnp.where(row == 1, bias_sum, norm_ref[...]))
+
+    def down_column(t):
+        return remote(
+            norms, norm_column.at[t - 1], column_sent.at[t - 1], column_got.at[t - 1],
+            w, lax.rem(n + t, narrow),
+        )
+
+    def over_plane(t):
+        return remote(
+            norm_half, norm_plane.at[t - 1], plane_sent.at[t - 1], plane_got.at[t - 1],
+            lax.rem(w + t, wide), n,
+        )
+
+    for t in range(1, narrow):
+        down_column(t).start()
+    total = norms[...]
+    for t in range(1, narrow):
+        arrived(norm_column.at[t - 1], column_got.at[t - 1])
+        total = total + norm_column[t - 1]
+    norm_half[...] = total
+    for t in range(1, wide):
+        over_plane(t).start()
+    for t in range(1, wide):
+        arrived(norm_plane.at[t - 1], plane_got.at[t - 1])
+        total = total + norm_plane[t - 1]
+    norms_out[...] = total
+
+    keep.wait()
+    for t in range(1, wide):
+        spread(t).wait_send()
+        arrived(shard_out.at[lax.rem(w + wide - t, wide)], piece_got.at[t])
+        over_plane(t).wait_send()
+    for t in range(1, narrow):
+        down_column(t).wait_send()
+    for h, i in halves:
+        first(h, i).wait_send()
+        second(h, i).wait_send()
+    for zs in order:
+        to_sibling(zs).wait_send()
+    fed(lines - 2)
+    for zs in range(lines):
+        for c in range(chunks):
+
+            @pl.when(jnp.logical_and(z >= 1, zs > z))
+            def _():
+                pass_on(zs, c, True).wait_send()
+
+            @pl.when(jnp.logical_and(z <= lines - 2, zs < z))
+            def _():
+                pass_on(zs, c, False).wait_send()
+
+
+def finish(wide, narrow, packed, weight, normed, tokens, middle, gain, norm_parts, piece, chunks=2):
+    side, lines = math.isqrt(wide), narrow // 2
+    rows, features = tokens.shape
+    columns = packed.shape[0]
+    dma = pltpu.SemaphoreType.DMA
+    vmem = pl.BlockSpec(memory_space=pltpu.VMEM)
+    anywhere = pl.BlockSpec(memory_space=pl.ANY)
+    return pl.pallas_call(
+        functools.partial(finish_kernel, wide, narrow, chunks),
+        in_specs=[vmem, vmem, anywhere, vmem, vmem, vmem, vmem, anywhere],
+        out_specs=(vmem, vmem, anywhere, vmem),
+        out_shape=(
+            jax.ShapeDtypeStruct((rows, features), bf16),
+            jax.ShapeDtypeStruct((columns, features), bf16),
+            jax.ShapeDtypeStruct((wide, *piece.shape), bf16),
+            jax.ShapeDtypeStruct((8, features), f32),
+        ),
+        scratch_shapes=[
+            pltpu.VMEM(normed.shape, bf16),
+            pltpu.VMEM((lines, rows, features), bf16),
+            pltpu.VMEM((lines, rows, features), bf16),
+            pltpu.VMEM((lines, rows, features), bf16),
+            pltpu.VMEM((lines + 1, rows, features), bf16),
+            pltpu.VMEM((columns, features), f32),
+            pltpu.VMEM((2, columns // 2, features), bf16),
+            pltpu.VMEM((2, side - 1, columns // 2, features), bf16),
+            pltpu.VMEM((2, side - 1, columns // 2, features), bf16),
+            pltpu.VMEM((2, columns // 2, features), bf16),
+            pltpu.VMEM((8, features), f32),
+            pltpu.VMEM((narrow - 1, 8, features), f32),
+            pltpu.VMEM((8, features), f32),
+            pltpu.VMEM((wide - 1, 8, features), f32),
+            dma(()),
+            dma(()),
+            dma((lines,)),
+            dma((lines,)),
+            dma((lines, chunks)),
+            dma((lines + 1, chunks)),
+            dma((wide,)),
+            dma((wide,)),
+            dma((2, side - 1)),
+            dma((2, side - 1)),
+            dma((2, side - 1)),
+            dma((2, side - 1)),
+            dma((narrow - 1,)),
+            dma((narrow - 1,)),
+            dma((wide - 1,)),
+            dma((wide - 1,)),
+        ],
+        compiler_params=pltpu.CompilerParams(
+            vmem_limit_bytes=58 << 20, collective_id=3, has_side_effects=True
+        ),
+        name="finish",
+    )(packed, weight, normed, tokens, middle, gain, norm_parts, piece)
 
 
 def product(spec, left, right):
     return jnp.einsum(spec, left, right, preferred_element_type=f32)
 
-
-def scatter_rows(partial_sum):
-    return lax.psum_scatter(
-        partial_sum.astype(bf16), "narrow", scatter_dimension=0, tiled=True
-    ).astype(f32)
-
-
-def greet(W,N,w,n):
-    bar=pltpu.get_barrier_semaphore()
-    z=n//2; core=lax.rem(n,2)
-    def col(t,_):
-        nn=lax.rem(n+t,N)
-        pl.semaphore_signal(bar,inc=1,device_id=(w,nn),device_id_type=MESH); return 0
-    lax.fori_loop(1,N,col,0)
-    def plane(t,_):
-        ww=lax.rem(w+t,W)
-        pl.semaphore_signal(bar,inc=1,device_id=(ww,n),device_id_type=MESH); return 0
-    lax.fori_loop(1,W,plane,0)
-    pl.semaphore_wait(bar,N-1+W-1)
 
 def gather_kernel(W,N,own,out,lsem,s1,s1b,r1,s2,r2,s3,r3,fs0,fr0,fs1,fr1,fs2,fr2,fs3,fr3):
     w=lax.axis_index("wide"); n=lax.axis_index("narrow")
@@ -329,13 +873,6 @@
       scratch_shapes=[D(()),D((H,)),D((H,)),D((H,)),D((H,2,W1)),D((H,2,W1)),D((H,2,W1)),D((H,2,W1)),D(()),D(()),D((H,)),D((H,)),D((H,2,W1)),D((H,2,W1)),D((H,2,W1)),D((H,2,W1))],
       compiler_params=pltpu.CompilerParams(collective_id=1,has_side_effects=True,vmem_limit_bytes=1<<20),name="gather_weights")(own)
 
-def scatter_share(partial_sum):
-    part = lax.psum_scatter(
-        partial_sum.astype(bf16), "narrow", scatter_dimension=0, tiled=True
-    )
-    return lax.psum(part, "wide").astype(f32)
-
-
 def body(
     tokens, cotangent, item_lengths, attn_gain, attn_bias, qkv_weight, proj_weight,
     mlp_gain, mlp_bias, up_weight, down_weight,
@@ -346,10 +883,14 @@
     gain_one, bias_one = attn_gain.astype(f32), attn_bias.astype(f32)
     gain_two, bias_two = mlp_gain.astype(f32), mlp_bias.astype(f32)
     wide, narrow = lax.axis_size("wide"), lax.axis_size("narrow")
+    qkv_turned = qkv_weight.T
     side = math.isqrt(wide)
 
     def cut(shard):
         return shard.reshape(side, side, 2, shard.shape[0] // (2 * wide), shard.shape[1])
+
+    def split_parts(total):
+        return total.reshape(narrow, side, side, 2, -1, total.shape[1])
 
     shards = [cut(up_weight.T), cut(down_weight), cut(proj_weight)]
     everything = gather_weights(wide, narrow, jnp.concatenate(shards, axis=3))
@@ -361,7 +902,7 @@
     rows = normed_all.shape[0]
     query_extra, key_extra = mask_rows(item_lengths, rows)
     packed = (
-        product("rd,dc->cr", normed_all, qkv_weight).astype(bf16).reshape(heads, 3, HEAD_DIM, rows)
+        product("rd,cd->cr", normed_all, qkv_turned).astype(bf16).reshape(heads, 3, HEAD_DIM, rows)
     )
     attended, log_total = attend_forward(packed, query_extra, key_extra)
     up_all = everything[:, :, :, :, :first].reshape(-1, tokens.shape[1])
@@ -389,25 +930,33 @@
         product("rd,ad->ar", grad_branch, proj_all).astype(bf16),
         "narrow", split_axis=0, concat_axis=1, tiled=True,
     ).reshape(heads, HEAD_DIM, rows)
-    grad_down = scatter_share(product("rf,rd->fd", hidden, cotangent))
-    grad_up = scatter_share(product("rf,rd->fd", grad_pre, expand_in)).T
-    grad_proj = scatter_share(product("ar,rd->ad", attended_rows, grad_branch))
-    grad_packed = attend_backward(
-        packed, query_extra, key_extra, attended, grad_attended, log_total, items
-    ).reshape(heads * 3 * HEAD_DIM, rows)
-    grad_normed = scatter_rows(product("cr,dc->rd", grad_packed, qkv_weight))
-    grad_qkv = product("rd,cr->dc", normed_all, grad_packed)
-    grad_token_norm, grad_gain_one, grad_bias_one = jax.vjp(
-        norm_forward, token_rows, gain_one, bias_one
-    )[1](grad_normed)
-    grad_tokens = (grad_middle + grad_token_norm).astype(bf16)
-    norm_parts = jnp.stack([grad_gain_one, grad_bias_one, grad_gain_two, grad_bias_two])
-    norm_sums = lax.psum(norm_parts, ("wide", "narrow"))
-    share = norm_sums.shape[1] // lax.axis_size("narrow")
+    grad_parts = jnp.concatenate(
+        [
+            split_parts(product("rf,rd->fd", grad_pre, expand_in).astype(bf16)),
+            split_parts(product("rf,rd->fd", hidden, cotangent).astype(bf16)),
+            split_parts(product("ar,rd->ad", attended_rows, grad_branch).astype(bf16)),
+        ],
+        axis=4,
+    )
+    grad_packed, grad_piece = attend_backward(
+        wide, narrow, packed, query_extra, key_extra, attended, grad_attended, log_total,
+        grad_parts, items,
+    )
+    grad_packed = grad_packed.reshape(heads * 3 * HEAD_DIM, rows)
+    norm_parts = jnp.zeros((8, tokens.shape[1]), f32)
+    norm_parts = norm_parts.at[2].set(grad_gain_two).at[3].set(grad_bias_two)
+    grad_tokens, grad_qkv, grad_shard, norm_sums = finish(
+        wide, narrow, grad_packed, qkv_turned, normed_all, tokens, grad_middle,
+        gain_one.reshape(1, -1), norm_parts, grad_piece,
+    )
+    grad_shard = grad_shard.astype(f32)
+    grad_up = grad_shard[:, :, :first].reshape(-1, tokens.shape[1]).T
+    grad_down = grad_shard[:, :, first : 2 * first].reshape(-1, tokens.shape[1])
+    grad_proj = grad_shard[:, :, 2 * first :].reshape(-1, tokens.shape[1])
+    share = norm_sums.shape[1] // narrow
     shares = lax.dynamic_slice_in_dim(norm_sums, lax.axis_index("narrow") * share, share, 1)
-    grad_qkv = lax.psum(grad_qkv.astype(bf16), "wide").astype(f32)
     return (
-        output, grad_tokens, shares[0], shares[1], grad_qkv, grad_proj,
+        output, grad_tokens, shares[0], shares[1], grad_qkv.T.astype(f32), grad_proj,
         shares[2], shares[3], grad_up, grad_down,
     )
 

time: 747 us -> 622 us (0.83)
  waiting for transfers between devices: 189 us -> 9.81 us
  Pallas kernels: 278 us -> 419 us
  blocking collectives: 79.3 us -> 0 us
  matrix products: 112 us -> 89.6 us
    pallas_call x1 -> x2, Pallas kernels: 82.7 us -> 222 us  [the longest x1 117 us: attend_backward(): pl.pallas_call(functools.partial(backward_kernel, block, rows, items, wid...]
    reduce_scatter x4 -> x0, waiting for transfers between devices: 134 us -> none  [the longest x1 79.3 us: scatter_rows(): lax.psum_scatter(partial_sum.astype(bf16), 'narrow', scatter_dimension=0,...]
    psum x1 -> x0, waiting for transfers between devices: 44.5 us -> none  [scatter_share(): return lax.psum(part, 'wide').astype(f32)]
    all_to_all x1 -> x0, blocking collectives: 41.1 us -> none  [body(): lax.all_to_all(product('rd,ad->ar', grad_branch, proj_all).astype(bf16),...]
    psum x1 -> x0, blocking collectives: 38.2 us -> none  [body(): norm_sums = lax.psum(norm_parts, ('wide', 'narrow'))]
    dot_general x12 -> x10, matrix products: 112 us -> 89.6 us  [product(): return jnp.einsum(spec, left, right, preferred_element_type=f32)]
    concatenate x0 -> x1, other arithmetic: none -> 16.5 us  [body(): jnp.concatenate([split_parts(product('rf,rd->fd', grad_pre, expand_in).as...]
    unnamed x62 -> x56, local copies, waits for them, and re-layouts: 15.2 us -> 14.6 us
  transfers between devices with their start and end apart: 7 -> 3, of which waited for: 4 -> 1; matrix products, arithmetic and copies ran while one was open for 11% -> 9% of each run, Pallas kernels for 31% -> 24%
where the time goes in v3:
time: 622 us; the launch traced here: 612 us
  Pallas kernels  419 us (67%)
  matrix products  89.6 us (14%)
  local copies, waits for them, and re-layouts  43.4 us (7%)
  other arithmetic  28.4 us (5%)
  between operations  14.9 us (2%)
  waiting for transfers between devices  9.81 us (2%)
  starting transfers between devices  7.54 us (1%)
    pallas_call x1, Pallas kernels, gather_weights(): pl.pallas_call(functools.partial(gather_kernel, W, N), out_shape=jax.Shap...  150 us
    pallas_call x1, Pallas kernels, attend_backward(): pl.pallas_call(functools.partial(backward_kernel, block, rows, items, wid...  117 us
    pallas_call x1, Pallas kernels, finish(): pl.pallas_call(functools.partial(finish_kernel, wide, narrow, chunks), in...  106 us
    dot_general x10, matrix products, product(): return jnp.einsum(spec, left, right, preferred_element_type=f32)  89.6 us
    pallas_call x1, Pallas kernels, attend_forward(): pl.pallas_call(functools.partial(forward_kernel, block, rows), grid=(head...  46.8 us
    concatenate x1, other arithmetic, body(): jnp.concatenate([split_parts(product('rf,rd->fd', grad_pre, expand_in).as...  16.5 us
    unnamed x56, local copies, waits for them, and re-layouts  14.6 us
  transfers between devices with their start and end apart: 3, of which 1 were waited for; matrix products, arithmetic and copies ran while one was open for 9% of the time, Pallas kernels for 24%

profile of v3, /device:TPU:0, one launch (start us, length us, event | category | flops | bytes accessed | tf_op | source)
XLA Modules:
  0.0 612.5 jit_solution(11204688838576556770)
XLA Ops:
  7.2 0.0 all-gather.2.cloned.1.call-start
  7.2 1.4 convert_reduce_fusion
  8.7 1.6 fusion.15
  10.3 0.7 convert_element_type.76
  11.0 0.7 convert_element_type.77
  11.7 2.6 fusion.18
  14.3 0.0 all-gather.2.cloned.1.call-update
  14.4 1.5 copy.41
  15.9 1.6 pad_maximum_fusion.1.own
  17.5 0.0 copy-start.22
  17.5 0.0 copy-start.16
  17.5 149.9 %gather_weights.1 = bf16[8,2,2,2,144,1024]{5,4,3,2,1,0:T(8,128)(2,1)S(1)} custom-call(bf16[2,2,2,144,1024]{4,3,2,1,0:T(8,128)(2,1)S(1)} %pad_maximum_fusion.1.own), custom_call_target="tpu_custom_call" | custom-call | tf_op jit(solution)/shard_map/gather_weights/pallas_call | solution.py:871
  167.4 6.5 %copy-done = bf16[8,2,2,2,144,1024]{5,4,3,2,1,0:T(8,128)(2,1)} copy-done((bf16[8,2,2,2,144,1024]{5,4,3,2,1,0:T(8,128)(2,1)}, bf16[8,2,2,2,144,1024]{5,4,3,2,1,0:T(8,128)(2,1)S(1)}, u32[]{:S(2)}) %copy-start) | copy-done | bytes 18874392
  173.9 0.1 select_reduce_fusion
  174.0 0.1 convert_reduce_fusion.1
  174.1 0.1 select_convert_fusion.1.qx_ref
  174.3 0.0 copy-start.2
  174.3 0.1 select_convert_fusion.kx_ref
  174.4 0.0 all-gather.2.cloned.1.call-done.normed_ref
  174.4 6.9 %convolution_convert_fusion.2 = bf16[4096,384]{0,1:T(8,128)(2,1)S(1)} fusion(bf16[4096,1024]{1,0:T(8,128)(2,1)} %all-gather.2.cloned.1.call-done.normed_ref, bf16[1024,384]{1,0:T(8,128)(2,1)S(1)} %copy-done.16), kind=kOutput, calls=%fused_computation.28 | convolution fusion | flops 3222798336 | bytes 12320768 | tf_op jit(solution)/shard_map/rd,cd->cr/dot_general | solution.py:766
  181.3 0.0 copy-start.20
  181.3 0.0 copy-start.21
  181.3 46.8 %attend_forward.1 = (bf16[2,64,4096]{2,1,0:T(8,128)(2,1)S(1)}, f32[2,1,4096]{2,1,0:T(1,128)S(1)}) custom-call(bf16[16,4096]{1,0:T(8,128)(2,1)S(1)} %select_convert_fusion.1.qx_ref, bf16[16,4096]{1,0:T(8,128)(2,1)S(1)} %select_convert_fusion.kx_ref, bf16[2,3,64,4096]{3,2,1,0:T(8,128)(2,1)S(1)} %bitcast.77, bf16[2,3,64,4096]{3,2,1,0:T(8,128)(2,1)S(1)} %bitcast.78, ...), custom_call_target="tpu_custom_call" | custom-call | flops 34359738368 | bytes 4194304 | tf_op jit(solution)/shard_map/attend_forward/pallas_call | solution.py:81
  228.1 1.0 copy-done.1
  229.1 0.4 copy.49
  229.5 1.3 copy.42
  230.8 3.8 all-to-all-start
  234.6 1.2 copy.45
  235.8 3.2 slice.59
  239.0 12.3 %fusion.26 = (bf16[8,2,2,2,64,1024]{5,4,3,2,1,0:T(8,128)(2,1)}, bf16[8,2,2,2,64,1024]{5,4,3,2,1,0:T(8,128)(2,1)}) fusion(bf16[8,2,2,2,144,1024]{5,4,3,2,1,0:T(8,128)(2,1)} %copy-done), kind=kLoop, calls=%fused_computation.75 | loop fusion | bytes 33554432 | tf_op jit(solution)/shard_map/slice | solution.py:909
  251.3 9.8 %all-to-all-done = bf16[128,8,512]{2,0,1:T(8,128)(2,1)S(1)} async-done(((bf16[128,8,512]{2,0,1:T(8,128)(2,1)}), bf16[128,8,512]{2,0,1:T(8,128)(2,1)S(1)}, u32[]{:S(2)}, u32[]{:S(2)}) %all-to-all-start) | async-done | bytes 1048608 | tf_op jit(solution)/shard_map/all_to_all | solution.py:911
  261.1 1.0 copy-done.11
  262.0 4.0 fusion.28
  266.1 0.4 multiply_reduce_fusion.2
  266.4 0.0 copy-start.14
  266.4 30.1 %multiply_convert_fusion = (bf16[512,4096]{1,0:T(8,128)(2,1)}, f32[512,4096]{1,0:T(8,128)}, f32[512,4096]{1,0:T(8,128)}) fusion(bf16[4096,1024]{1,0:T(8,128)(2,1)S(1)} %bitcast.90, f32[512,1024]{1,0:T(8,128)S(1)} %get-tuple-element.110, f32[1024]{0:T(1024)S(1)} %convert_element_type.82, f32[1024]{0:T(1024)S(1)} %convert_element_type.81, ...), kind=kOutput, calls=%fused_computation.12 | convolution fusion | flops 4433903616 | bytes 31469568 | tf_op jit(solution)/shard_map/rd,fd->rf/dot_general | solution.py:766
  296.6 11.8 %fusion.6 = bf16[512,4096]{1,0:T(8,128)(2,1)} fusion(f32[512,4096]{1,0:T(8,128)} %get-tuple-element.100, f32[512,4096]{1,0:T(8,128)} %get-tuple-element.111, bf16[4096,1024]{1,0:T(8,128)(2,1)S(1)} %bitcast.89, bf16[512,1024]{1,0:T(8,128)(2,1)S(1)} %copy-done.14), kind=kOutput, calls=%fused_computation.10 | convolution fusion | flops 4324327424 | bytes 30408704 | tf_op jit(solution)/shard_map/rd,fd->rf/dot_general | solution.py:766
  308.4 7.4 %multiply_reduce_fusion = (f32[1024]{0:T(1024)S(1)}, f32[512]{0:T(512)S(1)}, f32[1024]{0:T(1024)S(1)}, f32[512,1024]{1,0:T(8,128)S(1)}) fusion(f32[512,1024]{1,0:T(8,128)S(1)} %get-tuple-element.110, f32[512]{0:T(512)S(1)} %fusion.22, f32[512]{0:T(512)S(1)} %broadcast_multiply_fusion, f32[1024]{0:T(1024)S(1)} %convert_element_type.81, ...), kind=kOutput, calls=%fused_computation.40 | convolution fusion | flops 4299159040 | bytes 16795648 | tf_op jit(solution)/shard_map/rf,fd->rd/dot_general | solution.py:766
  315.7 0.0 copy-start.8
  315.8 0.7 fusion.24
  316.5 0.0 copy-start.12
  316.5 0.3 add_add_fusion.1.middle_ref
  316.8 0.5 copy-done.8
  317.3 2.3 convolution_convert_fusion.4
  319.7 2.6 convolution_convert_fusion.3
  322.2 7.2 %convolution_convert_fusion.1 = bf16[4096,1024]{1,0:T(8,128)(2,1)} fusion(bf16[512,4096]{1,0:T(8,128)(2,1)S(1)} %copy-done.23, f32[512,1024]{1,0:T(8,128)S(1)} %get-tuple-element.110, f32[1024]{0:T(1024)S(1)} %convert_element_type.82, f32[1024]{0:T(1024)S(1)} %convert_element_type.81, f32[512]{0:T(512)S(1)} %fusion.22, f32[512]{0:T(512)S(1)} %broadcast_multiply_fusion), kind=kOutput, calls=%fused_computation.27 | convolution fusion | flops 4301783040 | bytes 14692352 | tf_op jit(solution)/shard_map/rf,rd->fd/dot_general | solution.py:766
  329.4 3.7 all-to-all-start.1
  333.2 7.2 %convolution_convert_fusion = bf16[4096,1024]{1,0:T(8,128)(2,1)S(1)} fusion(bf16[512,4096]{1,0:T(8,128)(2,1)} %get-tuple-element.99, bf16[512,1024]{1,0:T(8,128)(2,1)} %param.16), kind=kOutput, calls=%fused_computation.26 | convolution fusion | flops 4299161600 | bytes 13631488 | tf_op jit(solution)/shard_map/rf,rd->fd/dot_general | solution.py:766
  340.4 16.5 %pad_maximum_fusion.parts_ref = bf16[8,2,2,2,144,1024]{5,4,3,2,1,0:T(8,128)(2,1)} fusion(bf16[8,2,2,2,16,1024]{5,4,3,2,1,0:T(8,128)(2,1)S(1)} %bitcast.101, bf16[8,2,2,2,64,1024]{5,4,3,2,1,0:T(8,128)(2,1)S(1)} %bitcast.93, bf16[8,2,2,2,64,1024]{5,4,3,2,1,0:T(8,128)(2,1)S(1)} %bitcast.92), kind=kLoop, calls=%fused_computation | loop fusion | flops 56623104 | bytes 37748736 | tf_op jit(solution)/shard_map/concatenate | solution.py:933
  356.9 0.1 scatter.9.norm_ref
  357.0 0.0 copy-start.18
  357.1 10.1 %add_convert_fusion = bf16[512,1024]{1,0:T(8,128)(2,1)} fusion(f32[512,1024]{1,0:T(8,128)S(1)} %get-tuple-element.110, bf16[512,4096]{1,0:T(8,128)(2,1)} %get-tuple-element.99, bf16[4096,1024]{1,0:T(8,128)(2,1)} %bitcast.86), kind=kOutput, calls=%fused_computation.43 | convolution fusion | flops 4296015872 | bytes 15728640 | tf_op jit(solution)/shard_map/rf,fd->rd/dot_general | solution.py:766
  367.2 0.6 copy.44
  367.8 1.5 reshape.193.do_ref
  369.3 116.7 %attend_backward.1 = (bf16[2,3,64,4096]{3,2,1,0:T(8,128)(2,1)}, bf16[2,144,1024]{2,1,0:T(8,128)(2,1)}) custom-call(bf16[16,4096]{1,0:T(8,128)(2,1)} %copy-done.2, bf16[16,4096]{1,0:T(8,128)(2,1)} %copy-done.3, bf16[2,3,64,4096]{3,2,1,0:T(8,128)(2,1)} %bitcast.80, bf16[2,3,64,4096]{3,2,1,0:T(8,128)(2,1)} %bitcast.81, bf16[2,3,64,4096]{3,2,1,0:T(8,128)(2,1)} %bitcast.82, ...), custom_call_target="tpu_custom_call" | custom-call | flops 85899345920 | bytes 8388608 | tf_op jit(solution)/shard_map/attend_backward/pallas_call | solution.py:399
  486.0 105.5 %finish.1 = (bf16[512,1024]{1,0:T(8,128)(2,1)}, bf16[384,1024]{1,0:T(8,128)(2,1)}, bf16[4,2,144,1024]{3,2,1,0:T(8,128)(2,1)}, f32[8,1024]{1,0:T(8,128)}) custom-call(bf16[384,4096]{1,0:T(8,128)(2,1)} %bitcast.100, bf16[384,1024]{1,0:T(8,128)(2,1)} %bitcast.99, bf16[4096,1024]{1,0:T(8,128)(2,1)} %all-gather.2.cloned.1.call-done.normed_ref, ...), custom_call_target="tpu_custom_call" | custom-call | tf_op jit(solution)/shard_map/finish/pallas_call | solution.py:716
  591.6 1.9 slice.69
  593.4 3.4 fusion.27
  596.9 0.7 constant_dynamic-slice_fusion
  597.5 0.5 slice_bitcast_fusion
  598.1 1.3 convert_bitcast_fusion
  599.4 3.0 copy.47
  602.4 1.8 copy.46
  604.2 1.0 copy.52
  (52 shorter events, 0.2 us)
Async XLA Ops:
  7.2 167.2 %all-gather.2.cloned.1.call-start = ((), (), s32[]{:S(2)}) async-start(), calls=%async_computation.2 | async-start | bytes 9437184 | tf_op jit(solution)/shard_map/all_gather | solution.py:900
  11.0 0.7 copy-start.19
  17.5 156.5 %copy-start.22 = (s32[1,4]{1,0:T(1,128)S(1)}, s32[1,4]{1,0:T(1,128)}, u32[]{:S(2)}) copy-start(s32[1,4]{1,0:T(1,128)} %param.17) | copy-start | bytes 52
  17.5 156.9 %copy-start.16 = (bf16[1024,384]{1,0:T(8,128)(2,1)S(1)}, bf16[1024,384]{1,0:T(8,128)(2,1)}, u32[]{:S(2)}) copy-start(bf16[1024,384]{1,0:T(8,128)(2,1)} %param.20) | copy-start | bytes 2359300
  167.4 6.5 %copy-start = (bf16[8,2,2,2,144,1024]{5,4,3,2,1,0:T(8,128)(2,1)}, bf16[8,2,2,2,144,1024]{5,4,3,2,1,0:T(8,128)(2,1)S(1)}, u32[]{:S(2)}) copy-start(bf16[8,2,2,2,144,1024]{5,4,3,2,1,0:T(8,128)(2,1)S(1)} %gather_weights.1) | copy-start | bytes 56623108
  174.3 7.0 %copy-start.2 = (bf16[16,4096]{1,0:T(8,128)(2,1)}, bf16[16,4096]{1,0:T(8,128)(2,1)S(1)}, u32[]{:S(2)}) copy-start(bf16[16,4096]{1,0:T(8,128)(2,1)S(1)} %select_convert_fusion.1.qx_ref) | copy-start | bytes 393220
  174.4 6.9 %copy-start.3 = (bf16[16,4096]{1,0:T(8,128)(2,1)}, bf16[16,4096]{1,0:T(8,128)(2,1)S(1)}, u32[]{:S(2)}) copy-start(bf16[16,4096]{1,0:T(8,128)(2,1)S(1)} %select_convert_fusion.kx_ref) | copy-start | bytes 393220
  181.3 46.8 %copy-start.4 = (bf16[4096,384]{0,1:T(8,128)(2,1)}, bf16[4096,384]{0,1:T(8,128)(2,1)S(1)}, u32[]{:S(2)}) copy-start(bf16[4096,384]{0,1:T(8,128)(2,1)S(1)} %convolution_convert_fusion.2) | copy-start | bytes 9437188
  181.3 54.5 %copy-start.20 = (bf16[1024]{0:T(1024)(128)(2,1)S(1)}, bf16[1024]{0:T(1024)(128)(2,1)}, u32[]{:S(2)}) copy-start(bf16[1024]{0:T(1024)(128)(2,1)} %param.22) | copy-start | bytes 6148
  181.3 54.5 %copy-start.21 = (bf16[1024]{0:T(1024)(128)(2,1)S(1)}, bf16[1024]{0:T(1024)(128)(2,1)}, u32[]{:S(2)}) copy-start(bf16[1024]{0:T(1024)(128)(2,1)} %param.23) | copy-start | bytes 6148
  228.1 1.0 copy-start.1
  228.1 1.4 copy-start.5
  230.8 30.3 %all-to-all-start = ((bf16[128,8,512]{2,0,1:T(8,128)(2,1)}), bf16[128,8,512]{2,0,1:T(8,128)(2,1)S(1)}, u32[]{:S(2)}, u32[]{:S(2)}) async-start(bf16[128,8,512]{2,0,1:T(8,128)(2,1)} %copy.42), calls=%async_computation | async-start | bytes 2097152 | tf_op jit(solution)/shard_map/all_to_all | solution.py:911
  239.0 23.0 %copy-start.6 = (bf16[512,1024]{1,0:T(8,128)(2,1)S(1)}, bf16[512,1024]{1,0:T(8,128)(2,1)}, u32[]{:S(2)}) copy-start(bf16[512,1024]{1,0:T(8,128)(2,1)} %token_ref.1) | copy-start | bytes 3145732
  261.1 1.0 copy-start.11
  261.1 5.4 copy-start.9
  262.0 34.5 %slice-start = ((s8[8388608]{0:T(1024)(128)(4,1)}), s8[4194304]{0:T(1024)(128)(4,1)S(1)}, s32[]{:S(2)}) async-start(s8[8388608]{0:T(1024)(128)(4,1)} %bitcast.87), calls=%async_computation.3 | async-start | bytes 8388608
  266.4 30.1 %slice-start.1 = ((s8[8388608]{0:T(1024)(128)(4,1)}), s8[4194304]{0:T(1024)(128)(4,1)S(1)}, s32[]{:S(2)}) async-start(s8[8388608]{0:T(1024)(128)(4,1)} %bitcast.87), calls=%async_computation.4 | async-start | bytes 8388608
  266.4 30.1 %copy-start.14 = (bf16[512,1024]{1,0:T(8,128)(2,1)S(1)}, bf16[512,1024]{1,0:T(8,128)(2,1)}, u32[]{:S(2)}) copy-start(bf16[512,1024]{1,0:T(8,128)(2,1)} %param.16) | copy-start | bytes 3145732
  315.7 1.6 copy-start.8
  316.5 3.2 copy-start.12
  317.3 2.3 copy-start.7
  317.3 4.9 copy-start.23
  329.4 37.8 %all-to-all-start.1 = ((bf16[8,128,512]{2,1,0:T(8,128)(2,1)}), bf16[8,128,512]{2,1,0:T(8,128)(2,1)S(1)}, u32[]{:S(2)}, u32[]{:S(2)}) async-start(bf16[8,128,512]{2,1,0:T(8,128)(2,1)} %bitcast.105), calls=%async_computation.1 | async-start | bytes 2097152 | tf_op jit(solution)/shard_map/all_to_all | solution.py:929
  333.2 7.2 %copy-start.10 = (bf16[4096,1024]{1,0:T(8,128)(2,1)S(1)}, bf16[4096,1024]{1,0:T(8,128)(2,1)}, u32[]{:S(2)}) copy-start(bf16[4096,1024]{1,0:T(8,128)(2,1)} %convolution_convert_fusion.1) | copy-start | bytes 25165828
  333.2 7.2 %copy-start.13 = (bf16[1024,1024]{1,0:T(8,128)(2,1)S(1)}, bf16[1024,1024]{1,0:T(8,128)(2,1)}, u32[]{:S(2)}) copy-start(bf16[1024,1024]{1,0:T(8,128)(2,1)} %convolution_convert_fusion.3) | copy-start | bytes 6291460
  357.0 10.1 %copy-start.18 = (f32[8,1024]{1,0:T(8,128)}, f32[8,1024]{1,0:T(8,128)S(1)}, u32[]{:S(2)}) copy-start(f32[8,1024]{1,0:T(8,128)S(1)} %scatter.9.norm_ref) | copy-start | bytes 98308
  591.6 6.5 %copy-start.17 = (bf16[384,1024]{1,0:T(8,128)(2,1)S(1)}, bf16[384,1024]{1,0:T(8,128)(2,1)}, u32[]{:S(2)}) copy-start(bf16[384,1024]{1,0:T(8,128)(2,1)} %get-tuple-element.52) | copy-start | bytes 2359300
  593.4 10.8 %copy-start.15 = (bf16[512,1024]{1,0:T(8,128)(2,1)S(1)}, bf16[512,1024]{1,0:T(8,128)(2,1)}, u32[]{:S(2)}) copy-start(bf16[512,1024]{1,0:T(8,128)(2,1)} %get-tuple-element.124) | copy-start | bytes 3145732
Sparse Core Ops, SparseCore 0:
  14.5 106.6 all-gather.1

commit v4 on v3

--- a/solution.py
+++ b/solution.py
@@ -16,17 +16,6 @@
 f32 = jnp.float32
 MESH = pl.DeviceIdType.MESH
 epsilon = 1e-05
-
-
-def norm_forward(values, norm_gain, norm_bias):
-    average = jnp.mean(values, axis=-1, keepdims=True)
-    centred = values - average
-    variance = jnp.mean(centred * centred, axis=-1, keepdims=True)
-    return centred * lax.rsqrt(variance + epsilon) * norm_gain + norm_bias
-
-
-def gelu_exact(values):
-    return jax.nn.gelu(values, approximate=False)
 
 
 def mask_rows(item_lengths, rows):
@@ -46,65 +35,125 @@
     return query_extra, key_extra
 
 
-def forward_kernel(block, rows, qx_ref, kx_ref, q_ref, k_ref, v_ref, o_ref, log_ref, keys):
-    width = q_ref.shape[-1]
-
-    @pl.when(pl.program_id(1) == 0)
+def forward_kernel(
+    wide, narrow, qx_ref, kx_ref, q_ref, k_ref, v_ref, own_ref, o_ref, log_ref, rows_ref, gathered,
+    keys, ready, copied, sent, got, *gather_refs,
+):
+    gather = Gather(wide, narrow, own_ref, gathered, *gather_refs)
+    w, n, lines = gather.w, gather.n, gather.lines
+    head, step = pl.program_id(0), pl.program_id(1)
+    moment = head * narrow + step
+    width = q_ref.shape[-1] // narrow
+    last = heads_of(ready, narrow) * narrow - 1
+
+    moves = [(0.0, lambda: greet(wide, narrow, w, n)), (0.1, gather.begin)]
+    for d in range(1, lines):
+        moves += [
+            (3.0 * d, functools.partial(gather.sides, d, gather.one)),
+            (3.0 * d + 2.1, functools.partial(gather.sides, d, gather.two)),
+            (3.0 * d + 5.2, functools.partial(gather.sides, d, gather.three)),
+        ]
+    moves.append((900.0, gather.finish))
+    moves.sort(key=lambda move: move[0])
+
+    def perform(lower, upper):
+        for time, move in moves:
+            if lower <= time < upper:
+                move()
+
+    for tick in range(last + 1):
+
+        @pl.when(moment == tick)
+        def _():
+            perform(tick, tick + 1)
+
+    @pl.when(step == 0)
     def _():
         keys[...] = jnp.concatenate([k_ref[0], kx_ref[...]], axis=0).T
 
-    query = jnp.concatenate([q_ref[0] * jnp.asarray(0.125, bf16), qx_ref[...]], axis=0)
-    maximum = jnp.full((1, width), -3e38, f32)
-    total = jnp.zeros((1, width), f32)
-    gathered = jnp.zeros((HEAD_DIM, width), f32)
-    for i in range(rows // block):
-        part = pl.ds(i * block, block)
-        scores = jnp.dot(keys[part, :], query, preferred_element_type=f32)
-        larger = jnp.maximum(maximum, jnp.max(scores, axis=0, keepdims=True))
-        raised = jnp.exp(scores - larger)
-        shrink = jnp.exp(maximum - larger)
-        total = shrink * total + jnp.sum(raised, axis=0, keepdims=True)
-        gathered = shrink * gathered + jnp.dot(
-            v_ref[0, :, part], raised.astype(bf16), preferred_element_type=f32
-        )
-        maximum = larger
-    o_ref[0] = (gathered / total).astype(bf16)
-    log_ref[0] = maximum + jnp.log(total)
-
-
-def attend_forward(packed, query_extra, key_extra, width=1024, block=1024):
+    owner = lax.rem(n + 1 + step, narrow)
+    columns = pl.ds(pl.multiple_of(owner * width, width), width)
+    query = jnp.concatenate(
+        [q_ref[0, :, columns] * jnp.asarray(0.125, bf16), qx_ref[:, columns]], axis=0
+    )
+    scores = jnp.dot(keys[...], query, preferred_element_type=f32)
+    maximum = jnp.max(scores, axis=0, keepdims=True)
+    raised = jnp.exp(scores - maximum)
+    total = jnp.sum(raised, axis=0, keepdims=True)
+    gathered_values = jnp.dot(v_ref[0], raised.astype(bf16), preferred_element_type=f32)
+    result = (gathered_values / total).astype(bf16)
+    o_ref[0, :, columns] = result
+    log_ref[0, :, columns] = maximum + jnp.log(total)
+    ready[moment] = result
+
+    def deliver(k, owner, h):
+        return remote(ready.at[k], rows_ref.at[n, h], sent.at[k], got.at[n, h], w, owner)
+
+    def deliver_here(k, h):
+        return pltpu.make_async_copy(ready.at[k], rows_ref.at[n, h], copied.at[h])
+
+    @pl.when(step < narrow - 1)
+    def _():
+        deliver(moment, owner, head).start()
+
+    @pl.when(step == narrow - 1)
+    def _():
+        deliver_here(moment, head).start()
+
+    @pl.when(moment == last)
+    def _():
+        perform(last + 1, 1000)
+        for h in range((last + 1) // narrow):
+            deliver_here(h * narrow + narrow - 1, h).wait()
+            for t in range(narrow - 1):
+                deliver(h * narrow + t, lax.rem(n + 1 + t, narrow), h).wait_send()
+                source = lax.rem(n + narrow - 1 - t, narrow)
+                arrived(rows_ref.at[source, h], got.at[source, h])
+
+
+def heads_of(ready, narrow):
+    return ready.shape[0] // narrow
+
+
+def attend_forward(wide, narrow, packed, query_extra, key_extra, own):
     heads, _, _, rows = packed.shape
+    width = rows // narrow
+    dma = pltpu.SemaphoreType.DMA
 
     def whole(j):
         return pl.BlockSpec((1, None, HEAD_DIM, rows), lambda h, i: (h, j, 0, 0))
 
+    extra = pl.BlockSpec((EXTRA, rows), lambda h, i: (0, 0))
+    anywhere = pl.BlockSpec(memory_space=pl.ANY)
     return pl.pallas_call(
-        functools.partial(forward_kernel, block, rows),
-        grid=(heads, rows // width),
-        in_specs=[
-            pl.BlockSpec((EXTRA, width), lambda h, i: (0, i)),
-            pl.BlockSpec((EXTRA, rows), lambda h, i: (0, 0)),
-            pl.BlockSpec((1, None, HEAD_DIM, width), lambda h, i: (h, 0, 0, i)),
-            whole(1),
-            whole(2),
-        ],
+        functools.partial(forward_kernel, wide, narrow),
+        grid=(heads, narrow),
+        in_specs=[extra, extra, whole(0), whole(1), whole(2), anywhere],
         out_specs=(
-            pl.BlockSpec((1, HEAD_DIM, width), lambda h, i: (h, 0, i)),
-            pl.BlockSpec((1, 1, width), lambda h, i: (h, 0, i)),
+            pl.BlockSpec((1, HEAD_DIM, rows), lambda h, i: (h, 0, 0)),
+            pl.BlockSpec((1, 1, rows), lambda h, i: (h, 0, 0)),
+            anywhere,
+            anywhere,
         ),
         out_shape=(
             jax.ShapeDtypeStruct((heads, HEAD_DIM, rows), bf16),
             jax.ShapeDtypeStruct((heads, 1, rows), f32),
-        ),
-        scratch_shapes=[pltpu.VMEM((rows, HEAD_DIM + EXTRA), bf16)],
-        compiler_params=pltpu.CompilerParams(vmem_limit_bytes=48 << 20),
-        cost_estimate=pl.CostEstimate(
-            flops=4 * heads * rows * rows * 256,
-            bytes_accessed=heads * rows * HEAD_DIM * 8,
-            transcendentals=heads * rows * rows,
+            jax.ShapeDtypeStruct((narrow, heads, HEAD_DIM, width), bf16),
+            jax.ShapeDtypeStruct((narrow, *own.shape), bf16),
+        ),
+        scratch_shapes=[
+            pltpu.VMEM((rows, HEAD_DIM + EXTRA), bf16),
+            pltpu.VMEM((heads * narrow, HEAD_DIM, width), bf16),
+            dma((heads,)),
+            dma((heads * narrow,)),
+            dma((narrow, heads)),
+            *Gather.scratch(wide, narrow),
+        ],
+        compiler_params=pltpu.CompilerParams(
+            vmem_limit_bytes=58 << 20, collective_id=4, has_side_effects=True
         ),
         name="attend_forward",
-    )(query_extra, key_extra, packed, packed, packed)
+    )(query_extra, key_extra, packed, packed, packed, own)
 
 
 def remote(src, dst, sent, received, wide_to, narrow_to):
@@ -161,7 +210,7 @@
 
 
 def reduce_steps(
-    wide, narrow, parts, final, held, from_sibling, from_first, from_second, from_line,
+    wide, narrow, parts, proj_parts, final, held, from_sibling, from_first, from_second, from_line,
     loaded, sib_sent, sib_got, first_sent, first_got, second_sent, second_got, line_sent, line_got,
 ):
     w, n = lax.axis_index("wide"), lax.axis_index("narrow")
@@ -175,13 +224,25 @@
     def other_b(i):
         return lax.rem(b + i, side)
 
+    most, least = parts.shape[4], proj_parts.shape[4]
+    sources = [(parts, pl.ds(0, most)), (proj_parts, pl.ds(most, least))]
+
     def to_sibling(zs):
-        return remote(
-            parts.at[2 * zs + 1 - core], from_sibling.at[zs], sib_sent.at[zs], sib_got.at[zs], w, sibling
-        )
+        shard = 2 * zs + 1 - core
+        return [
+            remote(
+                src.at[shard], from_sibling.at[zs, :, :, :, rows],
+                sib_sent.at[k, zs], sib_got.at[k, zs], w, sibling,
+            )
+            for k, (src, rows) in enumerate(sources)
+        ]
 
     def load(zs):
-        return pltpu.make_async_copy(parts.at[2 * zs + core], held.at[zs], loaded.at[zs])
+        shard = 2 * zs + core
+        return [
+            pltpu.make_async_copy(src.at[shard], held.at[zs, :, :, :, rows], loaded.at[k, zs])
+            for k, (src, rows) in enumerate(sources)
+        ]
 
     def first(zs, h, i):
         if h == 0:
@@ -217,12 +278,14 @@
     def begin():
         greet(wide, narrow, w, n)
         for zs in order:
-            to_sibling(zs).start()
-            load(zs).start()
+            for copy in to_sibling(zs) + load(zs):
+                copy.start()
 
     def combine(zs):
-        load(zs).wait()
-        arrived(from_sibling.at[zs], sib_got.at[zs])
+        for copy in load(zs):
+            copy.wait()
+        for k, (_, rows) in enumerate(sources):
+            arrived(from_sibling.at[zs, :, :, :, rows], sib_got.at[k, zs])
 
         def piece(j, carry):
             p, q = j // side, lax.rem(j, side)
@@ -269,7 +332,8 @@
                 total = total + from_line[slot, h].astype(f32)
             final[h] = total.astype(bf16)
         for zs in order:
-            to_sibling(zs).wait_send()
+            for copy in to_sibling(zs):
+                copy.wait_send()
             for h, i in halves:
                 first(zs, h, i).wait_send()
                 second(zs, h, i).wait_send()
@@ -299,9 +363,9 @@
         pltpu.VMEM((lines, 2, side - 1, side, rows, features), bf16),
         pltpu.VMEM((lines, 2, side - 1, rows, features), bf16),
         pltpu.VMEM((lines - 1, 2, rows, features), bf16),
-        dma((lines,)),
-        dma((lines,)),
-        dma((lines,)),
+        dma((2, lines)),
+        dma((2, lines)),
+        dma((2, lines)),
         dma((lines, 2, side - 1)),
         dma((lines, 2, side - 1)),
         dma((lines, 2, side - 1)),
@@ -313,14 +377,14 @@
 
 def backward_kernel(
     block, rows, items, wide, narrow, qx_ref, kx_ref, q_ref, k_ref, v_ref, o_ref, do_ref, log_ref,
-    parts_ref, grad_ref, final_ref, keys, values, grad_k, grad_v, *reduce_refs,
+    parts_ref, proj_parts_ref, grad_ref, final_ref, keys, values, grad_k, grad_v, *reduce_refs,
 ):
     width = q_ref.shape[-1]
     step = pl.program_id(1)
     steps_per_head = pl.num_programs(1)
     moment = pl.program_id(0) * steps_per_head + step
     ticks = ATTENTION_STEPS
-    moves, times = reduce_steps(wide, narrow, parts_ref, final_ref, *reduce_refs)
+    moves, times = reduce_steps(wide, narrow, parts_ref, proj_parts_ref, final_ref, *reduce_refs)
 
     def perform(lower, upper):
         for move, time in zip(moves, times):
@@ -386,11 +450,12 @@
 
 
 def attend_backward(
-    wide, narrow, packed, query_extra, key_extra, attended, grad, log_total, parts, items, block=512
+    wide, narrow, packed, query_extra, key_extra, attended, grad, log_total, parts,
+    proj_parts, items, block=512,
 ):
     heads, _, _, rows = packed.shape
     width = heads * rows // ATTENTION_STEPS
-    piece = parts.shape[4:]
+    piece = (parts.shape[4] + proj_parts.shape[4], parts.shape[5])
 
     def whole(j):
         return pl.BlockSpec((1, None, HEAD_DIM, rows), lambda h, i: (h, j, 0, 0))
@@ -409,6 +474,7 @@
             part,
             pl.BlockSpec((1, 1, width), lambda h, i: (h, 0, i)),
             pl.BlockSpec(memory_space=pl.ANY),
+            pl.BlockSpec(memory_space=pl.ANY),
         ],
         out_specs=(
             pl.BlockSpec((1, 3, HEAD_DIM, rows), lambda h, i: (h, 0, 0, 0)),
@@ -434,7 +500,157 @@
             transcendentals=heads * rows * rows,
         ),
         name="attend_backward",
-    )(query_extra, key_extra, packed, packed, packed, attended, grad, log_total, parts)
+    )(query_extra, key_extra, packed, packed, packed, attended, grad, log_total, parts, proj_parts)
+
+
+def contract(left, right, left_axis, right_axis):
+    return lax.dot_general(
+        left, right, (((left_axis,), (right_axis,)), ((), ())), preferred_element_type=f32
+    )
+
+
+def gelu_pair(values):
+    half = 0.5 + 0.5 * lax.erf(values * 0.7071067811865476)
+    slope = half + values * (jnp.exp(values * values * -0.5) * 0.3989422804014327)
+    return values * half, slope
+
+
+def mlp_kernel(
+    att_ref, proj_ref, token_ref, cot_ref, gain_ref, bias_ref, up_ref, down_ref,
+    out_ref, middle_out, att_out, proj_out, parts_ref, norm_ref,
+    middle, expand, out_total, expand_total,
+):
+    step = pl.program_id(0)
+    rows, features = token_ref.shape
+    few = 64
+
+    def by_rows(change):
+        def body(j, carry):
+            return change(pl.ds(pl.multiple_of(j * few, few), few), carry)
+
+        return body
+
+    @pl.when(step == 0)
+    def _():
+        middle[...] = token_ref[...].astype(f32) + contract(att_ref[...], proj_ref[...], 0, 0)
+        out_total[...] = jnp.zeros_like(out_total)
+        expand_total[...] = jnp.zeros_like(expand_total)
+
+        def norm(part, carry):
+            values = middle[part, :]
+            centred = values - jnp.mean(values, axis=-1, keepdims=True)
+            variance = jnp.mean(centred * centred, axis=-1, keepdims=True)
+            expand[part, :] = (
+                centred * lax.rsqrt(variance + epsilon) * gain_ref[...] + bias_ref[...]
+            ).astype(bf16)
+            return carry
+
+        lax.fori_loop(0, rows // few, by_rows(norm), 0)
+
+    def flat(ref):
+        if ref.shape[4] % 16:
+            return ref[0].astype(f32).reshape(-1, features).astype(bf16)
+        return ref[0].reshape(-1, features)
+
+    up, down = flat(up_ref), flat(down_ref)
+    units = up_ref.shape[4]
+    pieces = up_ref.shape[1:4]
+    hidden_parts, grad_parts = [], []
+    for part in (pl.ds(0, rows // 2), pl.ds(rows // 2, rows // 2)):
+        hidden, slope = gelu_pair(contract(expand[part, :], up, 1, 1))
+        grad_pre = (contract(cot_ref[part, :], down, 1, 1) * slope).astype(bf16)
+        hidden = hidden.astype(bf16)
+        out_total[part, :] += jnp.dot(hidden, down, preferred_element_type=f32)
+        expand_total[part, :] += jnp.dot(grad_pre, up, preferred_element_type=f32)
+        hidden_parts.append(hidden)
+        grad_parts.append(grad_pre)
+    grad_up = contract(jnp.concatenate(grad_parts, axis=0), expand[...], 0, 0)
+    grad_down = contract(jnp.concatenate(hidden_parts, axis=0), cot_ref[...], 0, 0)
+    parts_ref[0, :, :, :, 0:units, :] = grad_up.reshape(*pieces, units, features).astype(bf16)
+    parts_ref[0, :, :, :, units : 2 * units, :] = grad_down.reshape(
+        *pieces, units, features
+    ).astype(bf16)
+
+    @pl.when(step == pl.num_programs(0) - 1)
+    def _():
+        def finish_rows(part, carry):
+            gain_sum, bias_sum = carry
+            values = middle[part, :]
+            out_ref[part, :] = (values + out_total[part, :]).astype(bf16)
+            centred = values - jnp.mean(values, axis=-1, keepdims=True)
+            inverse = lax.rsqrt(jnp.mean(centred * centred, axis=-1, keepdims=True) + epsilon)
+            scaled = centred * inverse
+            grad = expand_total[part, :]
+            term = grad * gain_ref[...]
+            back = inverse * (
+                term
+                - jnp.mean(term, axis=-1, keepdims=True)
+                - scaled * jnp.mean(term * scaled, axis=-1, keepdims=True)
+            )
+            total = cot_ref[part, :].astype(f32) + back
+            middle_out[part, :] = total
+            expand[part, :] = total.astype(bf16)
+            gain_sum = gain_sum + jnp.sum(grad * scaled, axis=0, keepdims=True)
+            bias_sum = bias_sum + jnp.sum(grad, axis=0, keepdims=True)
+            return gain_sum, bias_sum
+
+        start = (jnp.zeros((1, features), f32), jnp.zeros((1, features), f32))
+        gain_sum, bias_sum = lax.fori_loop(0, rows // few, by_rows(finish_rows), start)
+        row = lax.broadcasted_iota(jnp.int32, (8, features), 0)
+        norm_ref[...] = jnp.where(row == 2, gain_sum, jnp.where(row == 3, bias_sum, 0.0))
+        branch = expand[...]
+        att_out[...] = contract(proj_ref[...], branch, 1, 1).astype(bf16)
+        proj_out[...] = jnp.dot(att_ref[...], branch, preferred_element_type=f32).astype(bf16)
+
+
+def mlp(attended, proj, tokens, cotangent, gain, bias, up_all, down_all, units):
+    rows, features = tokens.shape
+    narrow, side = up_all.shape[:2]
+
+    def whole(*shape):
+        return pl.BlockSpec(shape, lambda i: (0,) * len(shape))
+
+    weights = pl.BlockSpec((1, side, side, 2, units, features), lambda i: (i, 0, 0, 0, 0, 0))
+    return pl.pallas_call(
+        mlp_kernel,
+        grid=(narrow,),
+        in_specs=[
+            whole(*attended.shape),
+            whole(*proj.shape),
+            whole(rows, features),
+            whole(rows, features),
+            whole(1, features),
+            whole(1, features),
+            weights,
+            weights,
+        ],
+        out_specs=(
+            whole(rows, features),
+            whole(rows, features),
+            whole(*attended.shape),
+            whole(*proj.shape),
+            pl.BlockSpec(
+                (1, side, side, 2, 2 * units, features), lambda i: (i, 0, 0, 0, 0, 0)
+            ),
+            whole(8, features),
+        ),
+        out_shape=(
+            jax.ShapeDtypeStruct((rows, features), bf16),
+            jax.ShapeDtypeStruct((rows, features), f32),
+            jax.ShapeDtypeStruct(attended.shape, bf16),
+            jax.ShapeDtypeStruct(proj.shape, bf16),
+            jax.ShapeDtypeStruct((narrow, side, side, 2, 2 * units, features), bf16),
+            jax.ShapeDtypeStruct((8, features), f32),
+        ),
+        scratch_shapes=[
+            pltpu.VMEM((rows, features), f32),
+            pltpu.VMEM((rows, features), bf16),
+            pltpu.VMEM((rows, features), f32),
+            pltpu.VMEM((rows, features), f32),
+        ],
+        compiler_params=pltpu.CompilerParams(vmem_limit_bytes=58 << 20),
+        name="mlp",
+    )(attended, proj, tokens, cotangent, gain, bias, up_all, down_all)
 
 
 def finish_kernel(
@@ -762,129 +978,331 @@
     )(packed, weight, normed, tokens, middle, gain, norm_parts, piece)
 
 
-def product(spec, left, right):
-    return jnp.einsum(spec, left, right, preferred_element_type=f32)
-
-
-def gather_kernel(W,N,own,out,lsem,s1,s1b,r1,s2,r2,s3,r3,fs0,fr0,fs1,fr1,fs2,fr2,fs3,fr3):
-    w=lax.axis_index("wide"); n=lax.axis_index("narrow")
-    W1=math.isqrt(W); H=N//2
-    a=w//W1; b=lax.rem(w,W1); z=n//2; core=lax.rem(n,2); sib=n+1-2*core
-    greet(W,N,w,n)
-    def rc(src,dst,ss,rs,dw,dn):
-        return pltpu.make_async_remote_copy(src_ref=src,dst_ref=dst,send_sem=ss,recv_sem=rs,device_id=(dw,dn),device_id_type=MESH)
-    def arrived(ref,sem):
-        pltpu.make_async_copy(ref,ref,sem).wait()
-    oa=lambda i: lax.rem(a+i,W1)
-    ob=lambda i: lax.rem(b+i,W1)
-    def d1(zs,step):
-        return rc(out.at[2*zs+core,a,b],out.at[2*zs+core,a,b],s1b.at[zs],r1.at[zs],w,n+2*step)
-    def own1(step):
-        return rc(own.at[a,b],out.at[n,a,b],s1.at[z+step],r1.at[z],w,n+2*step)
-    def d2(ns,zs,h,i):
-        if h==0: return rc(out.at[ns,a,b,0],out.at[ns,a,b,0],s2.at[zs,0,i],r2.at[zs,0,b],a*W1+ob(i),n)
-        return rc(out.at[ns,a,b,1],out.at[ns,a,b,1],s2.at[zs,1,i],r2.at[zs,1,a],oa(i)*W1+b,n)
-    def d3(ns,zs,h,i):
-        if h==0: return rc(out.at[ns,a,:,0],out.at[ns,a,:,0],s3.at[zs,0,i],r3.at[zs,0,a],oa(i)*W1+b,n)
-        return rc(out.at[ns,:,b,1],out.at[ns,:,b,1],s3.at[zs,1,i],r3.at[zs,1,b],a*W1+ob(i),n)
-    f0=rc(own,out.at[n],fs0,fr0,w,sib)
-    def f1(ns,zs): return rc(out.at[ns,a,b],out.at[ns,a,b],fs1.at[zs],fr1.at[zs],w,sib)
-    def f2(ns,zs,h,i):
-        v=out.at[ns,a,ob(i),0] if h==0 else out.at[ns,oa(i),b,1]
-        k=ob(i) if h==0 else oa(i)
-        return rc(v,v,fs2.at[zs,h,k],fr2.at[zs,h,k],w,sib)
-    def f3(ns,zs,h,i):
-        v=out.at[ns,oa(i),:,0] if h==0 else out.at[ns,:,ob(i),1]
-        k=oa(i) if h==0 else ob(i)
-        return rc(v,v,fs3.at[zs,h,k],fr3.at[zs,h,k],w,sib)
-    local=pltpu.make_async_copy(own,out.at[n],lsem)
-    up=z<H-1; down=z>0
-    @pl.when(up)
-    def _(): own1(1).start()
-    @pl.when(down)
-    def _(): own1(-1).start()
-    local.start(); f0.start()
-    def sides(d,f):
-        @pl.when(jnp.logical_and(d<=H-1,z-d>=0))
-        def _(): f(z-d,1,up)
-        @pl.when(jnp.logical_and(d<=H-1,z+d<=H-1))
-        def _(): f(z+d,-1,down)
-    def step1(zs,step,more):
-        ns=2*zs+core
-        arrived(out.at[ns,a,b],r1.at[zs])
+class Gather:
+    def __init__(self, wide, narrow, own, out, *semaphores):
+        self.own, self.out = own, out
+        self.w, self.n = lax.axis_index("wide"), lax.axis_index("narrow")
+        self.side, self.lines = math.isqrt(wide), narrow // 2
+        self.a, self.b = self.w // self.side, lax.rem(self.w, self.side)
+        self.z, self.core = self.n // 2, lax.rem(self.n, 2)
+        self.sibling = self.n + 1 - 2 * self.core
+        (
+            self.copied, self.own_sent, self.passed, self.line_got, self.first_sent, self.first_got,
+            self.second_sent, self.second_got, self.f0_sent, self.f0_got, self.f1_sent, self.f1_got,
+            self.f2_sent, self.f2_got, self.f3_sent, self.f3_got,
+        ) = semaphores
+        self.pairs = [(h, i) for i in range(1, self.side) for h in (0, 1)]
+
+    @staticmethod
+    def scratch(wide, narrow):
+        side, lines = math.isqrt(wide), narrow // 2
+        dma = pltpu.SemaphoreType.DMA
+        line, plane = (lines,), (lines, 2, side)
+        shapes = [(), line, line, line, plane, plane, plane, plane, (), (), line, line]
+        return [dma(shape) for shape in shapes + [plane] * 4]
+
+    def other_a(self, i):
+        return lax.rem(self.a + i, self.side)
+
+    def other_b(self, i):
+        return lax.rem(self.b + i, self.side)
+
+    def own_on(self, way):
+        return remote(
+            self.own.at[self.a, self.b], self.out.at[self.n, self.a, self.b],
+            self.own_sent.at[self.z + way], self.line_got.at[self.z], self.w, self.n + 2 * way,
+        )
+
+    def pass_on(self, zs, way):
+        piece = self.out.at[2 * zs + self.core, self.a, self.b]
+        return remote(
+            piece, piece, self.passed.at[zs], self.line_got.at[zs], self.w, self.n + 2 * way
+        )
+
+    def first(self, zs, h, i):
+        shard = 2 * zs + self.core
+        piece = self.out.at[shard, self.a, self.b, h]
+        if h == 0:
+            to, mine = self.a * self.side + self.other_b(i), self.b
+        else:
+            to, mine = self.other_a(i) * self.side + self.b, self.a
+        return remote(
+            piece, piece, self.first_sent.at[zs, h, i], self.first_got.at[zs, h, mine], to, self.n
+        )
+
+    def second(self, zs, h, i):
+        shard = 2 * zs + self.core
+        if h == 0:
+            piece = self.out.at[shard, self.a, :, 0]
+            to, mine = self.other_a(i) * self.side + self.b, self.a
+        else:
+            piece = self.out.at[shard, :, self.b, 1]
+            to, mine = self.a * self.side + self.other_b(i), self.b
+        return remote(
+            piece, piece, self.second_sent.at[zs, h, i], self.second_got.at[zs, h, mine], to, self.n
+        )
+
+    def first_from(self, shard, h, i):
+        if h == 0:
+            return self.out.at[shard, self.a, self.other_b(i), 0], self.other_b(i)
+        return self.out.at[shard, self.other_a(i), self.b, 1], self.other_a(i)
+
+    def second_from(self, shard, h, i):
+        if h == 0:
+            return self.out.at[shard, self.other_a(i), :, 0], self.other_a(i)
+        return self.out.at[shard, :, self.other_b(i), 1], self.other_b(i)
+
+    def hand0(self):
+        return remote(
+            self.own, self.out.at[self.n], self.f0_sent, self.f0_got, self.w, self.sibling
+        )
+
+    def hand1(self, zs):
+        piece = self.out.at[2 * zs + self.core, self.a, self.b]
+        return remote(piece, piece, self.f1_sent.at[zs], self.f1_got.at[zs], self.w, self.sibling)
+
+    def hand2(self, zs, h, i):
+        piece, k = self.first_from(2 * zs + self.core, h, i)
+        return remote(
+            piece, piece, self.f2_sent.at[zs, h, k], self.f2_got.at[zs, h, k], self.w, self.sibling
+        )
+
+    def hand3(self, zs, h, i):
+        piece, k = self.second_from(2 * zs + self.core, h, i)
+        return remote(
+            piece, piece, self.f3_sent.at[zs, h, k], self.f3_got.at[zs, h, k], self.w, self.sibling
+        )
+
+    def keep(self):
+        return pltpu.make_async_copy(self.own, self.out.at[self.n], self.copied)
+
+    def sides(self, d, act):
+        if not 1 <= d <= self.lines - 1:
+            return
+        z, last = self.z, self.lines - 1
+
+        @pl.when(z >= d)
+        def _():
+            act(z - d, 1, z < last)
+
+        @pl.when(z + d <= last)
+        def _():
+            act(z + d, -1, z > 0)
+
+    def begin(self):
+        @pl.when(self.z < self.lines - 1)
+        def _():
+            self.own_on(1).start()
+
+        @pl.when(self.z > 0)
+        def _():
+            self.own_on(-1).start()
+
+        self.keep().start()
+        self.hand0().start()
+
+    def one(self, zs, way, more):
+        arrived(self.out.at[2 * zs + self.core, self.a, self.b], self.line_got.at[zs])
+
         @pl.when(more)
-        def _(): d1(zs,step).start()
-        for i in range(1,W1):
-            d2(ns,zs,0,i).start(); d2(ns,zs,1,i).start()
-        f1(ns,zs).start()
-    def step2(zs,step,more):
-        ns=2*zs+core
-        for i in range(1,W1):
-            arrived(out.at[ns,a,ob(i),0],r2.at[zs,0,ob(i)])
-        for i in range(1,W1): d3(ns,zs,0,i).start()
-        for i in range(1,W1):
-            arrived(out.at[ns,oa(i),b,1],r2.at[zs,1,oa(i)])
-        for i in range(1,W1): d3(ns,zs,1,i).start()
-        for i in range(1,W1):
-            f2(ns,zs,0,i).start(); f2(ns,zs,1,i).start()
-    def step3(zs,step,more):
-        ns=2*zs+core
-        for i in range(1,W1):
-            arrived(out.at[ns,oa(i),:,0],r3.at[zs,0,oa(i)])
-            f3(ns,zs,0,i).start()
-            arrived(out.at[ns,:,ob(i),1],r3.at[zs,1,ob(i)])
-            f3(ns,zs,1,i).start()
-    def run(d,_):
-        sides(d,step1)
-        @pl.when(d>1)
-        def _(): sides(d-1,step2)
-        @pl.when(d>2)
-        def _(): sides(d-2,step3)
-        return 0
-    lax.fori_loop(1,H+2,run,0)
-    local.wait()
-    f0.wait_send(); arrived(out.at[sib],fr0)
-    @pl.when(up)
-    def _(): own1(1).wait_send()
-    @pl.when(down)
-    def _(): own1(-1).wait_send()
-    def finish(zs,step,more):
-        ns=2*zs+core; nb=ns+1-2*core
+        def _():
+            self.pass_on(zs, way).start()
+
+        for h, i in self.pairs:
+            self.first(zs, h, i).start()
+        self.hand1(zs).start()
+
+    def two(self, zs, way, more):
+        for h in (0, 1):
+            for i in range(1, self.side):
+                piece, k = self.first_from(2 * zs + self.core, h, i)
+                arrived(piece, self.first_got.at[zs, h, k])
+            for i in range(1, self.side):
+                self.second(zs, h, i).start()
+        for h, i in self.pairs:
+            self.hand2(zs, h, i).start()
+
+    def three(self, zs, way, more):
+        for h, i in self.pairs:
+            piece, k = self.second_from(2 * zs + self.core, h, i)
+            arrived(piece, self.second_got.at[zs, h, k])
+            self.hand3(zs, h, i).start()
+
+    def round(self, d):
+        self.sides(d, self.one)
+        self.sides(d - 1, self.two)
+        self.sides(d - 2, self.three)
+
+    def finish_side(self, zs, way, more):
+        theirs = 2 * zs + 1 - self.core
+
         @pl.when(more)
-        def _(): d1(zs,step).wait_send()
-        f1(ns,zs).wait_send(); arrived(out.at[nb,a,b],fr1.at[zs])
-        for h in (0,1):
-            for i in range(1,W1):
-                d2(ns,zs,h,i).wait_send(); d3(ns,zs,h,i).wait_send()
-                f2(ns,zs,h,i).wait_send(); f3(ns,zs,h,i).wait_send()
-                v2=out.at[nb,a,ob(i),0] if h==0 else out.at[nb,oa(i),b,1]
-                arrived(v2,fr2.at[zs,h,ob(i) if h==0 else oa(i)])
-                v3=out.at[nb,oa(i),:,0] if h==0 else out.at[nb,:,ob(i),1]
-                arrived(v3,fr3.at[zs,h,oa(i) if h==0 else ob(i)])
-    def fin(d,_):
-        sides(d,finish); return 0
-    lax.fori_loop(1,H,fin,0)
-
-def gather_weights(W,N,own):
-    W1=math.isqrt(W); H=N//2
-    D=pltpu.SemaphoreType.DMA
-    return pl.pallas_call(functools.partial(gather_kernel,W,N),out_shape=jax.ShapeDtypeStruct((N,)+own.shape,bf16),
-      in_specs=[pl.BlockSpec(memory_space=pl.ANY)],out_specs=pl.BlockSpec(memory_space=pl.ANY),
-      scratch_shapes=[D(()),D((H,)),D((H,)),D((H,)),D((H,2,W1)),D((H,2,W1)),D((H,2,W1)),D((H,2,W1)),D(()),D(()),D((H,)),D((H,)),D((H,2,W1)),D((H,2,W1)),D((H,2,W1)),D((H,2,W1))],
-      compiler_params=pltpu.CompilerParams(collective_id=1,has_side_effects=True,vmem_limit_bytes=1<<20),name="gather_weights")(own)
+        def _():
+            self.pass_on(zs, way).wait_send()
+
+        self.hand1(zs).wait_send()
+        arrived(self.out.at[theirs, self.a, self.b], self.f1_got.at[zs])
+        for h, i in self.pairs:
+            self.first(zs, h, i).wait_send()
+            self.second(zs, h, i).wait_send()
+            self.hand2(zs, h, i).wait_send()
+            self.hand3(zs, h, i).wait_send()
+            piece, k = self.first_from(theirs, h, i)
+            arrived(piece, self.f2_got.at[zs, h, k])
+            piece, k = self.second_from(theirs, h, i)
+            arrived(piece, self.f3_got.at[zs, h, k])
+
+    def finish(self):
+        @pl.when(self.z < self.lines - 1)
+        def _():
+            self.own_on(1).wait_send()
+
+        @pl.when(self.z > 0)
+        def _():
+            self.own_on(-1).wait_send()
+
+        self.keep().wait()
+        self.hand0().wait_send()
+        arrived(self.out.at[self.sibling], self.f0_got)
+        for d in range(1, self.lines):
+            self.sides(d, self.finish_side)
+
+
+def start_kernel(
+    wide, narrow, token_ref, gain_ref, bias_ref, weight_ref, own_ref,
+    normed, packed, gathered, line_sent, line_got, sib_sent, sib_got, *gather_refs,
+):
+    gather = Gather(wide, narrow, own_ref, gathered, *gather_refs)
+    w, n, z, core = gather.w, gather.n, gather.z, gather.core
+    lines, sibling = gather.lines, gather.sibling
+    rows = token_ref.shape[0]
+
+    def norm_rows(j, carry):
+        part = pl.ds(pl.multiple_of(j * 64, 64), 64)
+        values = token_ref[part, :].astype(f32)
+        centred = values - jnp.mean(values, axis=-1, keepdims=True)
+        variance = jnp.mean(centred * centred, axis=-1, keepdims=True)
+        normed[n, part, :] = (
+            centred * lax.rsqrt(variance + epsilon) * gain_ref[...] + bias_ref[...]
+        ).astype(bf16)
+        return carry
+
+    lax.fori_loop(0, rows // 64, norm_rows, 0)
+    greet(wide, narrow, w, n)
+
+    def pass_on(zs, way):
+        block = normed.at[2 * zs + core]
+        k = (1 - way) // 2
+        return remote(block, block, line_sent.at[zs, k], line_got.at[zs], w, n + 2 * way)
+
+    def hand(zs):
+        block = normed.at[2 * zs + core]
+        return remote(block, block, sib_sent.at[zs], sib_got.at[zs], w, sibling)
+
+    def project(owner):
+        columns = pl.ds(pl.multiple_of(owner * rows, rows), rows)
+        packed[:, columns] = contract(weight_ref[...], normed[owner], 1, 1).astype(bf16)
+
+    @pl.when(z < lines - 1)
+    def _():
+        pass_on(z, 1).start()
+
+    @pl.when(z > 0)
+    def _():
+        pass_on(z, -1).start()
+
+    hand(z).start()
+    project(n)
+
+    def receive(zs, way, more):
+        arrived(normed.at[2 * zs + core], line_got.at[zs])
+
+        @pl.when(more)
+        def _():
+            pass_on(zs, way).start()
+
+        hand(zs).start()
+
+    def project_side(zs, way, more):
+        project(2 * zs + core)
+
+    def project_sibling(zs, way, more):
+        arrived(normed.at[2 * zs + 1 - core], sib_got.at[zs])
+        project(2 * zs + 1 - core)
+
+    for d in range(1, lines):
+        gather.sides(d, receive)
+        if d == 1:
+            gather.begin()
+            project_sibling(z, 0, None)
+        else:
+            gather.round(d - 1)
+            gather.sides(d - 1, project_sibling)
+        gather.sides(d, project_side)
+    gather.round(lines - 1)
+    gather.sides(lines - 1, project_sibling)
+    gather.round(lines)
+    gather.round(lines + 1)
+    gather.finish()
+
+    def sent_side(zs, way, more):
+        hand(zs).wait_send()
+
+        @pl.when(more)
+        def _():
+            pass_on(zs, way).wait_send()
+
+    @pl.when(z < lines - 1)
+    def _():
+        pass_on(z, 1).wait_send()
+
+    @pl.when(z > 0)
+    def _():
+        pass_on(z, -1).wait_send()
+
+    hand(z).wait_send()
+    for d in range(1, lines):
+        gather.sides(d, sent_side)
+
+
+def start(wide, narrow, tokens, gain, bias, weight, own):
+    rows, features = tokens.shape
+    lines = narrow // 2
+    dma = pltpu.SemaphoreType.DMA
+    vmem = pl.BlockSpec(memory_space=pltpu.VMEM)
+    anywhere = pl.BlockSpec(memory_space=pl.ANY)
+    return pl.pallas_call(
+        functools.partial(start_kernel, wide, narrow),
+        in_specs=[vmem, vmem, vmem, vmem, anywhere],
+        out_specs=(vmem, vmem, anywhere),
+        out_shape=(
+            jax.ShapeDtypeStruct((narrow, rows, features), bf16),
+            jax.ShapeDtypeStruct((weight.shape[0], narrow * rows), bf16),
+            jax.ShapeDtypeStruct((narrow, *own.shape), bf16),
+        ),
+        scratch_shapes=[
+            dma((lines, 2)), dma((lines,)), dma((lines,)), dma((lines,)),
+            *Gather.scratch(wide, narrow),
+        ],
+        compiler_params=pltpu.CompilerParams(
+            vmem_limit_bytes=58 << 20, collective_id=1, has_side_effects=True
+        ),
+        name="start",
+    )(tokens, gain, bias, weight, own)
+
 
 def body(
     tokens, cotangent, item_lengths, attn_gain, attn_bias, qkv_weight, proj_weight,
     mlp_gain, mlp_bias, up_weight, down_weight,
 ):
     items = item_lengths.shape[1]
-    token_rows = tokens.astype(f32)
     heads = qkv_weight.shape[1] // (3 * HEAD_DIM)
     gain_one, bias_one = attn_gain.astype(f32), attn_bias.astype(f32)
     gain_two, bias_two = mlp_gain.astype(f32), mlp_bias.astype(f32)
     wide, narrow = lax.axis_size("wide"), lax.axis_size("narrow")
+    side = math.isqrt(wide)
+    rows = narrow * tokens.shape[0]
     qkv_turned = qkv_weight.T
-    side = math.isqrt(wide)
 
     def cut(shard):
         return shard.reshape(side, side, 2, shard.shape[0] // (2 * wide), shard.shape[1])
@@ -892,59 +1310,32 @@
     def split_parts(total):
         return total.reshape(narrow, side, side, 2, -1, total.shape[1])
 
-    shards = [cut(up_weight.T), cut(down_weight), cut(proj_weight)]
-    everything = gather_weights(wide, narrow, jnp.concatenate(shards, axis=3))
-    first = shards[0].shape[3]
-    features = tokens.shape[1]
-    normed = norm_forward(token_rows, gain_one, bias_one).astype(bf16)
-    normed_all = lax.all_gather(normed, "narrow", axis=0, tiled=True)
-    normed_all, everything = lax.optimization_barrier((normed_all, everything))
-    rows = normed_all.shape[0]
+    own_up, own_rest = cut(up_weight.T), jnp.concatenate([cut(down_weight), cut(proj_weight)], axis=3)
+    first = own_up.shape[3]
     query_extra, key_extra = mask_rows(item_lengths, rows)
-    packed = (
-        product("rd,cd->cr", normed_all, qkv_turned).astype(bf16).reshape(heads, 3, HEAD_DIM, rows)
+    normed_all, packed, up_all = start(
+        wide, narrow, tokens, gain_one.reshape(1, -1), bias_one.reshape(1, -1), qkv_turned, own_up
     )
-    attended, log_total = attend_forward(packed, query_extra, key_extra)
-    up_all = everything[:, :, :, :, :first].reshape(-1, tokens.shape[1])
-    down_all = everything[:, :, :, :, first : 2 * first].reshape(-1, tokens.shape[1])
-    proj_all = everything[:, :, :, :, 2 * first :].reshape(-1, tokens.shape[1])
-    attended_rows = lax.all_to_all(
-        attended.reshape(heads * HEAD_DIM, rows), "narrow", split_axis=1, concat_axis=0, tiled=True
+    normed_all = normed_all.reshape(rows, -1)
+    packed = packed.reshape(heads, 3, HEAD_DIM, rows)
+    attended, log_total, attended_rows, rest_all = attend_forward(
+        wide, narrow, packed, query_extra, key_extra, own_rest
     )
-    branch = product("ar,ad->rd", attended_rows, proj_all)
-    middle = token_rows + branch
-    expand_in = norm_forward(middle, gain_two, bias_two).astype(bf16)
-    hidden_pre = product("rd,fd->rf", expand_in, up_all)
-    hidden = gelu_exact(hidden_pre).astype(bf16)
-    output = (middle + product("rf,fd->rd", hidden, down_all)).astype(bf16)
-
-    grad_hidden = product("rd,fd->rf", cotangent, down_all)
-    grad_pre = jax.vjp(gelu_exact, hidden_pre)[1](grad_hidden)[0].astype(bf16)
-    grad_expand = product("rf,fd->rd", grad_pre, up_all)
-    grad_middle_norm, grad_gain_two, grad_bias_two = jax.vjp(
-        norm_forward, middle, gain_two, bias_two
-    )[1](grad_expand)
-    grad_middle = cotangent.astype(f32) + grad_middle_norm
-    grad_branch = grad_middle.astype(bf16)
+    attended_rows = attended_rows.reshape(-1, tokens.shape[0])
+    proj_all = rest_all[:, :, :, :, first:].reshape(-1, tokens.shape[1])
+    output, grad_middle, grad_attended, grad_proj, grad_parts, norm_parts = mlp(
+        attended_rows, proj_all, tokens, cotangent, gain_two.reshape(1, -1),
+        bias_two.reshape(1, -1), up_all, rest_all, first,
+    )
     grad_attended = lax.all_to_all(
-        product("rd,ad->ar", grad_branch, proj_all).astype(bf16),
-        "narrow", split_axis=0, concat_axis=1, tiled=True,
+        grad_attended, "narrow", split_axis=0, concat_axis=1, tiled=True
     ).reshape(heads, HEAD_DIM, rows)
-    grad_parts = jnp.concatenate(
-        [
-            split_parts(product("rf,rd->fd", grad_pre, expand_in).astype(bf16)),
-            split_parts(product("rf,rd->fd", hidden, cotangent).astype(bf16)),
-            split_parts(product("ar,rd->ad", attended_rows, grad_branch).astype(bf16)),
-        ],
-        axis=4,
-    )
+    grad_proj_parts = split_parts(grad_proj)
     grad_packed, grad_piece = attend_backward(
         wide, narrow, packed, query_extra, key_extra, attended, grad_attended, log_total,
-        grad_parts, items,
+        grad_parts, grad_proj_parts, items,
     )
     grad_packed = grad_packed.reshape(heads * 3 * HEAD_DIM, rows)
-    norm_parts = jnp.zeros((8, tokens.shape[1]), f32)
-    norm_parts = norm_parts.at[2].set(grad_gain_two).at[3].set(grad_bias_two)
     grad_tokens, grad_qkv, grad_shard, norm_sums = finish(
         wide, narrow, grad_packed, qkv_turned, normed_all, tokens, grad_middle,
         gain_one.reshape(1, -1), norm_parts, grad_piece,

time: 622 us -> 514 us (0.83); the launches traced: 612 us -> 514 us
  matrix products: 89.6 us -> 0 us
  Pallas kernels: 419 us -> 453 us
  local copies, waits for them, and re-layouts: 43.4 us -> 19.7 us
  other arithmetic: 28.4 us -> 6.17 us
  waiting for transfers between devices: 9.81 us -> 26.6 us
  between operations: 14.9 us -> 0.78 us
    dot_general x10 -> x0, matrix products: 89.6 us -> none  [product(): return jnp.einsum(spec, left, right, preferred_element_type=f32)]
    pallas_call x2 -> x3, Pallas kernels: 197 us -> 233 us  [the longest x1 123 us: start(): pl.pallas_call(functools.partial(start_kernel, wide, narrow), in_specs=[v...]
    concatenate x2 -> x1, other arithmetic: 18.1 us -> 1.21 us  [body(): jnp.concatenate([cut(down_weight), cut(proj_weight)], axis=3)]
    all_to_all x2 -> x1, waiting for transfers between devices: 9.77 us -> 26.6 us  [body(): lax.all_to_all(grad_attended, 'narrow', split_axis=0, concat_axis=1, tile...]
    slice x2 -> x1, local copies, waits for them, and re-layouts: 15.5 us -> 3.24 us  [body(): proj_all = rest_all[:, :, :, :, first:].reshape(-1, tokens.shape[1])]
    unnamed x56 -> x21, local copies, waits for them, and re-layouts: 14.6 us -> 5.1 us
  transfers between devices with their start and end apart: 3 -> 1, of which waited for: 1 -> 1; matrix products, arithmetic and copies ran while one was open for 9% -> 0% of each run, Pallas kernels for 24% -> 0%
where the time goes in v4:
time: 514 us
  Pallas kernels  453 us (88%)
  waiting for transfers between devices  26.6 us (5%)
  local copies, waits for them, and re-layouts  19.7 us (4%)
  starting transfers between devices  7.34 us (1%)
  other arithmetic  6.17 us (1%)
    pallas_call x1, Pallas kernels, start(): pl.pallas_call(functools.partial(start_kernel, wide, narrow), in_specs=[v...  123 us
    pallas_call x1, Pallas kernels, attend_backward(): pl.pallas_call(functools.partial(backward_kernel, block, rows, items, wid...  113 us
    pallas_call x1, Pallas kernels, finish(): pl.pallas_call(functools.partial(finish_kernel, wide, narrow, chunks), in...  107 us
    pallas_call x1, Pallas kernels, attend_forward(): pl.pallas_call(functools.partial(forward_kernel, wide, narrow), grid=(hea...  67.3 us
    pallas_call x1, Pallas kernels, mlp(): pl.pallas_call(mlp_kernel, grid=(narrow,), in_specs=[whole(*attended.shap...  42.9 us
    all_to_all x1, waiting for transfers between devices, body(): lax.all_to_all(grad_attended, 'narrow', split_axis=0, concat_axis=1, tile...  26.6 us
  transfers between devices with their start and end apart: 1, of which 1 were waited for; matrix products, arithmetic and copies ran while one was open for 0% of the time, Pallas kernels for 0%

profile of v4, /device:TPU:0, one launch (start us, length us, event | category | flops | bytes accessed | tf_op | source)
XLA Modules:
  0.0 513.9 jit_solution(16122238206852941602)
XLA Ops:
  0.6 0.0 copy-start
  0.7 0.0 copy-start.5
  0.7 0.0 copy-start.8
  0.7 0.0 copy-start.1
  0.7 0.0 copy-start.4
  0.7 2.5 copy.31
  3.2 1.3 reshape.119
  4.5 0.0 copy-done
  4.5 1.3 copy.32
  5.8 0.0 copy-done.5
  5.8 0.6 reshape.121
  6.4 0.0 copy-done.8
  6.4 0.1 select_reduce_fusion
  6.5 0.1 convert_reduce_fusion
  6.6 0.8 select_convert_fusion.1.qx_ref
  7.4 0.7 select_convert_fusion.kx_ref
  8.1 0.0 copy-done.1
  8.1 0.0 copy-done.4
  8.1 1.2 pad_maximum_fusion.own_ref
  9.3 122.6 %start.1 = (bf16[8,512,1024]{2,1,0:T(8,128)(2,1)}, bf16[384,4096]{1,0:T(8,128)(2,1)}, bf16[8,2,2,2,64,1024]{5,4,3,2,1,0:T(8,128)(2,1)}) custom-call(bf16[512,1024]{1,0:T(8,128)(2,1)} %token_ref.5, f32[1,1024]{1,0:T(1,128)} %bitcast.54, f32[1,1024]{1,0:T(1,128)} %bitcast.56, bf16[384,1024]{1,0:T(8,128)(2,1)} %bitcast.41, bf16[2,2,2,64,1024]{4,3,2,1,0:T(8,128)(2,1)} %bitcast.44), custom_call_target="tpu_custom_call" | custom-call | tf_op jit(solution)/shard_map/start/pallas_call | solution.py:1274
  131.9 67.3 %attend_forward.1 = (bf16[2,64,4096]{2,1,0:T(8,128)(2,1)}, f32[2,1,4096]{2,1,0:T(1,128)}, bf16[8,2,64,512]{3,2,1,0:T(8,128)(2,1)}, bf16[8,2,2,2,80,1024]{5,4,3,2,1,0:T(8,128)(2,1)}) custom-call(bf16[16,4096]{1,0:T(8,128)(2,1)} %select_convert_fusion.1.qx_ref, bf16[16,4096]{1,0:T(8,128)(2,1)} %select_convert_fusion.kx_ref, bf16[2,3,64,4096]{3,2,1,0:T(8,128)(2,1)} %bitcast.32, ...), custom_call_target="tpu_custom_call" | custom-call | tf_op jit(solution)/shard_map/attend_forward/pallas_call | solution.py:128
  199.2 0.0 copy-start.6
  199.2 0.0 copy-start.7
  199.3 3.2 slice.24
  202.5 0.0 copy-done.6
  202.5 0.6 reshape.123
  203.1 0.0 copy-done.7
  203.1 0.6 reshape.125
  203.7 42.9 %mlp.1 = (bf16[512,1024]{1,0:T(8,128)(2,1)}, f32[512,1024]{1,0:T(8,128)}, bf16[1024,512]{1,0:T(8,128)(2,1)}, bf16[1024,1024]{1,0:T(8,128)(2,1)}, bf16[8,2,2,2,12...) custom-call(bf16[1024,512]{1,0:T(8,128)(2,1)} %bitcast.48, bf16[1024,1024]{1,0:T(8,128)(2,1)} %bitcast.40, ...), custom_call_target="tpu_custom_call" | custom-call | tf_op jit(solution)/shard_map/mlp/pallas_call | solution.py:614
  246.6 7.3 %all-to-all-start = ((bf16[8,128,512]{2,1,0:T(8,128)(2,1)}), bf16[8,128,512]{2,1,0:T(8,128)(2,1)S(1)}, u32[]{:S(2)}, u32[]{:S(2)}) async-start(bf16[8,128,512]{2,1,0:T(8,128)(2,1)} %bitcast.51), calls=%async_computation | async-start | bytes 2097152 | tf_op jit(solution)/shard_map/all_to_all | solution.py:1330
  254.0 26.6 %all-to-all-done = bf16[8,128,512]{2,1,0:T(8,128)(2,1)S(1)} async-done(((bf16[8,128,512]{2,1,0:T(8,128)(2,1)}), bf16[8,128,512]{2,1,0:T(8,128)(2,1)S(1)}, u32[]{:S(2)}, u32[]{:S(2)}) %all-to-all-start) | async-done | bytes 1048608 | tf_op jit(solution)/shard_map/all_to_all | solution.py:1330
  280.6 0.6 copy.33
  281.1 1.3 reshape.112.do_ref
  282.4 113.2 %attend_backward.1 = (bf16[2,3,64,4096]{3,2,1,0:T(8,128)(2,1)}, bf16[2,144,1024]{2,1,0:T(8,128)(2,1)}) custom-call(bf16[16,4096]{1,0:T(8,128)(2,1)} %select_convert_fusion.1.qx_ref, bf16[16,4096]{1,0:T(8,128)(2,1)} %select_convert_fusion.kx_ref, bf16[2,3,64,4096]{3,2,1,0:T(8,128)(2,1)} %bitcast.35, bf16[2,3,64,4096]{3,2,1,0:T(8,128)(2,1)} %bitcast.36, ...), custom_call_target="tpu_custom_call" | custom-call | flops 85899345920 | bytes 8388608 | tf_op jit(solution)/shard_map/attend_backward/pallas_call | solution.py:464
  395.6 107.3 %finish.1 = (bf16[512,1024]{1,0:T(8,128)(2,1)}, bf16[384,1024]{1,0:T(8,128)(2,1)}, bf16[4,2,144,1024]{3,2,1,0:T(8,128)(2,1)}, f32[8,1024]{1,0:T(8,128)}) custom-call(bf16[384,4096]{1,0:T(8,128)(2,1)} %bitcast.45, bf16[384,1024]{1,0:T(8,128)(2,1)} %bitcast.42, bf16[4096,1024]{1,0:T(8,128)(2,1)} %bitcast.38, bf16[512,1024]{1,0:T(8,128)(2,1)} %token_ref.5, ...), custom_call_target="tpu_custom_call" | custom-call | tf_op jit(solution)/shard_map/finish/pallas_call | solution.py:932
  503.0 3.3 fusion.1
  506.3 1.8 slice.32
  508.1 0.0 copy-start.3
  508.1 1.8 copy.34
  509.9 0.0 copy-done.3
  509.9 0.2 convert_bitcast_fusion
  510.1 0.0 copy-start.2
  510.1 1.6 copy.35
  511.7 0.7 constant_dynamic-slice_fusion
  512.4 0.5 slice_bitcast_fusion
  512.9 0.0 copy-done.2
  512.9 1.0 copy.37
  (2 shorter events, 0.0 us)
Async XLA Ops:
  0.6 3.8 copy-start
  0.7 5.1 copy-start.5
  0.7 5.7 %copy-start.8 = (s32[1,4]{1,0:T(1,128)S(1)}, s32[1,4]{1,0:T(1,128)}, u32[]{:S(2)}) copy-start(s32[1,4]{1,0:T(1,128)} %param.13) | copy-start | bytes 52
  0.7 7.4 %copy-start.1 = (bf16[512,1024]{1,0:T(8,128)(2,1)S(1)}, bf16[512,1024]{1,0:T(8,128)(2,1)}, u32[]{:S(2)}) copy-start(bf16[512,1024]{1,0:T(8,128)(2,1)} %param.21) | copy-start | bytes 3145732
  0.7 7.4 %copy-start.4 = (bf16[128,1024]{1,0:T(8,128)(2,1)S(1)}, bf16[128,1024]{1,0:T(8,128)(2,1)}, u32[]{:S(2)}) copy-start(bf16[128,1024]{1,0:T(8,128)(2,1)} %param.17) | copy-start | bytes 786436
  199.2 3.3 copy-start.6
  199.2 3.9 copy-start.7
  246.6 33.9 %all-to-all-start = ((bf16[8,128,512]{2,1,0:T(8,128)(2,1)}), bf16[8,128,512]{2,1,0:T(8,128)(2,1)S(1)}, u32[]{:S(2)}, u32[]{:S(2)}) async-start(bf16[8,128,512]{2,1,0:T(8,128)(2,1)} %bitcast.51), calls=%async_computation | async-start | bytes 2097152 | tf_op jit(solution)/shard_map/all_to_all | solution.py:1330
  508.1 1.8 copy-start.3
  510.1 2.8 copy-start.2

commit v5 on v4

--- a/solution.py
+++ b/solution.py
@@ -10,7 +10,7 @@
 
 HEAD_DIM = 64
 EXTRA = 16
-ATTENTION_STEPS = 16
+CHUNKS = 2
 EXCLUDED = -1e30
 bf16 = jnp.bfloat16
 f32 = jnp.float32
@@ -21,25 +21,24 @@
 def mask_rows(item_lengths, rows):
     lengths = item_lengths[0]
     items = lengths.shape[0]
-    index = jnp.arange(items)
-    ends = jnp.sum(jnp.where(index[:, None] >= index[None, :], lengths[None, :], 0), axis=1)
-    segment = jnp.sum((jnp.arange(rows)[None, :] >= ends[:, None]).astype(jnp.int32), axis=0)
+    ends = [sum(lengths[j] for j in range(i + 1)) for i in range(items)]
+    position = jnp.arange(rows)
+    segment = sum((position >= ends[i]).astype(jnp.int32) for i in range(items))
     extra = jnp.arange(EXTRA)[:, None]
     own = segment[None, :] == extra
-    query_extra = jnp.where(own & (extra <= items), 1.0, 0.0).astype(bf16)
+    mask = extra <= items
+    query_extra = jnp.where(own & mask, 1.0, 0.0)
     key_extra = jnp.where(
-        extra <= items,
-        jnp.where(own, 0.0, EXCLUDED),
-        jnp.where(extra <= items + 3, 1.0, 0.0),
-    ).astype(bf16)
-    return query_extra, key_extra
+        mask, jnp.where(own, 0.0, EXCLUDED), jnp.where(extra <= items + 3, 1.0, 0.0)
+    )
+    return jnp.where(jnp.arange(2)[:, None, None] == 0, query_extra, key_extra).astype(bf16)
 
 
 def forward_kernel(
-    wide, narrow, qx_ref, kx_ref, q_ref, k_ref, v_ref, own_ref, o_ref, log_ref, rows_ref, gathered,
+    wide, narrow, qx_ref, kx_ref, q_ref, k_ref, v_ref, own_ref, more_ref, o_ref, log_ref, rows_ref, gathered,
     keys, ready, copied, sent, got, *gather_refs,
 ):
-    gather = Gather(wide, narrow, own_ref, gathered, *gather_refs)
+    gather = Gather(wide, narrow, [own_ref, more_ref], gathered, *gather_refs)
     w, n, lines = gather.w, gather.n, gather.lines
     head, step = pl.program_id(0), pl.program_id(1)
     moment = head * narrow + step
@@ -115,20 +114,23 @@
     return ready.shape[0] // narrow
 
 
-def attend_forward(wide, narrow, packed, query_extra, key_extra, own):
+def attend_forward(wide, narrow, packed, extras, own, more):
     heads, _, _, rows = packed.shape
     width = rows // narrow
+    gathered = (narrow, *own.shape[:3], own.shape[3] + more.shape[3], own.shape[4])
     dma = pltpu.SemaphoreType.DMA
 
     def whole(j):
         return pl.BlockSpec((1, None, HEAD_DIM, rows), lambda h, i: (h, j, 0, 0))
 
-    extra = pl.BlockSpec((EXTRA, rows), lambda h, i: (0, 0))
+    def extra(j):
+        return pl.BlockSpec((None, EXTRA, rows), lambda h, i: (j, 0, 0))
+
     anywhere = pl.BlockSpec(memory_space=pl.ANY)
     return pl.pallas_call(
         functools.partial(forward_kernel, wide, narrow),
         grid=(heads, narrow),
-        in_specs=[extra, extra, whole(0), whole(1), whole(2), anywhere],
+        in_specs=[extra(0), extra(1), whole(0), whole(1), whole(2), anywhere, anywhere],
         out_specs=(
             pl.BlockSpec((1, HEAD_DIM, rows), lambda h, i: (h, 0, 0)),
             pl.BlockSpec((1, 1, rows), lambda h, i: (h, 0, 0)),
@@ -139,7 +141,7 @@
             jax.ShapeDtypeStruct((heads, HEAD_DIM, rows), bf16),
             jax.ShapeDtypeStruct((heads, 1, rows), f32),
             jax.ShapeDtypeStruct((narrow, heads, HEAD_DIM, width), bf16),
-            jax.ShapeDtypeStruct((narrow, *own.shape), bf16),
+            jax.ShapeDtypeStruct(gathered, bf16),
         ),
         scratch_shapes=[
             pltpu.VMEM((rows, HEAD_DIM + EXTRA), bf16),
@@ -147,13 +149,13 @@
             dma((heads,)),
             dma((heads * narrow,)),
             dma((narrow, heads)),
-            *Gather.scratch(wide, narrow),
+            *Gather.scratch(wide, narrow, gathered[4:]),
         ],
         compiler_params=pltpu.CompilerParams(
             vmem_limit_bytes=58 << 20, collective_id=4, has_side_effects=True
         ),
         name="attend_forward",
-    )(query_extra, key_extra, packed, packed, packed, own)
+    )(extras, extras, packed, packed, packed, own, more)
 
 
 def remote(src, dst, sent, received, wide_to, narrow_to):
@@ -276,7 +278,6 @@
     halves = [(h, i) for i in range(1, side) for h in (0, 1)]
 
     def begin():
-        greet(wide, narrow, w, n)
         for zs in order:
             for copy in to_sibling(zs) + load(zs):
                 copy.start()
@@ -376,15 +377,30 @@
 
 
 def backward_kernel(
-    block, rows, items, wide, narrow, qx_ref, kx_ref, q_ref, k_ref, v_ref, o_ref, do_ref, log_ref,
-    parts_ref, proj_parts_ref, grad_ref, final_ref, keys, values, grad_k, grad_v, *reduce_refs,
+    block, rows, items, wide, narrow, qx_ref, kx_ref, q_ref, k_ref, v_ref, o_ref, log_ref, own_ref,
+    parts_ref, proj_parts_ref, grad_ref, final_ref, keys, values, grad_k, grad_v,
+    theirs, own_copied, sent, got, *reduce_refs,
 ):
-    width = q_ref.shape[-1]
-    step = pl.program_id(1)
-    steps_per_head = pl.num_programs(1)
-    moment = pl.program_id(0) * steps_per_head + step
-    ticks = ATTENTION_STEPS
+    width = rows // narrow
+    head, step = pl.program_id(0), pl.program_id(1)
+    moment = head * narrow + step
+    ticks = own_ref.shape[1] * narrow
     moves, times = reduce_steps(wide, narrow, parts_ref, proj_parts_ref, final_ref, *reduce_refs)
+    w, n = lax.axis_index("wide"), lax.axis_index("narrow")
+
+    def keep():
+        return pltpu.make_async_copy(own_ref.at[n], theirs.at[n], own_copied)
+
+    def deliver(t):
+        to = lax.rem(n + t, narrow)
+        return remote(own_ref.at[to], theirs.at[n], sent.at[t], got.at[n], w, to)
+
+    @pl.when(moment == 0)
+    def _():
+        greet(wide, narrow, w, n)
+        keep().start()
+        for t in range(1, narrow):
+            deliver(t).start()
 
     def perform(lower, upper):
         for move, time in zip(moves, times):
@@ -414,11 +430,23 @@
             row == 1, high, jnp.where(row == 2, middle, jnp.where(row == 3, small, base))
         ).astype(bf16)
 
-    query = q_ref[0] * jnp.asarray(0.125, bf16)
-    grad = do_ref[0]
-    inner = jnp.sum(grad.astype(f32) * o_ref[0].astype(f32), axis=0, keepdims=True)
+    owner = lax.rem(n + narrow - step, narrow)
+    columns = pl.ds(pl.multiple_of(owner * width, width), width)
+
+    @pl.when(moment == 0)
+    def _():
+        keep().wait()
+
+    @pl.when(jnp.logical_and(moment > 0, head == 0))
+    def _():
+        arrived(theirs.at[owner], got.at[owner])
+
+    query = q_ref[0, :, columns] * jnp.asarray(0.125, bf16)
+    grad = theirs[owner, head]
+    attended = o_ref[0, :, columns].astype(f32)
+    inner = jnp.sum(grad.astype(f32) * attended, axis=0, keepdims=True)
     query_wide = jnp.concatenate(
-        [query, pieces(-log_ref[0], qx_ref[...].astype(f32))], axis=0
+        [query, pieces(-log_ref[0, :, columns], qx_ref[:, columns].astype(f32))], axis=0
     ).T
     grad_wide = jnp.concatenate(
         [grad, pieces(-inner, jnp.zeros((EXTRA, width), f32))], axis=0
@@ -435,11 +463,9 @@
         grad_q += lax.dot_general(
             k_ref[0, :, part], grad_scores, (((1,), (1,)), ((), ())), preferred_element_type=f32
         )
-    grad_ref[0, 0, :, pl.ds(pl.multiple_of(step * width, width), width)] = (
-        grad_q * 0.125
-    ).astype(bf16)
-
-    @pl.when(step == steps_per_head - 1)
+    grad_ref[0, 0, :, columns] = (grad_q * 0.125).astype(bf16)
+
+    @pl.when(step == narrow - 1)
     def _():
         grad_ref[0, 1] = grad_k[...].astype(bf16)
         grad_ref[0, 2] = grad_v[...].astype(bf16)
@@ -447,34 +473,39 @@
     @pl.when(moment == ticks - 1)
     def _():
         perform(ticks, 1000)
+        for t in range(1, narrow):
+            deliver(t).wait_send()
 
 
 def attend_backward(
-    wide, narrow, packed, query_extra, key_extra, attended, grad, log_total, parts,
+    wide, narrow, packed, extras, attended, grad, log_total, parts,
     proj_parts, items, block=512,
 ):
     heads, _, _, rows = packed.shape
-    width = heads * rows // ATTENTION_STEPS
     piece = (parts.shape[4] + proj_parts.shape[4], parts.shape[5])
+    dma = pltpu.SemaphoreType.DMA
 
     def whole(j):
         return pl.BlockSpec((1, None, HEAD_DIM, rows), lambda h, i: (h, j, 0, 0))
 
-    part = pl.BlockSpec((1, HEAD_DIM, width), lambda h, i: (h, 0, i))
+    def extra(j):
+        return pl.BlockSpec((None, EXTRA, rows), lambda h, i: (j, 0, 0))
+
+    anywhere = pl.BlockSpec(memory_space=pl.ANY)
     return pl.pallas_call(
         functools.partial(backward_kernel, block, rows, items, wide, narrow),
-        grid=(heads, rows // width),
+        grid=(heads, narrow),
         in_specs=[
-            pl.BlockSpec((EXTRA, width), lambda h, i: (0, i)),
-            pl.BlockSpec((EXTRA, rows), lambda h, i: (0, 0)),
-            pl.BlockSpec((1, None, HEAD_DIM, width), lambda h, i: (h, 0, 0, i)),
+            extra(0),
+            extra(1),
+            whole(0),
             whole(1),
             whole(2),
-            part,
-            part,
-            pl.BlockSpec((1, 1, width), lambda h, i: (h, 0, i)),
-            pl.BlockSpec(memory_space=pl.ANY),
-            pl.BlockSpec(memory_space=pl.ANY),
+            pl.BlockSpec((1, HEAD_DIM, rows), lambda h, i: (h, 0, 0)),
+            pl.BlockSpec((1, 1, rows), lambda h, i: (h, 0, 0)),
+            anywhere,
+            anywhere,
+            anywhere,
         ],
         out_specs=(
             pl.BlockSpec((1, 3, HEAD_DIM, rows), lambda h, i: (h, 0, 0, 0)),
@@ -489,6 +520,10 @@
             pltpu.VMEM((HEAD_DIM + EXTRA, rows), bf16),
             pltpu.VMEM((HEAD_DIM, rows), f32),
             pltpu.VMEM((HEAD_DIM, rows), f32),
+            pltpu.VMEM(grad.shape, bf16),
+            dma(()),
+            dma((narrow,)),
+            dma((narrow,)),
             *reduce_scratch(wide, narrow, *piece),
         ],
         compiler_params=pltpu.CompilerParams(
@@ -500,7 +535,11 @@
             transcendentals=heads * rows * rows,
         ),
         name="attend_backward",
-    )(query_extra, key_extra, packed, packed, packed, attended, grad, log_total, parts, proj_parts)
+    )(extras, extras, packed, packed, packed, attended, log_total, grad, parts, proj_parts)
+
+
+def as_row(ref):
+    return ref[...].astype(f32).reshape(1, -1)
 
 
 def contract(left, right, left_axis, right_axis):
@@ -541,7 +580,7 @@
             centred = values - jnp.mean(values, axis=-1, keepdims=True)
             variance = jnp.mean(centred * centred, axis=-1, keepdims=True)
             expand[part, :] = (
-                centred * lax.rsqrt(variance + epsilon) * gain_ref[...] + bias_ref[...]
+                centred * lax.rsqrt(variance + epsilon) * as_row(gain_ref) + as_row(bias_ref)
             ).astype(bf16)
             return carry
 
@@ -549,24 +588,32 @@
 
     def flat(ref):
         if ref.shape[4] % 16:
-            return ref[0].astype(f32).reshape(-1, features).astype(bf16)
-        return ref[0].reshape(-1, features)
+            return ref[0].astype(f32).reshape(-1, ref.shape[5]).astype(bf16)
+        return ref[0].reshape(-1, ref.shape[5])
 
     up, down = flat(up_ref), flat(down_ref)
-    units = up_ref.shape[4]
+    units = down_ref.shape[4]
     pieces = up_ref.shape[1:4]
+    columns = up_ref.shape[5]
     hidden_parts, grad_parts = [], []
     for part in (pl.ds(0, rows // 2), pl.ds(rows // 2, rows // 2)):
-        hidden, slope = gelu_pair(contract(expand[part, :], up, 1, 1))
+        hidden, slope = gelu_pair(
+            jnp.dot(expand[part, :], up, preferred_element_type=f32)
+        )
         grad_pre = (contract(cot_ref[part, :], down, 1, 1) * slope).astype(bf16)
         hidden = hidden.astype(bf16)
         out_total[part, :] += jnp.dot(hidden, down, preferred_element_type=f32)
-        expand_total[part, :] += jnp.dot(grad_pre, up, preferred_element_type=f32)
+        expand_total[part, :] += contract(grad_pre, up, 1, 1)
         hidden_parts.append(hidden)
         grad_parts.append(grad_pre)
-    grad_up = contract(jnp.concatenate(grad_parts, axis=0), expand[...], 0, 0)
+    grad_up = contract(expand[...], jnp.concatenate(grad_parts, axis=0), 0, 0)
     grad_down = contract(jnp.concatenate(hidden_parts, axis=0), cot_ref[...], 0, 0)
-    parts_ref[0, :, :, :, 0:units, :] = grad_up.reshape(*pieces, units, features).astype(bf16)
+    groups = features // columns
+    grad_up = grad_up.reshape(*pieces, groups, units, columns)
+    for g in range(groups):
+        parts_ref[0, :, :, :, 0:units, g * columns : (g + 1) * columns] = grad_up[
+            :, :, :, g
+        ].astype(bf16)
     parts_ref[0, :, :, :, units : 2 * units, :] = grad_down.reshape(
         *pieces, units, features
     ).astype(bf16)
@@ -581,7 +628,7 @@
             inverse = lax.rsqrt(jnp.mean(centred * centred, axis=-1, keepdims=True) + epsilon)
             scaled = centred * inverse
             grad = expand_total[part, :]
-            term = grad * gain_ref[...]
+            term = grad * as_row(gain_ref)
             back = inverse * (
                 term
                 - jnp.mean(term, axis=-1, keepdims=True)
@@ -610,7 +657,9 @@
     def whole(*shape):
         return pl.BlockSpec(shape, lambda i: (0,) * len(shape))
 
-    weights = pl.BlockSpec((1, side, side, 2, units, features), lambda i: (i, 0, 0, 0, 0, 0))
+    def weights(*piece):
+        return pl.BlockSpec((1, side, side, 2, *piece), lambda i: (i, 0, 0, 0, 0, 0))
+
     return pl.pallas_call(
         mlp_kernel,
         grid=(narrow,),
@@ -619,10 +668,10 @@
             whole(*proj.shape),
             whole(rows, features),
             whole(rows, features),
-            whole(1, features),
-            whole(1, features),
-            weights,
-            weights,
+            whole(*gain.shape),
+            whole(*bias.shape),
+            weights(*up_all.shape[4:]),
+            weights(units, features),
         ],
         out_specs=(
             whole(rows, features),
@@ -683,9 +732,8 @@
     for t in range(1, wide):
         spread(t).start()
 
-    order = []
-    for i in range((lines + 1) // 2):
-        order += [lines - 1 - i] if lines - 1 - i == i else [lines - 1 - i, i]
+    lower = z < lines // 2
+    order = [jnp.where(lower, lines - 1 - k, k) for k in range(lines)]
 
     def block(owner):
         columns = pl.ds(pl.multiple_of(owner * rows, rows), rows)
@@ -711,27 +759,31 @@
         arrived(from_sibling.at[zs], sib_got.at[zs])
         accumulate(held.at[zs], from_sibling.at[zs])
 
-    def feed(t):
+    flight = 2
+
+    def fed(k):
+        t, c = divmod(k, chunks)
+
         @pl.when(z == 0)
         def _():
-            for c in range(chunks):
-                pass_on(lines - 1 - t, c, True).start()
+            pass_on(lines - 1 - t, c, True).wait_send()
 
         @pl.when(z == lines - 1)
         def _():
-            for c in range(chunks):
-                pass_on(t, c, False).start()
-
-    def fed(t):
+            pass_on(t, c, False).wait_send()
+
+    def feed(k):
+        t, c = divmod(k, chunks)
+        if k >= flight:
+            fed(k - flight)
+
         @pl.when(z == 0)
         def _():
-            for c in range(chunks):
-                pass_on(lines - 1 - t, c, True).wait_send()
+            pass_on(lines - 1 - t, c, True).start()
 
         @pl.when(z == lines - 1)
         def _():
-            for c in range(chunks):
-                pass_on(t, c, False).wait_send()
+            pass_on(t, c, False).start()
 
     for i, zs in enumerate(order):
         for_sibling[zs] = block(2 * zs + 1 - core)
@@ -739,11 +791,10 @@
         held[zs] = block(2 * zs + core)
         if i >= 1:
             merge(order[i - 1])
-        if i == 2:
-            feed(0)
+        if i == 1:
+            for k in range(flight):
+                feed(k)
     merge(order[-1])
-    if lines <= 2:
-        feed(0)
 
     load.wait()
     total_qkv[...] = jnp.dot(packed_ref[...], normed[...], preferred_element_type=f32)
@@ -796,12 +847,12 @@
 
     qkv_first()
     for t in range(1, lines):
-        if t <= lines - 2:
-            fed(t - 1)
-            feed(t)
         below, above = lines - 1 - (t - z), t - (lines - 1 - z)
         for c in range(chunks):
             part = pl.ds(c * step, step)
+            k = (t - 1) * chunks + c + flight
+            if k < (lines - 1) * chunks:
+                feed(k)
             if t < lines - 1:
 
                 @pl.when(jnp.logical_and(z >= 1, t >= z))
@@ -850,7 +901,7 @@
             centred = values - jnp.mean(values, axis=-1, keepdims=True)
             inverse = lax.rsqrt(jnp.mean(centred * centred, axis=-1, keepdims=True) + epsilon)
             scaled = centred * inverse
-            term = grad * gain_ref[...]
+            term = grad * as_row(gain_ref)
             back = inverse * (
                 term
                 - jnp.mean(term, axis=-1, keepdims=True)
@@ -869,12 +920,15 @@
             gain_sum, bias_sum = gain_sum + sums[0], bias_sum + sums[1]
 
     row = lax.broadcasted_iota(jnp.int32, (8, features), 0)
-    norms[...] = jnp.where(row == 0, gain_sum, jnp.where(row == 1, bias_sum, norm_ref[...]))
+    parts = jnp.where(row == 0, gain_sum, jnp.where(row == 1, bias_sum, norm_ref[...]))
+    share = features // narrow
+    for owner in range(narrow):
+        norms[owner] = parts[:, owner * share : (owner + 1) * share]
 
     def down_column(t):
-        return remote(
-            norms, norm_column.at[t - 1], column_sent.at[t - 1], column_got.at[t - 1],
-            w, lax.rem(n + t, narrow),
+        to = lax.rem(n + t, narrow)
+        return remote(
+            norms.at[to], norm_column.at[t - 1], column_sent.at[t - 1], column_got.at[t - 1], w, to
         )
 
     def over_plane(t):
@@ -885,7 +939,7 @@
 
     for t in range(1, narrow):
         down_column(t).start()
-    total = norms[...]
+    total = norms[n]
     for t in range(1, narrow):
         arrived(norm_column.at[t - 1], column_got.at[t - 1])
         total = total + norm_column[t - 1]
@@ -909,7 +963,8 @@
         second(h, i).wait_send()
     for zs in order:
         to_sibling(zs).wait_send()
-    fed(lines - 2)
+    for k in range(flight):
+        fed((lines - 1) * chunks - 1 - k)
     for zs in range(lines):
         for c in range(chunks):
 
@@ -922,7 +977,7 @@
                 pass_on(zs, c, False).wait_send()
 
 
-def finish(wide, narrow, packed, weight, normed, tokens, middle, gain, norm_parts, piece, chunks=2):
+def finish(wide, narrow, packed, weight, normed, tokens, middle, gain, norm_parts, piece, chunks=4):
     side, lines = math.isqrt(wide), narrow // 2
     rows, features = tokens.shape
     columns = packed.shape[0]
@@ -937,7 +992,7 @@
             jax.ShapeDtypeStruct((rows, features), bf16),
             jax.ShapeDtypeStruct((columns, features), bf16),
             jax.ShapeDtypeStruct((wide, *piece.shape), bf16),
-            jax.ShapeDtypeStruct((8, features), f32),
+            jax.ShapeDtypeStruct((8, features // narrow), f32),
         ),
         scratch_shapes=[
             pltpu.VMEM(normed.shape, bf16),
@@ -950,10 +1005,10 @@
             pltpu.VMEM((2, side - 1, columns // 2, features), bf16),
             pltpu.VMEM((2, side - 1, columns // 2, features), bf16),
             pltpu.VMEM((2, columns // 2, features), bf16),
-            pltpu.VMEM((8, features), f32),
-            pltpu.VMEM((narrow - 1, 8, features), f32),
-            pltpu.VMEM((8, features), f32),
-            pltpu.VMEM((wide - 1, 8, features), f32),
+            pltpu.VMEM((narrow, 8, features // narrow), f32),
+            pltpu.VMEM((narrow - 1, 8, features // narrow), f32),
+            pltpu.VMEM((8, features // narrow), f32),
+            pltpu.VMEM((wide - 1, 8, features // narrow), f32),
             dma(()),
             dma(()),
             dma((lines,)),
@@ -978,28 +1033,58 @@
     )(packed, weight, normed, tokens, middle, gain, norm_parts, piece)
 
 
+def unpack_kernel(shard_ref, qkv_ref, qkv_out, proj_out, up_out, down_out):
+    wide = shard_ref.shape[0]
+    features = shard_ref.shape[3]
+    columns = up_out.shape[1]
+    groups = features // columns
+    units, few = down_out.shape[0] // (2 * wide), proj_out.shape[0] // (2 * wide)
+    for j in range(2 * wide):
+        w, h = divmod(j, 2)
+        for g in range(groups):
+            up_out[(j * groups + g) * units : (j * groups + g + 1) * units, :] = shard_ref[
+                w, h, 0:units, g * columns : (g + 1) * columns
+            ].astype(f32)
+        down_out[j * units : (j + 1) * units, :] = shard_ref[w, h, units : 2 * units, :].astype(f32)
+        proj_out[j * few : (j + 1) * few, :] = shard_ref[w, h, 2 * units :, :].astype(f32)
+    qkv_out[...] = qkv_ref[...].astype(f32).T
+
+
+def unpack(shard, qkv, proj_shape, up_shape, down_shape):
+    return pl.pallas_call(
+        unpack_kernel,
+        out_shape=tuple(
+            jax.ShapeDtypeStruct(shape, f32)
+            for shape in (qkv.shape[::-1], proj_shape, up_shape, down_shape)
+        ),
+        compiler_params=pltpu.CompilerParams(vmem_limit_bytes=48 << 20),
+        name="unpack",
+    )(shard, qkv)
+
+
 class Gather:
-    def __init__(self, wide, narrow, own, out, *semaphores):
-        self.own, self.out = own, out
+    def __init__(self, wide, narrow, owns, out, mine, *semaphores):
+        self.owns, self.out, self.mine = owns, out, mine
         self.w, self.n = lax.axis_index("wide"), lax.axis_index("narrow")
         self.side, self.lines = math.isqrt(wide), narrow // 2
         self.a, self.b = self.w // self.side, lax.rem(self.w, self.side)
         self.z, self.core = self.n // 2, lax.rem(self.n, 2)
         self.sibling = self.n + 1 - 2 * self.core
         (
-            self.copied, self.own_sent, self.passed, self.line_got, self.first_sent, self.first_got,
+            self.loaded, self.copied, self.own_sent, self.passed, self.line_got, self.first_sent, self.first_got,
             self.second_sent, self.second_got, self.f0_sent, self.f0_got, self.f1_sent, self.f1_got,
             self.f2_sent, self.f2_got, self.f3_sent, self.f3_got,
         ) = semaphores
         self.pairs = [(h, i) for i in range(1, self.side) for h in (0, 1)]
 
     @staticmethod
-    def scratch(wide, narrow):
+    def scratch(wide, narrow, piece):
         side, lines = math.isqrt(wide), narrow // 2
         dma = pltpu.SemaphoreType.DMA
         line, plane = (lines,), (lines, 2, side)
-        shapes = [(), line, line, line, plane, plane, plane, plane, (), (), line, line]
-        return [dma(shape) for shape in shapes + [plane] * 4]
+        shapes = [(2,), (), line, line, line, plane, plane, plane, plane, (), (), line, line]
+        mine = pltpu.VMEM((side, side, 2, *piece), bf16)
+        return [mine, *[dma(shape) for shape in shapes + [plane] * 4]]
 
     def other_a(self, i):
         return lax.rem(self.a + i, self.side)
@@ -1009,7 +1094,7 @@
 
     def own_on(self, way):
         return remote(
-            self.own.at[self.a, self.b], self.out.at[self.n, self.a, self.b],
+            self.mine.at[self.a, self.b], self.out.at[self.n, self.a, self.b],
             self.own_sent.at[self.z + way], self.line_got.at[self.z], self.w, self.n + 2 * way,
         )
 
@@ -1054,7 +1139,7 @@
 
     def hand0(self):
         return remote(
-            self.own, self.out.at[self.n], self.f0_sent, self.f0_got, self.w, self.sibling
+            self.mine, self.out.at[self.n], self.f0_sent, self.f0_got, self.w, self.sibling
         )
 
     def hand1(self, zs):
@@ -1073,8 +1158,16 @@
             piece, piece, self.f3_sent.at[zs, h, k], self.f3_got.at[zs, h, k], self.w, self.sibling
         )
 
+    def load(self):
+        copies, row = [], 0
+        for k, own in enumerate(self.owns):
+            part = self.mine.at[:, :, :, pl.ds(row, own.shape[3])]
+            copies.append(pltpu.make_async_copy(own, part, self.loaded.at[k]))
+            row += own.shape[3]
+        return copies
+
     def keep(self):
-        return pltpu.make_async_copy(self.own, self.out.at[self.n], self.copied)
+        return pltpu.make_async_copy(self.mine, self.out.at[self.n], self.copied)
 
     def sides(self, d, act):
         if not 1 <= d <= self.lines - 1:
@@ -1090,6 +1183,11 @@
             act(z + d, -1, z > 0)
 
     def begin(self):
+        for copy in self.load():
+            copy.start()
+        for copy in self.load():
+            copy.wait()
+
         @pl.when(self.z < self.lines - 1)
         def _():
             self.own_on(1).start()
@@ -1170,9 +1268,9 @@
 
 def start_kernel(
     wide, narrow, token_ref, gain_ref, bias_ref, weight_ref, own_ref,
-    normed, packed, gathered, line_sent, line_got, sib_sent, sib_got, *gather_refs,
+    normed, packed, turned, gathered, line_sent, line_got, sib_sent, sib_got, *gather_refs,
 ):
-    gather = Gather(wide, narrow, own_ref, gathered, *gather_refs)
+    gather = Gather(wide, narrow, [own_ref], gathered, *gather_refs)
     w, n, z, core = gather.w, gather.n, gather.z, gather.core
     lines, sibling = gather.lines, gather.sibling
     rows = token_ref.shape[0]
@@ -1183,84 +1281,100 @@
         centred = values - jnp.mean(values, axis=-1, keepdims=True)
         variance = jnp.mean(centred * centred, axis=-1, keepdims=True)
         normed[n, part, :] = (
-            centred * lax.rsqrt(variance + epsilon) * gain_ref[...] + bias_ref[...]
+            centred * lax.rsqrt(variance + epsilon) * as_row(gain_ref) + as_row(bias_ref)
         ).astype(bf16)
         return carry
 
     lax.fori_loop(0, rows // 64, norm_rows, 0)
     greet(wide, narrow, w, n)
 
-    def pass_on(zs, way):
-        block = normed.at[2 * zs + core]
+    step = rows // CHUNKS
+
+    def part_of(shard, c):
+        return normed.at[shard, pl.ds(c * step, step)]
+
+    def pass_on(zs, c, way):
+        block = part_of(2 * zs + core, c)
         k = (1 - way) // 2
-        return remote(block, block, line_sent.at[zs, k], line_got.at[zs], w, n + 2 * way)
-
-    def hand(zs):
-        block = normed.at[2 * zs + core]
-        return remote(block, block, sib_sent.at[zs], sib_got.at[zs], w, sibling)
-
-    def project(owner):
-        columns = pl.ds(pl.multiple_of(owner * rows, rows), rows)
-        packed[:, columns] = contract(weight_ref[...], normed[owner], 1, 1).astype(bf16)
-
-    @pl.when(z < lines - 1)
-    def _():
-        pass_on(z, 1).start()
-
-    @pl.when(z > 0)
-    def _():
-        pass_on(z, -1).start()
-
-    hand(z).start()
-    project(n)
-
-    def receive(zs, way, more):
-        arrived(normed.at[2 * zs + core], line_got.at[zs])
+        return remote(block, block, line_sent.at[zs, c, k], line_got.at[zs, c], w, n + 2 * way)
+
+    def hand(zs, c):
+        block = part_of(2 * zs + core, c)
+        return remote(block, block, sib_sent.at[zs, c], sib_got.at[zs, c], w, sibling)
+
+    def project(owner, c):
+        columns = pl.ds(pl.multiple_of(owner * rows + c * step, step), step)
+        packed[:, columns] = contract(
+            turned[...], normed[owner, pl.ds(c * step, step)], 1, 1
+        ).astype(bf16)
+
+    gather.begin()
+    for c in range(CHUNKS):
+
+        @pl.when(z < lines - 1)
+        def _():
+            pass_on(z, c, 1).start()
+
+        @pl.when(z > 0)
+        def _():
+            pass_on(z, c, -1).start()
+
+        hand(z, c).start()
+    turned[...] = weight_ref[...].T
+    for c in range(CHUNKS):
+        project(n, c)
+
+    def receive(c, zs, way, more):
+        arrived(part_of(2 * zs + core, c), line_got.at[zs, c])
 
         @pl.when(more)
         def _():
-            pass_on(zs, way).start()
-
-        hand(zs).start()
+            pass_on(zs, c, way).start()
+
+        hand(zs, c).start()
 
     def project_side(zs, way, more):
-        project(2 * zs + core)
+        for c in range(CHUNKS):
+            project(2 * zs + core, c)
 
     def project_sibling(zs, way, more):
-        arrived(normed.at[2 * zs + 1 - core], sib_got.at[zs])
-        project(2 * zs + 1 - core)
-
+        for c in range(CHUNKS):
+            arrived(part_of(2 * zs + 1 - core, c), sib_got.at[zs, c])
+            project(2 * zs + 1 - core, c)
+
+    project_sibling(z, 0, None)
     for d in range(1, lines):
-        gather.sides(d, receive)
-        if d == 1:
-            gather.begin()
-            project_sibling(z, 0, None)
-        else:
-            gather.round(d - 1)
+        gather.round(d)
+        if d == lines - 1:
+            gather.round(lines)
+            gather.round(lines + 1)
+        for c in range(CHUNKS):
+            gather.sides(d, functools.partial(receive, c))
+        if d > 1:
             gather.sides(d - 1, project_sibling)
         gather.sides(d, project_side)
-    gather.round(lines - 1)
     gather.sides(lines - 1, project_sibling)
-    gather.round(lines)
-    gather.round(lines + 1)
     gather.finish()
 
     def sent_side(zs, way, more):
-        hand(zs).wait_send()
-
-        @pl.when(more)
-        def _():
-            pass_on(zs, way).wait_send()
-
-    @pl.when(z < lines - 1)
-    def _():
-        pass_on(z, 1).wait_send()
-
-    @pl.when(z > 0)
-    def _():
-        pass_on(z, -1).wait_send()
-
-    hand(z).wait_send()
+        for c in range(CHUNKS):
+            hand(zs, c).wait_send()
+
+            @pl.when(more)
+            def _():
+                pass_on(zs, c, way).wait_send()
+
+    for c in range(CHUNKS):
+
+        @pl.when(z < lines - 1)
+        def _():
+            pass_on(z, c, 1).wait_send()
+
+        @pl.when(z > 0)
+        def _():
+            pass_on(z, c, -1).wait_send()
+
+        hand(z, c).wait_send()
     for d in range(1, lines):
         gather.sides(d, sent_side)
 
@@ -1274,15 +1388,16 @@
     return pl.pallas_call(
         functools.partial(start_kernel, wide, narrow),
         in_specs=[vmem, vmem, vmem, vmem, anywhere],
-        out_specs=(vmem, vmem, anywhere),
+        out_specs=(vmem, vmem, vmem, anywhere),
         out_shape=(
             jax.ShapeDtypeStruct((narrow, rows, features), bf16),
-            jax.ShapeDtypeStruct((weight.shape[0], narrow * rows), bf16),
+            jax.ShapeDtypeStruct((weight.shape[1], narrow * rows), bf16),
+            jax.ShapeDtypeStruct((weight.shape[1], features), bf16),
             jax.ShapeDtypeStruct((narrow, *own.shape), bf16),
         ),
         scratch_shapes=[
-            dma((lines, 2)), dma((lines,)), dma((lines,)), dma((lines,)),
-            *Gather.scratch(wide, narrow),
+            dma((lines, CHUNKS, 2)), dma((lines, CHUNKS)), dma((lines, CHUNKS)), dma((lines, CHUNKS)),
+            *Gather.scratch(wide, narrow, own.shape[3:]),
         ],
         compiler_params=pltpu.CompilerParams(
             vmem_limit_bytes=58 << 20, collective_id=1, has_side_effects=True
@@ -1297,12 +1412,9 @@
 ):
     items = item_lengths.shape[1]
     heads = qkv_weight.shape[1] // (3 * HEAD_DIM)
-    gain_one, bias_one = attn_gain.astype(f32), attn_bias.astype(f32)
-    gain_two, bias_two = mlp_gain.astype(f32), mlp_bias.astype(f32)
     wide, narrow = lax.axis_size("wide"), lax.axis_size("narrow")
     side = math.isqrt(wide)
     rows = narrow * tokens.shape[0]
-    qkv_turned = qkv_weight.T
 
     def cut(shard):
         return shard.reshape(side, side, 2, shard.shape[0] // (2 * wide), shard.shape[1])
@@ -1310,44 +1422,37 @@
     def split_parts(total):
         return total.reshape(narrow, side, side, 2, -1, total.shape[1])
 
-    own_up, own_rest = cut(up_weight.T), jnp.concatenate([cut(down_weight), cut(proj_weight)], axis=3)
-    first = own_up.shape[3]
-    query_extra, key_extra = mask_rows(item_lengths, rows)
-    normed_all, packed, up_all = start(
-        wide, narrow, tokens, gain_one.reshape(1, -1), bias_one.reshape(1, -1), qkv_turned, own_up
+    first = down_weight.shape[0] // (2 * wide)
+    extras = mask_rows(item_lengths, rows)
+    normed_all, packed, qkv_turned, up_all = start(
+        wide, narrow, tokens, attn_gain, attn_bias, qkv_weight, cut(up_weight)
     )
     normed_all = normed_all.reshape(rows, -1)
     packed = packed.reshape(heads, 3, HEAD_DIM, rows)
     attended, log_total, attended_rows, rest_all = attend_forward(
-        wide, narrow, packed, query_extra, key_extra, own_rest
+        wide, narrow, packed, extras, cut(down_weight), cut(proj_weight)
     )
     attended_rows = attended_rows.reshape(-1, tokens.shape[0])
     proj_all = rest_all[:, :, :, :, first:].reshape(-1, tokens.shape[1])
     output, grad_middle, grad_attended, grad_proj, grad_parts, norm_parts = mlp(
-        attended_rows, proj_all, tokens, cotangent, gain_two.reshape(1, -1),
-        bias_two.reshape(1, -1), up_all, rest_all, first,
+        attended_rows, proj_all, tokens, cotangent, mlp_gain, mlp_bias, up_all, rest_all, first
     )
-    grad_attended = lax.all_to_all(
-        grad_attended, "narrow", split_axis=0, concat_axis=1, tiled=True
-    ).reshape(heads, HEAD_DIM, rows)
+    grad_attended = grad_attended.reshape(narrow, heads, HEAD_DIM, -1)
     grad_proj_parts = split_parts(grad_proj)
     grad_packed, grad_piece = attend_backward(
-        wide, narrow, packed, query_extra, key_extra, attended, grad_attended, log_total,
+        wide, narrow, packed, extras, attended, grad_attended, log_total,
         grad_parts, grad_proj_parts, items,
     )
     grad_packed = grad_packed.reshape(heads * 3 * HEAD_DIM, rows)
-    grad_tokens, grad_qkv, grad_shard, norm_sums = finish(
+    grad_tokens, grad_qkv, grad_shard, shares = finish(
         wide, narrow, grad_packed, qkv_turned, normed_all, tokens, grad_middle,
-        gain_one.reshape(1, -1), norm_parts, grad_piece,
+        attn_gain, norm_parts, grad_piece,
     )
-    grad_shard = grad_shard.astype(f32)
-    grad_up = grad_shard[:, :, :first].reshape(-1, tokens.shape[1]).T
-    grad_down = grad_shard[:, :, first : 2 * first].reshape(-1, tokens.shape[1])
-    grad_proj = grad_shard[:, :, 2 * first :].reshape(-1, tokens.shape[1])
-    share = norm_sums.shape[1] // narrow
-    shares = lax.dynamic_slice_in_dim(norm_sums, lax.axis_index("narrow") * share, share, 1)
+    grad_qkv, grad_proj, grad_up, grad_down = unpack(
+        grad_shard, grad_qkv, proj_weight.shape, up_weight.shape, down_weight.shape
+    )
     return (
-        output, grad_tokens, shares[0], shares[1], grad_qkv.T.astype(f32), grad_proj,
+        output, grad_tokens, shares[0], shares[1], grad_qkv, grad_proj,
         shares[2], shares[3], grad_up, grad_down,
     )
 

time: 514 us -> 456 us (0.89)
  waiting for transfers between devices: 26.6 us -> 0 us
  Pallas kernels: 453 us -> 441 us
  local copies, waits for them, and re-layouts: 19.7 us -> 9.76 us
  starting transfers between devices: 7.34 us -> 0 us
    all_to_all x1 -> x0, waiting for transfers between devices: 26.6 us -> none  [body(): lax.all_to_all(grad_attended, 'narrow', split_axis=0, concat_axis=1, tile...]
    pallas_call x1, Pallas kernels: 123 us -> 105 us  [start(): pl.pallas_call(functools.partial(start_kernel, wide, narrow), in_specs=[v...]
    pallas_call x1, Pallas kernels: 113 us -> 121 us  [attend_backward(): pl.pallas_call(functools.partial(backward_kernel, block, rows, items, wid...]
    all_to_all x1 -> x0, starting transfers between devices: 7.34 us -> none  [body(): lax.all_to_all(grad_attended, 'narrow', split_axis=0, concat_axis=1, tile...]
    pallas_call x1, Pallas kernels: 107 us -> 100 us  [finish(): pl.pallas_call(functools.partial(finish_kernel, wide, narrow, chunks), in...]
  transfers between devices with their start and end apart: 1 -> 0, of which waited for: 1 -> 0; matrix products, arithmetic and copies ran while one was open for 0% -> 0% of each run, Pallas kernels for 0% -> 0%
where the time goes in v5:
time: 456 us; the launch traced here: 455 us
  Pallas kernels  441 us (97%)
  local copies, waits for them, and re-layouts  9.76 us (2%)
    pallas_call x1, Pallas kernels, attend_backward(): pl.pallas_call(functools.partial(backward_kernel, block, rows, items, wid...  121 us
    pallas_call x1, Pallas kernels, start(): pl.pallas_call(functools.partial(start_kernel, wide, narrow), in_specs=[v...  105 us
    pallas_call x1, Pallas kernels, finish(): pl.pallas_call(functools.partial(finish_kernel, wide, narrow, chunks), in...  100 us
    pallas_call x1, Pallas kernels, attend_forward(): pl.pallas_call(functools.partial(forward_kernel, wide, narrow), grid=(hea...  68.5 us
    pallas_call x1, Pallas kernels, mlp(): pl.pallas_call(mlp_kernel, grid=(narrow,), in_specs=[whole(*attended.shap...  43.4 us

profile of v5, /device:TPU:0, one launch (start us, length us, event | category | flops | bytes accessed | tf_op | source)
XLA Modules:
  0.0 455.4 jit_solution(10266336356216950699)
XLA Ops:
  0.7 1.4 fusion.2
  4.7 0.7 convert_add_fusion
  5.3 0.1 fusion.1
  5.5 0.8 select_convert_fusion.qx_ref.kx_ref
  6.2 104.9 %start.1 = (bf16[8,512,1024]{2,1,0:T(8,128)(2,1)}, bf16[384,4096]{1,0:T(8,128)(2,1)}, bf16[384,1024]{1,0:T(8,128)(2,1)}, bf16[8,2,2,2,128,512]{5,4,3,2,1,0:T(8,128)(2,1)}) custom-call(bf16[512,1024]{1,0:T(8,128)(2,1)} %token_ref.5, bf16[1024]{0:T(1024)(128)(2,1)} %gain_ref.5, bf16[1024]{0:T(1024)(128)(2,1)} %bias_ref.2, bf16[1024,384]{1,0:T(8,128)(2,1)} %weight_ref.1, ...), custom_call_target="tpu_custom_call" | custom-call | tf_op jit(solution)/shard_map/start/pallas_call | solution.py:1388
  111.2 68.5 %attend_forward.1 = (bf16[2,64,4096]{2,1,0:T(8,128)(2,1)}, f32[2,1,4096]{2,1,0:T(1,128)}, bf16[8,2,64,512]{3,2,1,0:T(8,128)(2,1)}, bf16[8,2,2,2,80,1024]{5,4,3,2,1,0:T(8,128)(2,1)}) custom-call(bf16[2,16,4096]{2,1,0:T(8,128)(2,1)} %select_convert_fusion.qx_ref.kx_ref, bf16[2,16,4096]{2,1,0:T(8,128)(2,1)} %select_convert_fusion.qx_ref.kx_ref, ...), custom_call_target="tpu_custom_call" | custom-call | tf_op jit(solution)/shard_map/attend_forward/pallas_call | solution.py:130
  179.7 3.2 slice.41
  182.9 43.4 %mlp.1 = (bf16[512,1024]{1,0:T(8,128)(2,1)}, f32[512,1024]{1,0:T(8,128)}, bf16[1024,512]{1,0:T(8,128)(2,1)}, bf16[1024,1024]{1,0:T(8,128)(2,1)}, bf16[8,2,2,2,12...) custom-call(bf16[1024,512]{1,0:T(8,128)(2,1)} %bitcast.31, bf16[1024,1024]{1,0:T(8,128)(2,1)} %bitcast.28, ...), custom_call_target="tpu_custom_call" | custom-call | tf_op jit(solution)/shard_map/mlp/pallas_call | solution.py:663
  226.4 120.8 %attend_backward.1 = (bf16[2,3,64,4096]{3,2,1,0:T(8,128)(2,1)}, bf16[2,144,1024]{2,1,0:T(8,128)(2,1)}) custom-call(bf16[2,16,4096]{2,1,0:T(8,128)(2,1)} %select_convert_fusion.qx_ref.kx_ref, bf16[2,16,4096]{2,1,0:T(8,128)(2,1)} %select_convert_fusion.qx_ref.kx_ref, bf16[2,3,64,4096]{3,2,1,0:T(8,128)(2,1)} %bitcast.25, bf16[2,3,64,4096]{3,2,1,0:T(8,128)(2,1)} %bitcast.26, ...), custom_call_target="tpu_custom_call" | custom-call | flops 85899345920 | bytes 8388608 | tf_op jit(solution)/shard_map/attend_backward/pallas_call | solution.py:495
  347.2 100.1 %finish.1 = (bf16[512,1024]{1,0:T(8,128)(2,1)}, bf16[384,1024]{1,0:T(8,128)(2,1)}, bf16[4,2,144,1024]{3,2,1,0:T(8,128)(2,1)}, f32[8,128]{1,0:T(8,128)}) custom-call(bf16[384,4096]{1,0:T(8,128)(2,1)} %bitcast.30, bf16[384,1024]{1,0:T(8,128)(2,1)} %get-tuple-element.45.weight_ref, bf16[4096,1024]{1,0:T(8,128)(2,1)} %bitcast.29, bf16[512,1024]{1,0:T(8,128)(2,1)} %token_ref.5, ...), custom_call_target="tpu_custom_call" | custom-call | tf_op jit(solution)/shard_map/finish/pallas_call | solution.py:987
  447.3 1.3 slice_bitcast_fusion
  448.6 0.0 copy-start
  448.6 1.7 copy-done
  450.3 0.0 copy-start.1
  450.3 1.1 copy-done.1
  451.4 0.0 copy-start.2
  451.4 2.9 unpack.1
  454.4 0.0 copy-done.2
  454.4 1.0 copy.22
  (3 shorter events, 0.0 us)
Async XLA Ops:
  448.6 1.7 copy-start
  450.3 1.1 copy-start.1
  451.4 3.0 copy-start.2

commit v6 on v5

--- a/solution.py
+++ b/solution.py
@@ -11,6 +11,8 @@
 HEAD_DIM = 64
 EXTRA = 16
 CHUNKS = 2
+REDUCE_START, REDUCE_STEP, REDUCE_FIRST, REDUCE_SECOND, SPREAD_AT = 2, 11, 8, 12, 8
+EARLY_RELAY = 17
 EXCLUDED = -1e30
 bf16 = jnp.bfloat16
 f32 = jnp.float32
@@ -73,7 +75,7 @@
     owner = lax.rem(n + 1 + step, narrow)
     columns = pl.ds(pl.multiple_of(owner * width, width), width)
     query = jnp.concatenate(
-        [q_ref[0, :, columns] * jnp.asarray(0.125, bf16), qx_ref[:, columns]], axis=0
+        [q_ref[0, :, columns], qx_ref[:, columns]], axis=0
     )
     scores = jnp.dot(keys[...], query, preferred_element_type=f32)
     maximum = jnp.max(scores, axis=0, keepdims=True)
@@ -212,13 +214,18 @@
 
 
 def reduce_steps(
-    wide, narrow, parts, proj_parts, final, held, from_sibling, from_first, from_second, from_line,
-    loaded, sib_sent, sib_got, first_sent, first_got, second_sent, second_got, line_sent, line_got,
+    wide, narrow, parts, proj_parts, landed, final, held, staged, from_first, from_second, from_line,
+    mine, loaded, sib_sent, sib_got, first_sent, first_got, second_sent, second_got, line_sent, line_got,
 ):
     w, n = lax.axis_index("wide"), lax.axis_index("narrow")
     side, lines = math.isqrt(wide), narrow // 2
     a, b, z, core = w // side, lax.rem(w, side), n // 2, lax.rem(n, 2)
     sibling = n + 1 - 2 * core
+    slots = held.shape[0]
+    most, least = parts.shape[4], proj_parts.shape[4]
+    sources = [(parts, pl.ds(0, most)), (proj_parts, pl.ds(most, least))]
+    order = [lax.rem(z + 1 + j, lines) for j in range(lines)]
+    halves = [(h, i) for i in range(1, side) for h in (0, 1)]
 
     def other_a(i):
         return lax.rem(a + i, side)
@@ -226,316 +233,161 @@
     def other_b(i):
         return lax.rem(b + i, side)
 
-    most, least = parts.shape[4], proj_parts.shape[4]
-    sources = [(parts, pl.ds(0, most)), (proj_parts, pl.ds(most, least))]
-
-    def to_sibling(zs):
-        shard = 2 * zs + 1 - core
+    def to_sibling(j):
+        shard = 2 * order[j] + 1 - core
         return [
             remote(
-                src.at[shard], from_sibling.at[zs, :, :, :, rows],
-                sib_sent.at[k, zs], sib_got.at[k, zs], w, sibling,
+                src.at[shard], landed.at[j, :, :, :, rows],
+                sib_sent.at[k, j], sib_got.at[k, j], w, sibling,
             )
             for k, (src, rows) in enumerate(sources)
         ]
 
-    def load(zs):
-        shard = 2 * zs + core
+    def load(j):
+        shard, slot = 2 * order[j] + core, j % slots
         return [
-            pltpu.make_async_copy(src.at[shard], held.at[zs, :, :, :, rows], loaded.at[k, zs])
+            pltpu.make_async_copy(src.at[shard], held.at[slot, :, :, :, rows], loaded.at[k])
             for k, (src, rows) in enumerate(sources)
         ]
 
-    def first(zs, h, i):
+    def stage(j):
+        return pltpu.make_async_copy(landed.at[j], staged, loaded.at[2])
+
+    def first(j, h, i):
+        slot, k = j % slots, i - 1
         if h == 0:
-            src, to = held.at[zs, other_a(i), :, 0], other_a(i) * side + b
+            src, to = held.at[slot, other_a(i), :, 0], other_a(i) * side + b
         else:
-            src, to = held.at[zs, :, other_b(i), 1], a * side + other_b(i)
-        k = i - 1
-        return remote(
-            src, from_first.at[zs, h, k], first_sent.at[zs, h, k], first_got.at[zs, h, k], to, n
-        )
-
-    def second(zs, h, i):
+            src, to = held.at[slot, :, other_b(i), 1], a * side + other_b(i)
+        return remote(
+            src, from_first.at[j, h, k], first_sent.at[j, h, k], first_got.at[j, h, k], to, n
+        )
+
+    def second(j, h, i):
+        slot, k = j % slots, i - 1
         if h == 0:
-            src, to = held.at[zs, a, other_b(i), 0], a * side + other_b(i)
+            src, to = held.at[slot, a, other_b(i), 0], a * side + other_b(i)
         else:
-            src, to = held.at[zs, other_a(i), b, 1], other_a(i) * side + b
-        k = i - 1
-        return remote(
-            src, from_second.at[zs, h, k], second_sent.at[zs, h, k], second_got.at[zs, h, k], to, n
-        )
-
-    def along(zs):
-        slot = jnp.where(z < zs, z, z - 1)
-        return remote(
-            held.at[zs, a, b], from_line.at[slot], line_sent.at[zs], line_got.at[slot], w, 2 * zs + core
-        )
-
-    order = []
-    for i in range((lines + 1) // 2):
-        order += [lines - 1 - i] if lines - 1 - i == i else [lines - 1 - i, i]
-    halves = [(h, i) for i in range(1, side) for h in (0, 1)]
+            src, to = held.at[slot, other_a(i), b, 1], other_a(i) * side + b
+        return remote(
+            src, from_second.at[j, h, k], second_sent.at[j, h, k], second_got.at[j, h, k], to, n
+        )
+
+    def along(j):
+        zs = order[j]
+        place = jnp.where(z < zs, z, z - 1)
+        return remote(
+            held.at[j % slots, a, b], from_line.at[place], line_sent.at[j], line_got.at[place],
+            w, 2 * zs + core,
+        )
 
     def begin():
-        for zs in order:
-            for copy in to_sibling(zs) + load(zs):
+        for j in range(lines):
+            for copy in to_sibling(j):
                 copy.start()
 
-    def combine(zs):
-        for copy in load(zs):
+    def sent(j):
+        for h, i in halves:
+            first(j, h, i).wait_send()
+            second(j, h, i).wait_send()
+
+        if j < lines - 1:
+            along(j).wait_send()
+
+    def combine(j):
+        slot = j % slots
+        if j >= slots:
+            sent(j - slots)
+        for copy in load(j):
+            copy.start()
+        for k, (_, rows) in enumerate(sources):
+            arrived(landed.at[j, :, :, :, rows], sib_got.at[k, j])
+        stage(j).start()
+        for copy in load(j):
             copy.wait()
-        for k, (_, rows) in enumerate(sources):
-            arrived(from_sibling.at[zs, :, :, :, rows], sib_got.at[k, zs])
-
-        def piece(j, carry):
-            p, q = j // side, lax.rem(j, side)
+        stage(j).wait()
+
+        def piece(t, carry):
+            p, q = t // side, lax.rem(t, side)
             for h in (0, 1):
-                accumulate(held.at[zs, p, q, h], from_sibling.at[zs, p, q, h])
+                accumulate(held.at[slot, p, q, h], staged.at[p, q, h])
             return carry
 
         lax.fori_loop(0, wide, piece, 0)
         for h, i in halves:
-            first(zs, h, i).start()
-
-    def narrow_down(zs):
+            first(j, h, i).start()
+
+    def narrow_down(j):
+        slot = j % slots
         for h in (0, 1):
             for i in range(1, side):
-                arrived(from_first.at[zs, h, i - 1], first_got.at[zs, h, i - 1])
-
-            def piece(j, carry, h=h):
-                into = held.at[zs, a, j, 0] if h == 0 else held.at[zs, j, b, 1]
-                accumulate(into, *[from_first.at[zs, h, i, j] for i in range(side - 1)])
+                arrived(from_first.at[j, h, i - 1], first_got.at[j, h, i - 1])
+
+            def piece(t, carry, h=h):
+                into = held.at[slot, a, t, 0] if h == 0 else held.at[slot, t, b, 1]
+                accumulate(into, *[from_first.at[j, h, i, t] for i in range(side - 1)])
                 return carry
 
             lax.fori_loop(0, side, piece, 0)
         for h, i in halves:
-            second(zs, h, i).start()
-
-    def send_home(zs):
+            second(j, h, i).start()
+
+    def send_home(j):
+        slot = j % slots
         for h, i in halves:
-            arrived(from_second.at[zs, h, i - 1], second_got.at[zs, h, i - 1])
+            arrived(from_second.at[j, h, i - 1], second_got.at[j, h, i - 1])
         for h in (0, 1):
             accumulate(
-                held.at[zs, a, b, h], *[from_second.at[zs, h, i] for i in range(side - 1)]
+                held.at[slot, a, b, h], *[from_second.at[j, h, i] for i in range(side - 1)]
             )
 
-        @pl.when(z != zs)
-        def _():
-            along(zs).start()
+        if j < lines - 1:
+            along(j).start()
+        else:
+            mine[...] = held[slot, a, b]
 
     def finish():
-        for slot in range(lines - 1):
-            arrived(from_line.at[slot], line_got.at[slot])
+        for place in range(lines - 1):
+            arrived(from_line.at[place], line_got.at[place])
         for h in (0, 1):
-            total = held[z, a, b, h].astype(f32)
-            for slot in range(lines - 1):
-                total = total + from_line[slot, h].astype(f32)
+            total = mine[h].astype(f32)
+            for place in range(lines - 1):
+                total = total + from_line[place, h].astype(f32)
             final[h] = total.astype(bf16)
-        for zs in order:
-            for copy in to_sibling(zs):
+
+    def close():
+        for j in range(lines):
+            for copy in to_sibling(j):
                 copy.wait_send()
-            for h, i in halves:
-                first(zs, h, i).wait_send()
-                second(zs, h, i).wait_send()
-
-            @pl.when(z != zs)
-            def _():
-                along(zs).wait_send()
+        for j in range(max(0, lines - slots), lines):
+            sent(j)
 
     steps = [(0.0, begin)]
-    for i, zs in enumerate(order):
-        at = 1 + 4 * i
+    for j in range(lines):
+        at = REDUCE_START + REDUCE_STEP * j
         steps += [
-            (at, functools.partial(combine, zs)),
-            (at + 3.2, functools.partial(narrow_down, zs)),
-            (at + 5.4, functools.partial(send_home, zs)),
+            (at, functools.partial(combine, j)),
+            (at + REDUCE_FIRST, functools.partial(narrow_down, j)),
+            (at + REDUCE_SECOND, functools.partial(send_home, j)),
         ]
-    steps.append((99, finish))
-    return [step for _, step in sorted(steps, key=lambda s: s[0])], sorted(at for at, _ in steps)
-
-
-def reduce_scratch(wide, narrow, rows, features):
+    return sorted(steps, key=lambda step: step[0]), finish, close
+
+
+def reduce_scratch(wide, narrow, rows, features, slots=3):
     side, lines = math.isqrt(wide), narrow // 2
     dma = pltpu.SemaphoreType.DMA
+    plane = (lines, 2, side - 1)
     return [
-        pltpu.VMEM((lines, side, side, 2, rows, features), bf16),
-        pltpu.VMEM((lines, side, side, 2, rows, features), bf16),
+        pltpu.VMEM((slots, side, side, 2, rows, features), bf16),
+        pltpu.VMEM((side, side, 2, rows, features), bf16),
         pltpu.VMEM((lines, 2, side - 1, side, rows, features), bf16),
         pltpu.VMEM((lines, 2, side - 1, rows, features), bf16),
         pltpu.VMEM((lines - 1, 2, rows, features), bf16),
-        dma((2, lines)),
-        dma((2, lines)),
-        dma((2, lines)),
-        dma((lines, 2, side - 1)),
-        dma((lines, 2, side - 1)),
-        dma((lines, 2, side - 1)),
-        dma((lines, 2, side - 1)),
+        pltpu.VMEM((2, rows, features), bf16),
+        *[dma(shape) for shape in [(3,), (2, lines), (2, lines), plane, plane, plane, plane]],
         dma((lines,)),
         dma((lines - 1,)),
     ]
-
-
-def backward_kernel(
-    block, rows, items, wide, narrow, qx_ref, kx_ref, q_ref, k_ref, v_ref, o_ref, log_ref, own_ref,
-    parts_ref, proj_parts_ref, grad_ref, final_ref, keys, values, grad_k, grad_v,
-    theirs, own_copied, sent, got, *reduce_refs,
-):
-    width = rows // narrow
-    head, step = pl.program_id(0), pl.program_id(1)
-    moment = head * narrow + step
-    ticks = own_ref.shape[1] * narrow
-    moves, times = reduce_steps(wide, narrow, parts_ref, proj_parts_ref, final_ref, *reduce_refs)
-    w, n = lax.axis_index("wide"), lax.axis_index("narrow")
-
-    def keep():
-        return pltpu.make_async_copy(own_ref.at[n], theirs.at[n], own_copied)
-
-    def deliver(t):
-        to = lax.rem(n + t, narrow)
-        return remote(own_ref.at[to], theirs.at[n], sent.at[t], got.at[n], w, to)
-
-    @pl.when(moment == 0)
-    def _():
-        greet(wide, narrow, w, n)
-        keep().start()
-        for t in range(1, narrow):
-            deliver(t).start()
-
-    def perform(lower, upper):
-        for move, time in zip(moves, times):
-            if lower <= time < upper:
-                move()
-
-    for tick in range(ticks):
-
-        @pl.when(moment == tick)
-        def _():
-            perform(tick, tick + 1)
-
-    @pl.when(step == 0)
-    def _():
-        keys[...] = jnp.concatenate([k_ref[0], kx_ref[...]], axis=0)
-        values[...] = jnp.concatenate([v_ref[0], kx_ref[...]], axis=0)
-        grad_k[...] = jnp.zeros_like(grad_k)
-        grad_v[...] = jnp.zeros_like(grad_v)
-
-    row = lax.broadcasted_iota(jnp.int32, (EXTRA, width), 0) - items
-
-    def pieces(term, base):
-        high = term.astype(bf16).astype(f32)
-        middle = (term - high).astype(bf16).astype(f32)
-        small = term - high - middle
-        return jnp.where(
-            row == 1, high, jnp.where(row == 2, middle, jnp.where(row == 3, small, base))
-        ).astype(bf16)
-
-    owner = lax.rem(n + narrow - step, narrow)
-    columns = pl.ds(pl.multiple_of(owner * width, width), width)
-
-    @pl.when(moment == 0)
-    def _():
-        keep().wait()
-
-    @pl.when(jnp.logical_and(moment > 0, head == 0))
-    def _():
-        arrived(theirs.at[owner], got.at[owner])
-
-    query = q_ref[0, :, columns] * jnp.asarray(0.125, bf16)
-    grad = theirs[owner, head]
-    attended = o_ref[0, :, columns].astype(f32)
-    inner = jnp.sum(grad.astype(f32) * attended, axis=0, keepdims=True)
-    query_wide = jnp.concatenate(
-        [query, pieces(-log_ref[0, :, columns], qx_ref[:, columns].astype(f32))], axis=0
-    ).T
-    grad_wide = jnp.concatenate(
-        [grad, pieces(-inner, jnp.zeros((EXTRA, width), f32))], axis=0
-    ).T
-    grad_q = jnp.zeros((HEAD_DIM, width), f32)
-    for i in range(rows // block):
-        part = pl.ds(i * block, block)
-        probs = jnp.exp(jnp.dot(query_wide, keys[:, part], preferred_element_type=f32))
-        grad_scores = (
-            probs * jnp.dot(grad_wide, values[:, part], preferred_element_type=f32)
-        ).astype(bf16)
-        grad_v[:, part] += jnp.dot(grad, probs.astype(bf16), preferred_element_type=f32)
-        grad_k[:, part] += jnp.dot(query, grad_scores, preferred_element_type=f32)
-        grad_q += lax.dot_general(
-            k_ref[0, :, part], grad_scores, (((1,), (1,)), ((), ())), preferred_element_type=f32
-        )
-    grad_ref[0, 0, :, columns] = (grad_q * 0.125).astype(bf16)
-
-    @pl.when(step == narrow - 1)
-    def _():
-        grad_ref[0, 1] = grad_k[...].astype(bf16)
-        grad_ref[0, 2] = grad_v[...].astype(bf16)
-
-    @pl.when(moment == ticks - 1)
-    def _():
-        perform(ticks, 1000)
-        for t in range(1, narrow):
-            deliver(t).wait_send()
-
-
-def attend_backward(
-    wide, narrow, packed, extras, attended, grad, log_total, parts,
-    proj_parts, items, block=512,
-):
-    heads, _, _, rows = packed.shape
-    piece = (parts.shape[4] + proj_parts.shape[4], parts.shape[5])
-    dma = pltpu.SemaphoreType.DMA
-
-    def whole(j):
-        return pl.BlockSpec((1, None, HEAD_DIM, rows), lambda h, i: (h, j, 0, 0))
-
-    def extra(j):
-        return pl.BlockSpec((None, EXTRA, rows), lambda h, i: (j, 0, 0))
-
-    anywhere = pl.BlockSpec(memory_space=pl.ANY)
-    return pl.pallas_call(
-        functools.partial(backward_kernel, block, rows, items, wide, narrow),
-        grid=(heads, narrow),
-        in_specs=[
-            extra(0),
-            extra(1),
-            whole(0),
-            whole(1),
-            whole(2),
-            pl.BlockSpec((1, HEAD_DIM, rows), lambda h, i: (h, 0, 0)),
-            pl.BlockSpec((1, 1, rows), lambda h, i: (h, 0, 0)),
-            anywhere,
-            anywhere,
-            anywhere,
-        ],
-        out_specs=(
-            pl.BlockSpec((1, 3, HEAD_DIM, rows), lambda h, i: (h, 0, 0, 0)),
-            pl.BlockSpec((2, *piece), lambda h, i: (0, 0, 0)),
-        ),
-        out_shape=(
-            jax.ShapeDtypeStruct((heads, 3, HEAD_DIM, rows), bf16),
-            jax.ShapeDtypeStruct((2, *piece), bf16),
-        ),
-        scratch_shapes=[
-            pltpu.VMEM((HEAD_DIM + EXTRA, rows), bf16),
-            pltpu.VMEM((HEAD_DIM + EXTRA, rows), bf16),
-            pltpu.VMEM((HEAD_DIM, rows), f32),
-            pltpu.VMEM((HEAD_DIM, rows), f32),
-            pltpu.VMEM(grad.shape, bf16),
-            dma(()),
-            dma((narrow,)),
-            dma((narrow,)),
-            *reduce_scratch(wide, narrow, *piece),
-        ],
-        compiler_params=pltpu.CompilerParams(
-            vmem_limit_bytes=58 << 20, collective_id=2, has_side_effects=True
-        ),
-        cost_estimate=pl.CostEstimate(
-            flops=10 * heads * rows * rows * 256,
-            bytes_accessed=heads * rows * HEAD_DIM * 16,
-            transcendentals=heads * rows * rows,
-        ),
-        name="attend_backward",
-    )(extras, extras, packed, packed, packed, attended, log_total, grad, parts, proj_parts)
 
 
 def as_row(ref):
@@ -702,128 +554,293 @@
     )(attended, proj, tokens, cotangent, gain, bias, up_all, down_all)
 
 
-def finish_kernel(
-    wide, narrow, chunks,
-    packed_ref, weight_ref, normed_ref, token_ref, middle_ref, gain_ref, norm_ref, piece_ref,
-    tokens_out, qkv_out, shard_out, norms_out,
-    normed, held, for_sibling, from_sibling, from_line, total_qkv, own_qkv, first_qkv, second_qkv,
-    half_qkv, norms, norm_column, norm_half, norm_plane,
-    loaded, copied, sib_sent, sib_got, line_sent, line_got, piece_sent, piece_got,
-    first_sent, first_got, second_sent, second_got, column_sent, column_got, plane_sent, plane_got,
+def backward_kernel(
+    wide, narrow, items, chunks,
+    extra_ref, packed_ref, att_ref, log_ref, own_ref, parts_ref, proj_parts_ref, weight_ref,
+    normed_ref, token_ref, middle_ref, gain_ref, norm_ref,
+    tokens_out, qkv_out, shard_out, norms_out, landed,
+    keys, values, queries, grads, grad_q, grad_k, grad_v, block_grad,
+    normed, total_qkv, for_sibling, from_sibling, held, from_line,
+    first_qkv, second_qkv, norms, norm_column, norm_half, norm_plane, piece,
+    middle,
+    packed_got, own_got, do_sent, do_got, normed_got, middle_got, copied, sib_sent, sib_got,
+    line_sent, line_got, piece_sent, piece_got, first_sent, first_got, second_sent, second_got,
+    column_sent, column_got, plane_sent, plane_got, *reduce_refs,
 ):
     w, n = lax.axis_index("wide"), lax.axis_index("narrow")
     side, lines = math.isqrt(wide), narrow // 2
     a, b, z, core = w // side, lax.rem(w, side), n // 2, lax.rem(n, 2)
     sibling = n + 1 - 2 * core
-    rows, features = held.shape[1:]
+    heads = keys.shape[0]
+    rows, features = token_ref.shape
     step = rows // chunks
-    load = pltpu.make_async_copy(normed_ref, normed, loaded)
-    load.start()
+    lower = z < lines // 2
+    moves, reduce_finish, reduce_close = reduce_steps(
+        wide, narrow, parts_ref, proj_parts_ref, landed, piece, *reduce_refs
+    )
+
+    def line_at(k):
+        climbing = jnp.where(
+            k < lines - 1 - z, lines - 1 - k, jnp.where(k < lines - 1, k - (lines - 1 - z), z)
+        )
+        falling = jnp.where(k < z, k, jnp.where(k < lines - 1, lines - 1 - (k - z), z))
+        return jnp.where(lower, climbing, falling)
+
+    def block_at(j):
+        odd = lax.rem(j, 2)
+        return 2 * line_at(j // 2) + jnp.where(odd == 1, core, 1 - core)
+
+    def columns(owner):
+        return pl.ds(pl.multiple_of(owner * rows, rows), rows)
+
+    def packed_copy(h, j):
+        into = (queries, keys, values)[j]
+        return pltpu.make_async_copy(
+            packed_ref.at[h, j], into.at[h, pl.ds(0, HEAD_DIM)], packed_got.at[h, j]
+        )
+
+    def keep(h):
+        return pltpu.make_async_copy(
+            own_ref.at[n, h], grads.at[h, pl.ds(0, HEAD_DIM), columns(n)], own_got.at[h]
+        )
+
+    def deliver(t, h):
+        to = lax.rem(n + t, narrow)
+        return remote(
+            own_ref.at[to, h], grads.at[h, pl.ds(0, HEAD_DIM), columns(n)],
+            do_sent.at[t, h], do_got.at[n, h], w, to,
+        )
+
+    def fetch(j):
+        owner = block_at(j)
+        return pltpu.make_async_copy(
+            normed_ref.at[pl.ds(pl.multiple_of(owner * rows, rows), rows)],
+            normed.at[lax.rem(j, 2)], normed_got.at[lax.rem(j, 2)],
+        )
+
+    for h in range(heads):
+        for j in range(3):
+            packed_copy(h, j).start()
+        keep(h).start()
+    fetch(0).start()
     greet(wide, narrow, w, n)
-
-    keep = pltpu.make_async_copy(piece_ref, shard_out.at[w], copied)
-    keep.start()
-
-    def spread(t):
-        return remote(
-            piece_ref, shard_out.at[w], piece_sent.at[t], piece_got.at[t], lax.rem(w + t, wide), n
-        )
-
-    for t in range(1, wide):
-        spread(t).start()
-
-    lower = z < lines // 2
-    order = [jnp.where(lower, lines - 1 - k, k) for k in range(lines)]
-
-    def block(owner):
-        columns = pl.ds(pl.multiple_of(owner * rows, rows), rows)
-        return lax.dot_general(
-            packed_ref[:, columns], weight_ref[...], (((0,), (0,)), ((), ())),
-            preferred_element_type=f32,
+    for t in range(1, narrow):
+        for h in range(heads):
+            deliver(t, h).start()
+    grad_q[...] = jnp.zeros_like(grad_q)
+    grad_k[...] = jnp.zeros_like(grad_k)
+    grad_v[...] = jnp.zeros_like(grad_v)
+    total_qkv[...] = jnp.zeros_like(total_qkv)
+    for h in range(heads):
+        keys[h, HEAD_DIM:, :] = extra_ref[1]
+        values[h, HEAD_DIM:, :] = extra_ref[1]
+    for h in range(heads):
+        for j in range(3):
+            packed_copy(h, j).wait()
+        keep(h).wait()
+
+    row = lax.broadcasted_iota(jnp.int32, (EXTRA, rows), 0) - items
+
+    def pieces(term, base):
+        high = term.astype(bf16).astype(f32)
+        mid = (term - high).astype(bf16).astype(f32)
+        small = term - high - mid
+        return jnp.where(
+            row == 1, high, jnp.where(row == 2, mid, jnp.where(row == 3, small, base))
         ).astype(bf16)
 
-    def to_sibling(zs):
-        return remote(
-            for_sibling.at[zs], from_sibling.at[zs], sib_sent.at[zs], sib_got.at[zs], w, sibling
+    def prepare(j):
+        owner = block_at(j)
+        where = columns(owner)
+
+        @pl.when(owner != n)
+        def _():
+            for h in range(heads):
+                arrived(grads.at[h, pl.ds(0, HEAD_DIM), where], do_got.at[owner, h])
+
+        for h in range(heads):
+            grad = grads[h, 0:HEAD_DIM, where].astype(f32)
+            inner = jnp.sum(grad * att_ref[h, :, where].astype(f32), axis=0, keepdims=True)
+            grads[h, HEAD_DIM:, where] = pieces(-inner, jnp.zeros((EXTRA, rows), f32))
+            queries[h, HEAD_DIM:, where] = pieces(
+                -log_ref[h, :, where], extra_ref[0, :, where].astype(f32)
+            )
+
+    def to_sibling(zs, slot):
+        return remote(
+            for_sibling.at[slot], from_sibling.at[zs], sib_sent.at[slot], sib_got.at[zs], w, sibling
         )
 
     def pass_on(zs, c, up):
         part = pl.ds(c * step, step)
-        slot = zs if up else jnp.where(z - 1 == zs, lines, zs)
-        to = n + 2 if up else n - 2
-        return remote(
-            held.at[zs, part], from_line.at[slot, part], line_sent.at[zs, c], line_got.at[slot, c], w, to
-        )
-
-    def merge(zs):
-        arrived(from_sibling.at[zs], sib_got.at[zs])
-        accumulate(held.at[zs], from_sibling.at[zs])
-
-    flight = 2
-
-    def fed(k):
-        t, c = divmod(k, chunks)
-
-        @pl.when(z == 0)
-        def _():
-            pass_on(lines - 1 - t, c, True).wait_send()
-
-        @pl.when(z == lines - 1)
-        def _():
-            pass_on(t, c, False).wait_send()
-
-    def feed(k):
-        t, c = divmod(k, chunks)
-        if k >= flight:
-            fed(k - flight)
-
-        @pl.when(z == 0)
-        def _():
-            pass_on(lines - 1 - t, c, True).start()
-
-        @pl.when(z == lines - 1)
-        def _():
-            pass_on(t, c, False).start()
-
-    for i, zs in enumerate(order):
-        for_sibling[zs] = block(2 * zs + 1 - core)
-        to_sibling(zs).start()
-        held[zs] = block(2 * zs + core)
-        if i >= 1:
-            merge(order[i - 1])
-        if i == 1:
-            for k in range(flight):
-                feed(k)
-    merge(order[-1])
-
-    load.wait()
-    total_qkv[...] = jnp.dot(packed_ref[...], normed[...], preferred_element_type=f32)
+        place = zs if up else jnp.where(z - 1 == zs, lines, zs)
+        return remote(
+            held.at[zs, part], from_line.at[place, part], line_sent.at[zs, c],
+            line_got.at[place, c], w, n + 2 if up else n - 2,
+        )
+
+    def relay(zs, c, up):
+        part = pl.ds(c * step, step)
+        arrived(from_line.at[zs, part], line_got.at[zs, c])
+        accumulate(held.at[zs, part], from_line.at[zs, part])
+        pass_on(zs, c, up).start()
+
+    def early_relay():
+        @pl.when(jnp.logical_and(lower, z >= 1))
+        def _():
+            for c in range(chunks):
+                relay(lines - 1, c, True)
+
+        @pl.when(jnp.logical_and(z >= lines // 2, z <= lines - 2))
+        def _():
+            for c in range(chunks):
+                relay(0, c, False)
+
+    def emit(j):
+        j = jnp.asarray(j, jnp.int32)
+        owner = block_at(j)
+        where = columns(owner)
+        for h in range(heads):
+            for k, total in enumerate((grad_q, grad_k, grad_v)):
+                at = (h * 3 + k) * HEAD_DIM
+                value = total[h, :, where]
+                block_grad[at : at + HEAD_DIM, :] = (
+                    value * HEAD_DIM**-0.5 if k == 0 else value
+                ).astype(bf16)
+        zs, slot = line_at(j // 2), lax.rem(j // 2, 2)
+        product = contract(block_grad[...], weight_ref[...], 0, 0).astype(bf16)
+
+        @pl.when(lax.rem(j, 2) == 0)
+        def _():
+            @pl.when(j >= 4)
+            def _():
+                to_sibling(zs, slot).wait_send()
+
+            for_sibling[slot] = product
+            to_sibling(zs, slot).start()
+
+        @pl.when(lax.rem(j, 2) == 1)
+        def _():
+            held[zs] = product
+
+        fetch(j).wait()
+
+        @pl.when(j < narrow - 1)
+        def _():
+            fetch(j + 1).start()
+
+        total_qkv[...] += jnp.dot(
+            block_grad[...], normed[lax.rem(j, 2)], preferred_element_type=f32
+        )
+
+        @pl.when(lax.rem(j, 2) == 1)
+        def _():
+            arrived(from_sibling.at[zs], sib_got.at[zs])
+            accumulate(held.at[zs], from_sibling.at[zs])
+
+            @pl.when(jnp.logical_and(z == 0, zs != z))
+            def _():
+                for c in range(chunks):
+                    pass_on(zs, c, True).start()
+
+            @pl.when(jnp.logical_and(z == lines - 1, zs != z))
+            def _():
+                for c in range(chunks):
+                    pass_on(zs, c, False).start()
+
+    def spread(t):
+        return remote(
+            piece, shard_out.at[w], piece_sent.at[t], piece_got.at[t], lax.rem(w + t, wide), n
+        )
+
+    stay = pltpu.make_async_copy(piece, shard_out.at[w], copied)
+
+    def spread_all():
+        reduce_finish()
+        stay.start()
+        for t in range(1, wide):
+            spread(t).start()
+
+    prepare(narrow - 1)
+    pairs = narrow * narrow
+    moves = moves + [(6 * narrow - 8 + EARLY_RELAY, early_relay), (pairs - SPREAD_AT, spread_all)]
+    moves.sort(key=lambda move: move[0])
+    ticks = {}
+    for time, move in moves:
+        ticks.setdefault(min(int(time), pairs - 1), []).append(move)
+
+    def pair(p, carry):
+        for tick, group in ticks.items():
+
+            @pl.when(p == tick)
+            def _():
+                for move in group:
+                    move()
+
+        late = p - 2 * narrow
+        stage = sum(
+            (late >= j * (2 * narrow - 2 - j)).astype(jnp.int32) for j in range(1, narrow - 2)
+        )
+        r = late - stage * (2 * narrow - 2 - stage)
+        across = r < narrow - stage
+        near = late < 0
+        qi = jnp.where(
+            near,
+            jnp.where(p < narrow, narrow - 1, narrow - 2),
+            jnp.where(across, stage, 2 * stage + 1 + r - narrow),
+        )
+        ki = jnp.where(near, lax.rem(p, narrow), jnp.where(across, stage + r, stage))
+
+        @pl.when((p == narrow) | (late == 0) | ((stage == 0) & (r >= narrow)))
+        def _():
+            prepare(qi)
+
+        at_q, at_k = columns(block_at(qi)), columns(block_at(ki))
+        for h in range(heads):
+            probs = jnp.exp(contract(queries[h, :, at_q], keys[h, :, at_k], 0, 0))
+            scores = (probs * contract(grads[h, :, at_q], values[h, :, at_k], 0, 0)).astype(bf16)
+            grad_v[h, :, at_k] += jnp.dot(
+                grads[h, 0:HEAD_DIM, at_q], probs.astype(bf16), preferred_element_type=f32
+            )
+            grad_k[h, :, at_k] += jnp.dot(
+                queries[h, 0:HEAD_DIM, at_q], scores, preferred_element_type=f32
+            )
+            grad_q[h, :, at_q] += contract(keys[h, 0:HEAD_DIM, at_k], scores, 1, 1)
+
+        @pl.when(r == 2 * (narrow - stage) - 4)
+        def _():
+            emit(stage)
+
+        return carry
+
+    lax.fori_loop(0, pairs, pair, 0)
+    emit(narrow - 2)
+    emit(narrow - 1)
+
     half = total_qkv.shape[0] // 2
+    own_qkv, half_qkv = for_sibling.at[:, 0:half], normed.at[:, 0:half]
+    for slot in range(min(2, lines)):
+        to_sibling(0, slot).wait_send()
     for h in (0, 1):
         own_qkv[h] = total_qkv[h * half : (h + 1) * half].astype(bf16)
-
-    def along(h, i):
+    halves = [(h, i) for i in range(1, side) for h in (0, 1)]
+
+    def plane_at(h, i):
         if h == 0:
             return lax.rem(a + i, side) * side + b
         return a * side + lax.rem(b + i, side)
 
-    halves = [(h, i) for i in range(1, side) for h in (0, 1)]
-
     def first(h, i):
         return remote(
             own_qkv.at[h], first_qkv.at[h, i - 1], first_sent.at[h, i - 1], first_got.at[h, i - 1],
-            along(h, i), n,
+            plane_at(h, i), n,
         )
 
     def second(h, i):
         return remote(
-            half_qkv.at[h], second_qkv.at[h, i - 1], second_sent.at[h, i - 1], second_got.at[h, i - 1],
-            along(1 - h, i), n,
-        )
-
-    def qkv_first():
-        for h, i in halves:
-            first(h, i).start()
+            half_qkv.at[h], second_qkv.at[h, i - 1], second_sent.at[h, i - 1],
+            second_got.at[h, i - 1], plane_at(1 - h, i), n,
+        )
 
     def qkv_second():
         for h, i in halves:
@@ -845,39 +862,36 @@
                 total = total + second_qkv[h, i - 1].astype(f32)
             qkv_out[h * half : (h + 1) * half] = total.astype(bf16)
 
-    qkv_first()
+    for h, i in halves:
+        first(h, i).start()
+
+    def fetch_middle(c):
+        return pltpu.make_async_copy(middle_ref.at[pl.ds(c * step, step)], middle, middle_got)
+
+    fetch_middle(0).start()
     for t in range(1, lines):
         below, above = lines - 1 - (t - z), t - (lines - 1 - z)
         for c in range(chunks):
-            part = pl.ds(c * step, step)
-            k = (t - 1) * chunks + c + flight
-            if k < (lines - 1) * chunks:
-                feed(k)
             if t < lines - 1:
 
-                @pl.when(jnp.logical_and(z >= 1, t >= z))
+                @pl.when((z >= 1) & (t >= z) & ~(lower & (t == z)))
                 def _():
-                    arrived(from_line.at[below, part], line_got.at[below, c])
-                    accumulate(held.at[below, part], from_line.at[below, part])
-                    pass_on(below, c, True).start()
-
-                @pl.when(jnp.logical_and(z <= lines - 2, above >= 0))
+                    relay(below, c, True)
+
+                @pl.when((z <= lines - 2) & (above >= 0) & ~((z >= lines // 2) & (above == 0)))
                 def _():
-                    arrived(from_line.at[above, part], line_got.at[above, c])
-                    accumulate(held.at[above, part], from_line.at[above, part])
-                    pass_on(above, c, False).start()
-        if t == 1:
-            qkv_second()
-        if t == min(2, lines - 1):
-            qkv_last()
-
-    def zero_edges(at_edge, slot):
+                    relay(above, c, False)
+
+    qkv_second()
+
+    def zero_edges(at_edge, place):
         @pl.when(at_edge)
         def _():
-            from_line[slot] = jnp.zeros((rows, features), bf16)
+            from_line[place] = jnp.zeros((rows, features), bf16)
 
     zero_edges(z == 0, z)
     zero_edges(z == lines - 1, lines)
+    gain_sum = bias_sum = jnp.zeros((1, features), f32)
     for c in range(chunks):
         part = pl.ds(c * step, step)
 
@@ -888,10 +902,13 @@
         @pl.when(z <= lines - 2)
         def _():
             arrived(from_line.at[lines, part], line_got.at[lines, c])
+
+        fetch_middle(c).wait()
 
         def norm_rows(j, carry):
             gain_sum, bias_sum = carry
             few = pl.ds(pl.multiple_of(c * step + j * 32, 32), 32)
+            near = pl.ds(pl.multiple_of(j * 32, 32), 32)
             grad = (
                 held[z, few].astype(f32)
                 + from_line[z, few].astype(f32)
@@ -907,17 +924,14 @@
                 - jnp.mean(term, axis=-1, keepdims=True)
                 - scaled * jnp.mean(term * scaled, axis=-1, keepdims=True)
             )
-            tokens_out[few, :] = (middle_ref[few, :] + back).astype(bf16)
+            tokens_out[few, :] = (middle[near, :] + back).astype(bf16)
             gain_sum = gain_sum + jnp.sum(grad * scaled, axis=0, keepdims=True)
             bias_sum = bias_sum + jnp.sum(grad, axis=0, keepdims=True)
             return gain_sum, bias_sum
 
-        start = (jnp.zeros((1, features), f32), jnp.zeros((1, features), f32))
-        sums = lax.fori_loop(0, step // 32, norm_rows, start)
-        if c == 0:
-            gain_sum, bias_sum = sums
-        else:
-            gain_sum, bias_sum = gain_sum + sums[0], bias_sum + sums[1]
+        gain_sum, bias_sum = lax.fori_loop(0, step // 32, norm_rows, (gain_sum, bias_sum))
+        if c + 1 < chunks:
+            fetch_middle(c + 1).start()
 
     row = lax.broadcasted_iota(jnp.int32, (8, features), 0)
     parts = jnp.where(row == 0, gain_sum, jnp.where(row == 1, bias_sum, norm_ref[...]))
@@ -951,86 +965,109 @@
         total = total + norm_plane[t - 1]
     norms_out[...] = total
 
-    keep.wait()
+    qkv_last()
+    stay.wait()
+    reduce_close()
     for t in range(1, wide):
         spread(t).wait_send()
         arrived(shard_out.at[lax.rem(w + wide - t, wide)], piece_got.at[t])
         over_plane(t).wait_send()
     for t in range(1, narrow):
         down_column(t).wait_send()
+        for h in range(heads):
+            deliver(t, h).wait_send()
     for h, i in halves:
         first(h, i).wait_send()
         second(h, i).wait_send()
-    for zs in order:
-        to_sibling(zs).wait_send()
-    for k in range(flight):
-        fed((lines - 1) * chunks - 1 - k)
     for zs in range(lines):
         for c in range(chunks):
 
-            @pl.when(jnp.logical_and(z >= 1, zs > z))
+            @pl.when(zs > z)
             def _():
                 pass_on(zs, c, True).wait_send()
 
-            @pl.when(jnp.logical_and(z <= lines - 2, zs < z))
+            @pl.when(zs < z)
             def _():
                 pass_on(zs, c, False).wait_send()
 
 
-def finish(wide, narrow, packed, weight, normed, tokens, middle, gain, norm_parts, piece, chunks=4):
+def backward(
+    wide, narrow, extras, packed, attended, log_total, grad, parts, proj_parts, weight, normed,
+    tokens, middle, gain, norm_parts, items, chunks=4,
+):
     side, lines = math.isqrt(wide), narrow // 2
+    heads, _, _, total_rows = packed.shape
     rows, features = tokens.shape
-    columns = packed.shape[0]
+    held_columns = weight.shape[0]
+    piece = (parts.shape[4] + proj_parts.shape[4], features)
+    depth = HEAD_DIM + EXTRA
     dma = pltpu.SemaphoreType.DMA
     vmem = pl.BlockSpec(memory_space=pltpu.VMEM)
     anywhere = pl.BlockSpec(memory_space=pl.ANY)
+    plane = (2, side - 1)
     return pl.pallas_call(
-        functools.partial(finish_kernel, wide, narrow, chunks),
-        in_specs=[vmem, vmem, anywhere, vmem, vmem, vmem, vmem, anywhere],
-        out_specs=(vmem, vmem, anywhere, vmem),
+        functools.partial(backward_kernel, wide, narrow, items, chunks),
+        in_specs=[
+            vmem, anywhere, vmem, vmem, anywhere, anywhere, anywhere, vmem,
+            anywhere, vmem, anywhere, vmem, vmem,
+        ],
+        out_specs=(vmem, vmem, anywhere, vmem, anywhere),
         out_shape=(
             jax.ShapeDtypeStruct((rows, features), bf16),
-            jax.ShapeDtypeStruct((columns, features), bf16),
-            jax.ShapeDtypeStruct((wide, *piece.shape), bf16),
+            jax.ShapeDtypeStruct((held_columns, features), bf16),
+            jax.ShapeDtypeStruct((wide, 2, *piece), bf16),
             jax.ShapeDtypeStruct((8, features // narrow), f32),
+            jax.ShapeDtypeStruct((lines, side, side, 2, *piece), bf16),
         ),
         scratch_shapes=[
-            pltpu.VMEM(normed.shape, bf16),
-            pltpu.VMEM((lines, rows, features), bf16),
+            *[pltpu.VMEM((heads, depth, total_rows), bf16)] * 4,
+            *[pltpu.VMEM((heads, HEAD_DIM, total_rows), f32)] * 3,
+            pltpu.VMEM((held_columns, rows), bf16),
+            pltpu.VMEM((2, rows, features), bf16),
+            pltpu.VMEM((held_columns, features), f32),
+            pltpu.VMEM((2, rows, features), bf16),
             pltpu.VMEM((lines, rows, features), bf16),
             pltpu.VMEM((lines, rows, features), bf16),
             pltpu.VMEM((lines + 1, rows, features), bf16),
-            pltpu.VMEM((columns, features), f32),
-            pltpu.VMEM((2, columns // 2, features), bf16),
-            pltpu.VMEM((2, side - 1, columns // 2, features), bf16),
-            pltpu.VMEM((2, side - 1, columns // 2, features), bf16),
-            pltpu.VMEM((2, columns // 2, features), bf16),
+            pltpu.VMEM((2, side - 1, held_columns // 2, features), bf16),
+            pltpu.VMEM((2, side - 1, held_columns // 2, features), bf16),
             pltpu.VMEM((narrow, 8, features // narrow), f32),
             pltpu.VMEM((narrow - 1, 8, features // narrow), f32),
             pltpu.VMEM((8, features // narrow), f32),
             pltpu.VMEM((wide - 1, 8, features // narrow), f32),
+            pltpu.VMEM((2, *piece), bf16),
+            pltpu.VMEM((rows // chunks, features), f32),
+            dma((heads, 3)),
+            dma((heads,)),
+            dma((narrow, heads)),
+            dma((narrow, heads)),
+            dma((2,)),
             dma(()),
             dma(()),
-            dma((lines,)),
+            dma((2,)),
             dma((lines,)),
             dma((lines, chunks)),
             dma((lines + 1, chunks)),
             dma((wide,)),
             dma((wide,)),
-            dma((2, side - 1)),
-            dma((2, side - 1)),
-            dma((2, side - 1)),
-            dma((2, side - 1)),
+            dma(plane),
+            dma(plane),
+            dma(plane),
+            dma(plane),
             dma((narrow - 1,)),
             dma((narrow - 1,)),
             dma((wide - 1,)),
             dma((wide - 1,)),
+            *reduce_scratch(wide, narrow, *piece),
         ],
         compiler_params=pltpu.CompilerParams(
-            vmem_limit_bytes=58 << 20, collective_id=3, has_side_effects=True
+            vmem_limit_bytes=61 << 20, collective_id=2, has_side_effects=True
         ),
-        name="finish",
-    )(packed, weight, normed, tokens, middle, gain, norm_parts, piece)
+        name="backward",
+    )(
+        extras, packed, attended, log_total, grad, parts, proj_parts, weight, normed,
+        tokens, middle, gain, norm_parts,
+    )
 
 
 def unpack_kernel(shard_ref, qkv_ref, qkv_out, proj_out, up_out, down_out):
@@ -1304,9 +1341,12 @@
 
     def project(owner, c):
         columns = pl.ds(pl.multiple_of(owner * rows + c * step, step), step)
-        packed[:, columns] = contract(
-            turned[...], normed[owner, pl.ds(c * step, step)], 1, 1
-        ).astype(bf16)
+        product = contract(turned[...], normed[owner, pl.ds(c * step, step)], 1, 1).astype(bf16)
+        for j in range(product.shape[0] // HEAD_DIM):
+            part = product[j * HEAD_DIM : (j + 1) * HEAD_DIM]
+            if j % 3 == 0:
+                part = part * jnp.asarray(HEAD_DIM**-0.5, bf16)
+            packed[j * HEAD_DIM : (j + 1) * HEAD_DIM, columns] = part
 
     gather.begin()
     for c in range(CHUNKS):
@@ -1439,14 +1479,9 @@
     )
     grad_attended = grad_attended.reshape(narrow, heads, HEAD_DIM, -1)
     grad_proj_parts = split_parts(grad_proj)
-    grad_packed, grad_piece = attend_backward(
-        wide, narrow, packed, extras, attended, grad_attended, log_total,
-        grad_parts, grad_proj_parts, items,
-    )
-    grad_packed = grad_packed.reshape(heads * 3 * HEAD_DIM, rows)
-    grad_tokens, grad_qkv, grad_shard, shares = finish(
-        wide, narrow, grad_packed, qkv_turned, normed_all, tokens, grad_middle,
-        attn_gain, norm_parts, grad_piece,
+    grad_tokens, grad_qkv, grad_shard, shares, _ = backward(
+        wide, narrow, extras, packed, attended, log_total, grad_attended, grad_parts,
+        grad_proj_parts, qkv_turned, normed_all, tokens, grad_middle, attn_gain, norm_parts, items,
     )
     grad_qkv, grad_proj, grad_up, grad_down = unpack(
         grad_shard, grad_qkv, proj_weight.shape, up_weight.shape, down_weight.shape

time: 456 us -> 417 us (0.914)
  Pallas kernels: 441 us -> 402 us
    pallas_call x2 -> x1, Pallas kernels: 221 us -> 182 us  [backward(): pl.pallas_call(functools.partial(backward_kernel, wide, narrow, items, ch...]
where the time goes in v6:
time: 417 us
  Pallas kernels  402 us (96%)
  local copies, waits for them, and re-layouts  9.76 us (2%)
    pallas_call x1, Pallas kernels, backward(): pl.pallas_call(functools.partial(backward_kernel, wide, narrow, items, ch...  182 us
    pallas_call x1, Pallas kernels, start(): pl.pallas_call(functools.partial(start_kernel, wide, narrow), in_specs=[v...  105 us
    pallas_call x1, Pallas kernels, attend_forward(): pl.pallas_call(functools.partial(forward_kernel, wide, narrow), grid=(hea...  68.5 us
    pallas_call x1, Pallas kernels, mlp(): pl.pallas_call(mlp_kernel, grid=(narrow,), in_specs=[whole(*attended.shap...  43.4 us

profile of v6, /device:TPU:0, one launch (start us, length us, event | category | flops | bytes accessed | tf_op | source)
XLA Modules:
  0.0 416.6 jit_solution(517414853846810942)
XLA Ops:
  0.7 1.4 fusion.2
  4.7 0.7 convert_add_fusion
  5.3 0.1 fusion.1
  5.5 0.8 select_convert_fusion.qx_ref.kx_ref.extra_ref
  6.2 104.9 %start.1 = (bf16[8,512,1024]{2,1,0:T(8,128)(2,1)}, bf16[384,4096]{1,0:T(8,128)(2,1)}, bf16[384,1024]{1,0:T(8,128)(2,1)}, bf16[8,2,2,2,128,512]{5,4,3,2,1,0:T(8,128)(2,1)}) custom-call(bf16[512,1024]{1,0:T(8,128)(2,1)} %token_ref.5, bf16[1024]{0:T(1024)(128)(2,1)} %gain_ref.5, bf16[1024]{0:T(1024)(128)(2,1)} %bias_ref.2, bf16[1024,384]{1,0:T(8,128)(2,1)} %weight_ref.1, ...), custom_call_target="tpu_custom_call" | custom-call | tf_op jit(solution)/shard_map/start/pallas_call | solution.py:1428
  111.2 68.5 %attend_forward.1 = (bf16[2,64,4096]{2,1,0:T(8,128)(2,1)}, f32[2,1,4096]{2,1,0:T(1,128)}, bf16[8,2,64,512]{3,2,1,0:T(8,128)(2,1)}, bf16[8,2,2,2,80,1024]{5,4,3,2,1,0:T(8,128)(2,1)}) custom-call(bf16[2,16,4096]{2,1,0:T(8,128)(2,1)} %select_convert_fusion.qx_ref.kx_ref.extra_ref, bf16[2,16,4096]{2,1,0:T(8,128)(2,1)} %select_convert_fusion.qx_ref.kx_ref.extra_ref, ...), custom_call_target="tpu_custom_call" | custom-call | tf_op jit(solution)/shard_map/attend_forward/pallas_call | solution.py:132
  179.7 3.2 slice.41
  182.9 43.4 %mlp.1 = (bf16[512,1024]{1,0:T(8,128)(2,1)}, f32[512,1024]{1,0:T(8,128)}, bf16[1024,512]{1,0:T(8,128)(2,1)}, bf16[1024,1024]{1,0:T(8,128)(2,1)}, bf16[8,2,2,2,12...) custom-call(bf16[1024,512]{1,0:T(8,128)(2,1)} %bitcast.29, bf16[1024,1024]{1,0:T(8,128)(2,1)} %bitcast.25, ...), custom_call_target="tpu_custom_call" | custom-call | tf_op jit(solution)/shard_map/mlp/pallas_call | solution.py:515
  226.4 182.2 %backward.1 = (bf16[512,1024]{1,0:T(8,128)(2,1)}, bf16[384,1024]{1,0:T(8,128)(2,1)}, bf16[4,2,144,1024]{3,2,1,0:T(8,128)(2,1)}, f32[8,128]{1,0:T(8,128)}, bf16[4,2,2,2,144,1024]{5,4,3,2,1,0:T(8,128)(2,1)}) custom-call(bf16[2,16,4096]{2,1,0:T(8,128)(2,1)} %select_convert_fusion.qx_ref.kx_ref.extra_ref, bf16[2,3,64,4096]{3,2,1,0:T(8,128)(2,1)} %bitcast.24, ...), custom_call_target="tpu_custom_call" | custom-call | tf_op jit(solution)/shard_map/backward/pallas_call | solution.py:1008
  408.6 1.3 slice_bitcast_fusion
  409.9 0.0 copy-start
  409.9 1.7 copy-done
  411.6 0.0 copy-start.1
  411.6 1.1 copy-done.1
  412.7 0.0 copy-start.2
  412.7 2.9 unpack.1
  415.7 0.0 copy-done.2
  415.7 1.0 copy.22
  (3 shorter events, 0.0 us)
Async XLA Ops:
  409.9 1.7 copy-start
  411.6 1.1 copy-start.1
  412.7 3.0 copy-start.2

commit v7 on v6

--- a/solution.py
+++ b/solution.py
@@ -20,20 +20,20 @@
 epsilon = 1e-05
 
 
-def mask_rows(item_lengths, rows):
-    lengths = item_lengths[0]
-    items = lengths.shape[0]
-    ends = [sum(lengths[j] for j in range(i + 1)) for i in range(items)]
-    position = jnp.arange(rows)
-    segment = sum((position >= ends[i]).astype(jnp.int32) for i in range(items))
-    extra = jnp.arange(EXTRA)[:, None]
-    own = segment[None, :] == extra
-    mask = extra <= items
-    query_extra = jnp.where(own & mask, 1.0, 0.0)
-    key_extra = jnp.where(
-        mask, jnp.where(own, 0.0, EXCLUDED), jnp.where(extra <= items + 3, 1.0, 0.0)
-    )
-    return jnp.where(jnp.arange(2)[:, None, None] == 0, query_extra, key_extra).astype(bf16)
+def mask_rows(length_ref, extras):
+    items = length_ref.shape[1]
+    rows = extras.shape[2]
+    position = lax.broadcasted_iota(jnp.int32, (EXTRA, rows), 1)
+    extra = lax.broadcasted_iota(jnp.int32, (EXTRA, rows), 0)
+    segment, end = jnp.zeros((EXTRA, rows), jnp.int32), 0
+    for i in range(items):
+        end = end + length_ref[0, i]
+        segment = segment + jnp.where(position >= end, 1, 0)
+    own = jnp.where(segment == extra, 1.0, 0.0)
+    mask = jnp.where(extra <= items, 1.0, 0.0)
+    ones = jnp.where(extra <= items + 3, 1.0, 0.0) * (1.0 - mask)
+    extras[0] = (own * mask).astype(bf16)
+    extras[1] = ((1.0 - own) * mask * EXCLUDED + ones).astype(bf16)
 
 
 def forward_kernel(
@@ -47,7 +47,7 @@
     width = q_ref.shape[-1] // narrow
     last = heads_of(ready, narrow) * narrow - 1
 
-    moves = [(0.0, lambda: greet(wide, narrow, w, n)), (0.1, gather.begin)]
+    moves = []
     for d in range(1, lines):
         moves += [
             (3.0 * d, functools.partial(gather.sides, d, gather.one)),
@@ -62,15 +62,24 @@
             if lower <= time < upper:
                 move()
 
-    for tick in range(last + 1):
-
-        @pl.when(moment == tick)
-        def _():
-            perform(tick, tick + 1)
+    @pl.when(moment == 0)
+    def _():
+        greet_all(wide, narrow, w, n)
 
     @pl.when(step == 0)
     def _():
         keys[...] = jnp.concatenate([k_ref[0], kx_ref[...]], axis=0).T
+
+    @pl.when(moment == 0)
+    def _():
+        greeted(wide, narrow)
+        gather.begin()
+
+    for tick in range(last + 1):
+
+        @pl.when(moment == tick)
+        def _():
+            perform(tick, tick + 1)
 
     owner = lax.rem(n + 1 + step, narrow)
     columns = pl.ds(pl.multiple_of(owner * width, width), width)
@@ -175,7 +184,7 @@
     pltpu.make_async_copy(ref, ref, semaphore).wait()
 
 
-def greet(wide, narrow, w, n):
+def greet_all(wide, narrow, w, n):
     barrier = pltpu.get_barrier_semaphore()
 
     def column(t, carry):
@@ -192,7 +201,10 @@
 
     lax.fori_loop(1, narrow, column, 0)
     lax.fori_loop(1, wide, plane, 0)
-    pl.semaphore_wait(barrier, narrow + wide - 2)
+
+
+def greeted(wide, narrow):
+    pl.semaphore_wait(pltpu.get_barrier_semaphore(), narrow + wide - 2)
 
 
 def accumulate(into, *others):
@@ -407,9 +419,9 @@
 
 
 def mlp_kernel(
-    att_ref, proj_ref, token_ref, cot_ref, gain_ref, bias_ref, up_ref, down_ref,
+    att_ref, rest_ref, token_ref, cot_ref, gain_ref, bias_ref, up_ref, down_ref,
     out_ref, middle_out, att_out, proj_out, parts_ref, norm_ref,
-    middle, expand, out_total, expand_total,
+    middle, expand, out_total, expand_total, proj_ref, proj_got,
 ):
     step = pl.program_id(0)
     rows, features = token_ref.shape
@@ -421,8 +433,20 @@
 
         return body
 
+    if rest_ref.ndim == 2:
+        fetch = pltpu.make_async_copy(rest_ref, proj_ref, proj_got)
+    else:
+        few_rows = rest_ref.shape[4] - down_ref.shape[4]
+        fetch = pltpu.make_async_copy(
+            rest_ref.at[:, :, :, :, pl.ds(down_ref.shape[4], few_rows)],
+            proj_ref.reshape(*rest_ref.shape[:4], few_rows, features),
+            proj_got,
+        )
+
     @pl.when(step == 0)
     def _():
+        fetch.start()
+        fetch.wait()
         middle[...] = token_ref[...].astype(f32) + contract(att_ref[...], proj_ref[...], 0, 0)
         out_total[...] = jnp.zeros_like(out_total)
         expand_total[...] = jnp.zeros_like(expand_total)
@@ -502,9 +526,10 @@
         proj_out[...] = jnp.dot(att_ref[...], branch, preferred_element_type=f32).astype(bf16)
 
 
-def mlp(attended, proj, tokens, cotangent, gain, bias, up_all, down_all, units):
+def mlp(attended, rest, tokens, cotangent, gain, bias, up_all, down_all, units):
     rows, features = tokens.shape
     narrow, side = up_all.shape[:2]
+    proj_shape = (attended.shape[0], features)
 
     def whole(*shape):
         return pl.BlockSpec(shape, lambda i: (0,) * len(shape))
@@ -517,7 +542,7 @@
         grid=(narrow,),
         in_specs=[
             whole(*attended.shape),
-            whole(*proj.shape),
+            pl.BlockSpec(memory_space=pl.ANY),
             whole(rows, features),
             whole(rows, features),
             whole(*gain.shape),
@@ -529,7 +554,7 @@
             whole(rows, features),
             whole(rows, features),
             whole(*attended.shape),
-            whole(*proj.shape),
+            whole(*proj_shape),
             pl.BlockSpec(
                 (1, side, side, 2, 2 * units, features), lambda i: (i, 0, 0, 0, 0, 0)
             ),
@@ -539,7 +564,7 @@
             jax.ShapeDtypeStruct((rows, features), bf16),
             jax.ShapeDtypeStruct((rows, features), f32),
             jax.ShapeDtypeStruct(attended.shape, bf16),
-            jax.ShapeDtypeStruct(proj.shape, bf16),
+            jax.ShapeDtypeStruct(proj_shape, bf16),
             jax.ShapeDtypeStruct((narrow, side, side, 2, 2 * units, features), bf16),
             jax.ShapeDtypeStruct((8, features), f32),
         ),
@@ -548,10 +573,12 @@
             pltpu.VMEM((rows, features), bf16),
             pltpu.VMEM((rows, features), f32),
             pltpu.VMEM((rows, features), f32),
+            pltpu.VMEM(proj_shape, bf16),
+            pltpu.SemaphoreType.DMA(()),
         ],
         compiler_params=pltpu.CompilerParams(vmem_limit_bytes=58 << 20),
         name="mlp",
-    )(attended, proj, tokens, cotangent, gain, bias, up_all, down_all)
+    )(attended, rest, tokens, cotangent, gain, bias, up_all, down_all)
 
 
 def backward_kernel(
@@ -623,14 +650,15 @@
             packed_copy(h, j).start()
         keep(h).start()
     fetch(0).start()
-    greet(wide, narrow, w, n)
-    for t in range(1, narrow):
-        for h in range(heads):
-            deliver(t, h).start()
+    greet_all(wide, narrow, w, n)
     grad_q[...] = jnp.zeros_like(grad_q)
     grad_k[...] = jnp.zeros_like(grad_k)
     grad_v[...] = jnp.zeros_like(grad_v)
     total_qkv[...] = jnp.zeros_like(total_qkv)
+    greeted(wide, narrow)
+    for t in range(1, narrow):
+        for h in range(heads):
+            deliver(t, h).start()
     for h in range(heads):
         keys[h, HEAD_DIM:, :] = extra_ref[1]
         values[h, HEAD_DIM:, :] = extra_ref[1]
@@ -1304,13 +1332,15 @@
 
 
 def start_kernel(
-    wide, narrow, token_ref, gain_ref, bias_ref, weight_ref, own_ref,
-    normed, packed, turned, gathered, line_sent, line_got, sib_sent, sib_got, *gather_refs,
+    wide, narrow, length_ref, token_ref, gain_ref, bias_ref, weight_ref, own_ref,
+    normed, packed, turned, extras, gathered, line_sent, line_got, sib_sent, sib_got, *gather_refs,
 ):
     gather = Gather(wide, narrow, [own_ref], gathered, *gather_refs)
     w, n, z, core = gather.w, gather.n, gather.z, gather.core
     lines, sibling = gather.lines, gather.sibling
     rows = token_ref.shape[0]
+
+    greet_all(wide, narrow, w, n)
 
     def norm_rows(j, carry):
         part = pl.ds(pl.multiple_of(j * 64, 64), 64)
@@ -1322,9 +1352,6 @@
         ).astype(bf16)
         return carry
 
-    lax.fori_loop(0, rows // 64, norm_rows, 0)
-    greet(wide, narrow, w, n)
-
     step = rows // CHUNKS
 
     def part_of(shard, c):
@@ -1348,8 +1375,12 @@
                 part = part * jnp.asarray(HEAD_DIM**-0.5, bf16)
             packed[j * HEAD_DIM : (j + 1) * HEAD_DIM, columns] = part
 
-    gather.begin()
+    norm_blocks = rows // 64 // CHUNKS
     for c in range(CHUNKS):
+        lax.fori_loop(c * norm_blocks, (c + 1) * norm_blocks, norm_rows, 0)
+        if c == 0:
+            greeted(wide, narrow)
+            gather.begin()
 
         @pl.when(z < lines - 1)
         def _():
@@ -1361,6 +1392,7 @@
 
         hand(z, c).start()
     turned[...] = weight_ref[...].T
+    mask_rows(length_ref, extras)
     for c in range(CHUNKS):
         project(n, c)
 
@@ -1419,7 +1451,7 @@
         gather.sides(d, sent_side)
 
 
-def start(wide, narrow, tokens, gain, bias, weight, own):
+def start(wide, narrow, lengths, tokens, gain, bias, weight, own):
     rows, features = tokens.shape
     lines = narrow // 2
     dma = pltpu.SemaphoreType.DMA
@@ -1427,12 +1459,13 @@
     anywhere = pl.BlockSpec(memory_space=pl.ANY)
     return pl.pallas_call(
         functools.partial(start_kernel, wide, narrow),
-        in_specs=[vmem, vmem, vmem, vmem, anywhere],
-        out_specs=(vmem, vmem, vmem, anywhere),
+        in_specs=[pl.BlockSpec(memory_space=pltpu.SMEM), vmem, vmem, vmem, vmem, anywhere],
+        out_specs=(vmem, vmem, vmem, vmem, anywhere),
         out_shape=(
             jax.ShapeDtypeStruct((narrow, rows, features), bf16),
             jax.ShapeDtypeStruct((weight.shape[1], narrow * rows), bf16),
             jax.ShapeDtypeStruct((weight.shape[1], features), bf16),
+            jax.ShapeDtypeStruct((2, EXTRA, narrow * rows), bf16),
             jax.ShapeDtypeStruct((narrow, *own.shape), bf16),
         ),
         scratch_shapes=[
@@ -1443,7 +1476,7 @@
             vmem_limit_bytes=58 << 20, collective_id=1, has_side_effects=True
         ),
         name="start",
-    )(tokens, gain, bias, weight, own)
+    )(lengths, tokens, gain, bias, weight, own)
 
 
 def body(
@@ -1463,9 +1496,8 @@
         return total.reshape(narrow, side, side, 2, -1, total.shape[1])
 
     first = down_weight.shape[0] // (2 * wide)
-    extras = mask_rows(item_lengths, rows)
-    normed_all, packed, qkv_turned, up_all = start(
-        wide, narrow, tokens, attn_gain, attn_bias, qkv_weight, cut(up_weight)
+    normed_all, packed, qkv_turned, extras, up_all = start(
+        wide, narrow, item_lengths, tokens, attn_gain, attn_bias, qkv_weight, cut(up_weight)
     )
     normed_all = normed_all.reshape(rows, -1)
     packed = packed.reshape(heads, 3, HEAD_DIM, rows)
@@ -1473,7 +1505,9 @@
         wide, narrow, packed, extras, cut(down_weight), cut(proj_weight)
     )
     attended_rows = attended_rows.reshape(-1, tokens.shape[0])
-    proj_all = rest_all[:, :, :, :, first:].reshape(-1, tokens.shape[1])
+    proj_all = rest_all
+    if (rest_all.shape[4] - first) % 16:
+        proj_all = rest_all[:, :, :, :, first:].reshape(-1, tokens.shape[1])
     output, grad_middle, grad_attended, grad_proj, grad_parts, norm_parts = mlp(
         attended_rows, proj_all, tokens, cotangent, mlp_gain, mlp_bias, up_all, rest_all, first
     )

time: 417 us -> 406 us (0.974)
  local copies, waits for them, and re-layouts: 9.76 us -> 5.12 us
    slice x2 -> x0, local copies, waits for them, and re-layouts: 4.64 us -> none  [the longest x1 3.24 us: body(): proj_all = rest_all[:, :, :, :, first:].reshape(-1, tokens.shape[1])]
where the time goes in v7:
time: 406 us
  Pallas kernels  400 us (99%)
  local copies, waits for them, and re-layouts  5.12 us (1%)
    pallas_call x1, Pallas kernels, backward(): pl.pallas_call(functools.partial(backward_kernel, wide, narrow, items, ch...  181 us
    pallas_call x1, Pallas kernels, start(): pl.pallas_call(functools.partial(start_kernel, wide, narrow), in_specs=[p...  103 us
    pallas_call x1, Pallas kernels, attend_forward(): pl.pallas_call(functools.partial(forward_kernel, wide, narrow), grid=(hea...  67.7 us
    pallas_call x1, Pallas kernels, mlp(): pl.pallas_call(mlp_kernel, grid=(narrow,), in_specs=[whole(*attended.shap...  44.6 us

profile of v7, /device:TPU:0, one launch (start us, length us, event | category | flops | bytes accessed | tf_op | source)
XLA Modules:
  0.0 405.9 jit_solution(9783582471098150058)
XLA Ops:
  0.6 103.4 %start.1 = (bf16[8,512,1024]{2,1,0:T(8,128)(2,1)}, bf16[384,4096]{1,0:T(8,128)(2,1)}, bf16[384,1024]{1,0:T(8,128)(2,1)}, bf16[2,16,4096]{2,1,0:T(8,128)(2,1)}, bf16[8,2,2,2,128,512]{5,4,3,2,1,0:T(8,128)(2,1)}) custom-call(s32[1,4]{1,0:T(1,128)} %length_ref.1, bf16[512,1024]{1,0:T(8,128)(2,1)} %token_ref.5, bf16[1024]{0:T(1024)(128)(2,1)} %gain_ref.5, ...), custom_call_target="tpu_custom_call" | custom-call | tf_op jit(solution)/shard_map/start/pallas_call | solution.py:1460
  104.1 67.7 %attend_forward.1 = (bf16[2,64,4096]{2,1,0:T(8,128)(2,1)}, f32[2,1,4096]{2,1,0:T(1,128)}, bf16[8,2,64,512]{3,2,1,0:T(8,128)(2,1)}, bf16[8,2,2,2,80,1024]{5,4,3,2,1,0:T(8,128)(2,1)}) custom-call(bf16[2,16,4096]{2,1,0:T(8,128)(2,1)} %get-tuple-element.33.qx_ref.kx_ref.extra_ref, bf16[2,16,4096]{2,1,0:T(8,128)(2,1)} %get-tuple-element.33.qx_ref.kx_ref.extra_ref, ...), custom_call_target="tpu_custom_call" | custom-call | tf_op jit(solution)/shard_map/attend_forward/pallas_call | solution.py:141
  171.7 44.6 %mlp.1 = (bf16[512,1024]{1,0:T(8,128)(2,1)}, f32[512,1024]{1,0:T(8,128)}, bf16[1024,512]{1,0:T(8,128)(2,1)}, bf16[1024,1024]{1,0:T(8,128)(2,1)}, bf16[8,2,2,2,12...) custom-call(bf16[1024,512]{1,0:T(8,128)(2,1)} %bitcast.23, ...), custom_call_target="tpu_custom_call" | custom-call | tf_op jit(solution)/shard_map/mlp/pallas_call | solution.py:540
  216.4 181.5 %backward.1 = (bf16[512,1024]{1,0:T(8,128)(2,1)}, bf16[384,1024]{1,0:T(8,128)(2,1)}, bf16[4,2,144,1024]{3,2,1,0:T(8,128)(2,1)}, f32[8,128]{1,0:T(8,128)}, bf16[4,2,2,2,144,1024]{5,4,3,2,1,0:T(8,128)(2,1)}) custom-call(bf16[2,16,4096]{2,1,0:T(8,128)(2,1)} %get-tuple-element.33.qx_ref.kx_ref.extra_ref, bf16[2,3,64,4096]{3,2,1,0:T(8,128)(2,1)} %bitcast.19, ...), custom_call_target="tpu_custom_call" | custom-call | tf_op jit(solution)/shard_map/backward/pallas_call | solution.py:1036
  397.8 1.4 slice_bitcast_fusion
  399.2 0.0 copy-start
  399.2 1.7 copy-done
  400.9 0.0 copy-start.1
  400.9 1.1 copy-done.1
  402.0 0.0 copy-start.2
  402.0 2.9 unpack.1
  404.9 0.0 copy-done.2
  404.9 1.0 copy.22
Async XLA Ops:
  399.2 1.7 copy-start
  400.9 1.1 copy-start.1
  402.0 3.0 copy-start.2

commit v8 on v7

--- a/solution.py
+++ b/solution.py
@@ -11,7 +11,7 @@
 HEAD_DIM = 64
 EXTRA = 16
 CHUNKS = 2
-REDUCE_START, REDUCE_STEP, REDUCE_FIRST, REDUCE_SECOND, SPREAD_AT = 2, 11, 8, 12, 8
+REDUCE_START, REDUCE_STEP, REDUCE_FIRST, REDUCE_SECOND, SPREAD_AT = 3, 11, 8, 12, 8
 EARLY_RELAY = 17
 EXCLUDED = -1e30
 bf16 = jnp.bfloat16
@@ -50,9 +50,9 @@
     moves = []
     for d in range(1, lines):
         moves += [
-            (3.0 * d, functools.partial(gather.sides, d, gather.one)),
-            (3.0 * d + 2.1, functools.partial(gather.sides, d, gather.two)),
-            (3.0 * d + 5.2, functools.partial(gather.sides, d, gather.three)),
+            (3.5 * d, functools.partial(gather.sides, d, gather.one)),
+            (3.5 * d + 2.5, functools.partial(gather.sides, d, gather.two)),
+            (3.5 * d + 5.5, functools.partial(gather.sides, d, gather.three)),
         ]
     moves.append((900.0, gather.finish))
     moves.sort(key=lambda move: move[0])
@@ -86,11 +86,19 @@
     query = jnp.concatenate(
         [q_ref[0, :, columns], qx_ref[:, columns]], axis=0
     )
-    scores = jnp.dot(keys[...], query, preferred_element_type=f32)
-    maximum = jnp.max(scores, axis=0, keepdims=True)
-    raised = jnp.exp(scores - maximum)
-    total = jnp.sum(raised, axis=0, keepdims=True)
-    gathered_values = jnp.dot(v_ref[0], raised.astype(bf16), preferred_element_type=f32)
+    maximum = jnp.full((1, width), -3e38, f32)
+    total, gathered_values = 0.0, 0.0
+    half = keys.shape[0] // 2
+    for part in (pl.ds(0, half), pl.ds(half, half)):
+        scores = jnp.dot(keys[part, :], query, preferred_element_type=f32)
+        larger = jnp.maximum(maximum, jnp.max(scores, axis=0, keepdims=True))
+        shrink = jnp.exp(maximum - larger)
+        raised = jnp.exp(scores - larger)
+        total = shrink * total + jnp.sum(raised, axis=0, keepdims=True)
+        gathered_values = shrink * gathered_values + jnp.dot(
+            v_ref[0, :, part], raised.astype(bf16), preferred_element_type=f32
+        )
+        maximum = larger
     result = (gathered_values / total).astype(bf16)
     o_ref[0, :, columns] = result
     log_ref[0, :, columns] = maximum + jnp.log(total)

time: 406 us -> 401 us (0.988)
  Pallas kernels: 400 us -> 395 us
where the time goes in v8:
time: 401 us
  Pallas kernels  395 us (99%)
  local copies, waits for them, and re-layouts  5.12 us (1%)
    pallas_call x1, Pallas kernels, backward(): pl.pallas_call(functools.partial(backward_kernel, wide, narrow, items, ch...  179 us
    pallas_call x1, Pallas kernels, start(): pl.pallas_call(functools.partial(start_kernel, wide, narrow), in_specs=[p...  103 us
    pallas_call x1, Pallas kernels, attend_forward(): pl.pallas_call(functools.partial(forward_kernel, wide, narrow), grid=(hea...  65.6 us
    pallas_call x1, Pallas kernels, mlp(): pl.pallas_call(mlp_kernel, grid=(narrow,), in_specs=[whole(*attended.shap...  44.6 us

profile of v8, /device:TPU:0, one launch (start us, length us, event | category | flops | bytes accessed | tf_op | source)
XLA Modules:
  0.0 400.8 jit_solution(15375265762922735409)
XLA Ops:
  0.6 103.2 %start.1 = (bf16[8,512,1024]{2,1,0:T(8,128)(2,1)}, bf16[384,4096]{1,0:T(8,128)(2,1)}, bf16[384,1024]{1,0:T(8,128)(2,1)}, bf16[2,16,4096]{2,1,0:T(8,128)(2,1)}, bf16[8,2,2,2,128,512]{5,4,3,2,1,0:T(8,128)(2,1)}) custom-call(s32[1,4]{1,0:T(1,128)} %length_ref.1, bf16[512,1024]{1,0:T(8,128)(2,1)} %token_ref.5, bf16[1024]{0:T(1024)(128)(2,1)} %gain_ref.5, ...), custom_call_target="tpu_custom_call" | custom-call | tf_op jit(solution)/shard_map/start/pallas_call | solution.py:1468
  103.9 65.6 %attend_forward.1 = (bf16[2,64,4096]{2,1,0:T(8,128)(2,1)}, f32[2,1,4096]{2,1,0:T(1,128)}, bf16[8,2,64,512]{3,2,1,0:T(8,128)(2,1)}, bf16[8,2,2,2,80,1024]{5,4,3,2,1,0:T(8,128)(2,1)}) custom-call(bf16[2,16,4096]{2,1,0:T(8,128)(2,1)} %get-tuple-element.33.qx_ref.kx_ref.extra_ref, bf16[2,16,4096]{2,1,0:T(8,128)(2,1)} %get-tuple-element.33.qx_ref.kx_ref.extra_ref, ...), custom_call_target="tpu_custom_call" | custom-call | tf_op jit(solution)/shard_map/attend_forward/pallas_call | solution.py:149
  169.5 44.6 %mlp.1 = (bf16[512,1024]{1,0:T(8,128)(2,1)}, f32[512,1024]{1,0:T(8,128)}, bf16[1024,512]{1,0:T(8,128)(2,1)}, bf16[1024,1024]{1,0:T(8,128)(2,1)}, bf16[8,2,2,2,12...) custom-call(bf16[1024,512]{1,0:T(8,128)(2,1)} %bitcast.23, ...), custom_call_target="tpu_custom_call" | custom-call | tf_op jit(solution)/shard_map/mlp/pallas_call | solution.py:548
  214.2 178.6 %backward.1 = (bf16[512,1024]{1,0:T(8,128)(2,1)}, bf16[384,1024]{1,0:T(8,128)(2,1)}, bf16[4,2,144,1024]{3,2,1,0:T(8,128)(2,1)}, f32[8,128]{1,0:T(8,128)}, bf16[4,2,2,2,144,1024]{5,4,3,2,1,0:T(8,128)(2,1)}) custom-call(bf16[2,16,4096]{2,1,0:T(8,128)(2,1)} %get-tuple-element.33.qx_ref.kx_ref.extra_ref, bf16[2,3,64,4096]{3,2,1,0:T(8,128)(2,1)} %bitcast.19, ...), custom_call_target="tpu_custom_call" | custom-call | tf_op jit(solution)/shard_map/backward/pallas_call | solution.py:1044
  392.7 1.4 slice_bitcast_fusion
  394.1 0.0 copy-start
  394.1 1.7 copy-done
  395.8 0.0 copy-start.1
  395.8 1.1 copy-done.1
  396.9 0.0 copy-start.2
  396.9 2.9 unpack.1
  399.8 0.0 copy-done.2
  399.8 1.0 copy.22
Async XLA Ops:
  394.1 1.7 copy-start
  395.8 1.1 copy-start.1
  396.9 3.0 copy-start.2

commit v9 on v8

--- a/solution.py
+++ b/solution.py
@@ -11,7 +11,7 @@
 HEAD_DIM = 64
 EXTRA = 16
 CHUNKS = 2
-REDUCE_START, REDUCE_STEP, REDUCE_FIRST, REDUCE_SECOND, SPREAD_AT = 3, 11, 8, 12, 8
+REDUCE_START, REDUCE_STEP, REDUCE_FIRST, REDUCE_SECOND, SPREAD_AT = 3, 11, 9, 13, 8
 EARLY_RELAY = 17
 EXCLUDED = -1e30
 bf16 = jnp.bfloat16

time: 401 us -> 399 us (level)
  no operation moved by 1% of the time
where the time goes in v9:
time: 399 us
  Pallas kernels  393 us (98%)
  local copies, waits for them, and re-layouts  5.12 us (1%)
    pallas_call x1, Pallas kernels, backward(): pl.pallas_call(functools.partial(backward_kernel, wide, narrow, items, ch...  176 us
    pallas_call x1, Pallas kernels, start(): pl.pallas_call(functools.partial(start_kernel, wide, narrow), in_specs=[p...  103 us
    pallas_call x1, Pallas kernels, attend_forward(): pl.pallas_call(functools.partial(forward_kernel, wide, narrow), grid=(hea...  65.6 us
    pallas_call x1, Pallas kernels, mlp(): pl.pallas_call(mlp_kernel, grid=(narrow,), in_specs=[whole(*attended.shap...  44.6 us

profile of v9, /device:TPU:0, one launch (start us, length us, event | category | flops | bytes accessed | tf_op | source)
XLA Modules:
  0.0 398.7 jit_solution(14885329563263476667)
XLA Ops:
  0.6 103.2 %start.1 = (bf16[8,512,1024]{2,1,0:T(8,128)(2,1)}, bf16[384,4096]{1,0:T(8,128)(2,1)}, bf16[384,1024]{1,0:T(8,128)(2,1)}, bf16[2,16,4096]{2,1,0:T(8,128)(2,1)}, bf16[8,2,2,2,128,512]{5,4,3,2,1,0:T(8,128)(2,1)}) custom-call(s32[1,4]{1,0:T(1,128)} %length_ref.1, bf16[512,1024]{1,0:T(8,128)(2,1)} %token_ref.5, bf16[1024]{0:T(1024)(128)(2,1)} %gain_ref.5, ...), custom_call_target="tpu_custom_call" | custom-call | tf_op jit(solution)/shard_map/start/pallas_call | solution.py:1468
  103.9 65.6 %attend_forward.1 = (bf16[2,64,4096]{2,1,0:T(8,128)(2,1)}, f32[2,1,4096]{2,1,0:T(1,128)}, bf16[8,2,64,512]{3,2,1,0:T(8,128)(2,1)}, bf16[8,2,2,2,80,1024]{5,4,3,2,1,0:T(8,128)(2,1)}) custom-call(bf16[2,16,4096]{2,1,0:T(8,128)(2,1)} %get-tuple-element.33.qx_ref.kx_ref.extra_ref, bf16[2,16,4096]{2,1,0:T(8,128)(2,1)} %get-tuple-element.33.qx_ref.kx_ref.extra_ref, ...), custom_call_target="tpu_custom_call" | custom-call | tf_op jit(solution)/shard_map/attend_forward/pallas_call | solution.py:149
  169.5 44.6 %mlp.1 = (bf16[512,1024]{1,0:T(8,128)(2,1)}, f32[512,1024]{1,0:T(8,128)}, bf16[1024,512]{1,0:T(8,128)(2,1)}, bf16[1024,1024]{1,0:T(8,128)(2,1)}, bf16[8,2,2,2,12...) custom-call(bf16[1024,512]{1,0:T(8,128)(2,1)} %bitcast.23, ...), custom_call_target="tpu_custom_call" | custom-call | tf_op jit(solution)/shard_map/mlp/pallas_call | solution.py:548
  214.2 176.5 %backward.1 = (bf16[512,1024]{1,0:T(8,128)(2,1)}, bf16[384,1024]{1,0:T(8,128)(2,1)}, bf16[4,2,144,1024]{3,2,1,0:T(8,128)(2,1)}, f32[8,128]{1,0:T(8,128)}, bf16[4,2,2,2,144,1024]{5,4,3,2,1,0:T(8,128)(2,1)}) custom-call(bf16[2,16,4096]{2,1,0:T(8,128)(2,1)} %get-tuple-element.33.qx_ref.kx_ref.extra_ref, bf16[2,3,64,4096]{3,2,1,0:T(8,128)(2,1)} %bitcast.19, ...), custom_call_target="tpu_custom_call" | custom-call | tf_op jit(solution)/shard_map/backward/pallas_call | solution.py:1044
  390.6 1.4 slice_bitcast_fusion
  392.0 0.0 copy-start
  392.0 1.7 copy-done
  393.6 0.0 copy-start.1
  393.6 1.1 copy-done.1
  394.8 0.0 copy-start.2
  394.8 2.9 unpack.1
  397.7 0.0 copy-done.2
  397.7 1.0 copy.22
Async XLA Ops:
  392.0 1.7 copy-start
  393.6 1.1 copy-start.1
  394.8 3.0 copy-start.2

commit v10 on v9

--- a/solution.py
+++ b/solution.py
@@ -302,9 +302,8 @@
         )
 
     def begin():
-        for j in range(lines):
-            for copy in to_sibling(j):
-                copy.start()
+        for copy in to_sibling(0):
+            copy.start()
 
     def sent(j):
         for h, i in halves:
@@ -316,6 +315,9 @@
 
     def combine(j):
         slot = j % slots
+        if j + 1 < lines:
+            for copy in to_sibling(j + 1):
+                copy.start()
         if j >= slots:
             sent(j - slots)
         for copy in load(j):

time: 399 us -> 398 us (level)
  no operation moved by 1% of the time
where the time goes in v10:
time: 398 us; the launch traced here: 397 us
  Pallas kernels  391 us (98%)
  local copies, waits for them, and re-layouts  5.12 us (1%)
    pallas_call x1, Pallas kernels, backward(): pl.pallas_call(functools.partial(backward_kernel, wide, narrow, items, ch...  175 us
    pallas_call x1, Pallas kernels, start(): pl.pallas_call(functools.partial(start_kernel, wide, narrow), in_specs=[p...  103 us
    pallas_call x1, Pallas kernels, attend_forward(): pl.pallas_call(functools.partial(forward_kernel, wide, narrow), grid=(hea...  65.6 us
    pallas_call x1, Pallas kernels, mlp(): pl.pallas_call(mlp_kernel, grid=(narrow,), in_specs=[whole(*attended.shap...  44.6 us

profile of v10, /device:TPU:0, one launch (start us, length us, event | category | flops | bytes accessed | tf_op | source)
XLA Modules:
  0.0 397.3 jit_solution(12060705433952939030)
XLA Ops:
  0.6 103.2 %start.1 = (bf16[8,512,1024]{2,1,0:T(8,128)(2,1)}, bf16[384,4096]{1,0:T(8,128)(2,1)}, bf16[384,1024]{1,0:T(8,128)(2,1)}, bf16[2,16,4096]{2,1,0:T(8,128)(2,1)}, bf16[8,2,2,2,128,512]{5,4,3,2,1,0:T(8,128)(2,1)}) custom-call(s32[1,4]{1,0:T(1,128)} %length_ref.1, bf16[512,1024]{1,0:T(8,128)(2,1)} %token_ref.5, bf16[1024]{0:T(1024)(128)(2,1)} %gain_ref.5, ...), custom_call_target="tpu_custom_call" | custom-call | tf_op jit(solution)/shard_map/start/pallas_call | solution.py:1470
  103.9 65.6 %attend_forward.1 = (bf16[2,64,4096]{2,1,0:T(8,128)(2,1)}, f32[2,1,4096]{2,1,0:T(1,128)}, bf16[8,2,64,512]{3,2,1,0:T(8,128)(2,1)}, bf16[8,2,2,2,80,1024]{5,4,3,2,1,0:T(8,128)(2,1)}) custom-call(bf16[2,16,4096]{2,1,0:T(8,128)(2,1)} %get-tuple-element.33.qx_ref.kx_ref.extra_ref, bf16[2,16,4096]{2,1,0:T(8,128)(2,1)} %get-tuple-element.33.qx_ref.kx_ref.extra_ref, ...), custom_call_target="tpu_custom_call" | custom-call | tf_op jit(solution)/shard_map/attend_forward/pallas_call | solution.py:149
  169.5 44.6 %mlp.1 = (bf16[512,1024]{1,0:T(8,128)(2,1)}, f32[512,1024]{1,0:T(8,128)}, bf16[1024,512]{1,0:T(8,128)(2,1)}, bf16[1024,1024]{1,0:T(8,128)(2,1)}, bf16[8,2,2,2,12...) custom-call(bf16[1024,512]{1,0:T(8,128)(2,1)} %bitcast.23, ...), custom_call_target="tpu_custom_call" | custom-call | tf_op jit(solution)/shard_map/mlp/pallas_call | solution.py:550
  214.2 175.0 %backward.1 = (bf16[512,1024]{1,0:T(8,128)(2,1)}, bf16[384,1024]{1,0:T(8,128)(2,1)}, bf16[4,2,144,1024]{3,2,1,0:T(8,128)(2,1)}, f32[8,128]{1,0:T(8,128)}, bf16[4,2,2,2,144,1024]{5,4,3,2,1,0:T(8,128)(2,1)}) custom-call(bf16[2,16,4096]{2,1,0:T(8,128)(2,1)} %get-tuple-element.33.qx_ref.kx_ref.extra_ref, bf16[2,3,64,4096]{3,2,1,0:T(8,128)(2,1)} %bitcast.19, ...), custom_call_target="tpu_custom_call" | custom-call | tf_op jit(solution)/shard_map/backward/pallas_call | solution.py:1046
  389.2 1.4 slice_bitcast_fusion
  390.5 0.0 copy-start
  390.5 1.7 copy-done
  392.2 0.0 copy-start.1
  392.2 1.1 copy-done.1
  393.3 0.0 copy-start.2
  393.3 2.9 unpack.1
  396.3 0.0 copy-done.2
  396.3 1.0 copy.22
Async XLA Ops:
  390.5 1.7 copy-start
  392.2 1.1 copy-start.1
  393.3 3.0 copy-start.2
